TPU v7x, 32 devices: a whole 2x2x4 slice. The times are simulated.
32 devices in a mesh: dp: 8 (over z, x), seq: 4 (over y, core).
Axes of the slice: x: 2, y: 2, z: 4, core: 2. Of those that a mesh axis runs over, the one named last changes fastest.
Arguments:
- tokens: bfloat16 [16, 1024, 768], P('dp', 'seq'), may hold values from -6 to 6
- cotangent: bfloat16 [16, 1024, 768], P('dp', 'seq'), may hold values from -6 to 6
- prefix: int32 [16], P('dp'), may hold values from 102 to 512
- ln1_gain: bfloat16 [768], P(('dp', 'seq')), may hold values from 0.5 to 1.5
- ln1_bias: bfloat16 [768], P(('dp', 'seq')), may hold values from -1.25 to 1.25
- w_qkv: bfloat16 [768, 2304], P(('dp', 'seq')), may hold values from -0.21875 to 0.21875
- b_qkv: bfloat16 [2304], P(('dp', 'seq')), may hold values from -1.75 to 1.75
- w_out: bfloat16 [768, 768], P(('dp', 'seq')), may hold values from -4 to 4
- b_out: bfloat16 [768], P(('dp', 'seq')), may hold values from -1.75 to 1.75
- ln2_gain: bfloat16 [768], P(('dp', 'seq')), may hold values from 0.5 to 1.5
- ln2_bias: bfloat16 [768], P(('dp', 'seq')), may hold values from -1.25 to 1.25
- w_up: bfloat16 [768, 3072], P(('dp', 'seq')), may hold values from -0.21875 to 0.21875
- b_up: bfloat16 [3072], P(('dp', 'seq')), may hold values from -1.75 to 1.75
- w_down: bfloat16 [3072, 768], P(('dp', 'seq')), may hold values from -0.109375 to 0.109375
- b_down: bfloat16 [768], P(('dp', 'seq')), may hold values from -1.75 to 1.75
Outputs:
- block_out: bfloat16 [16, 1024, 768], P('dp', 'seq')
- grad_tokens: bfloat16 [16, 1024, 768], P('dp', 'seq')
- grad_ln1_gain: float32 [768], P(('dp', 'seq'))
- grad_ln1_bias: float32 [768], P(('dp', 'seq'))
- grad_w_qkv: float32 [768, 2304], P(('dp', 'seq'))
- grad_b_qkv: float32 [2304], P(('dp', 'seq'))
- grad_w_out: float32 [768, 768], P(('dp', 'seq'))
- grad_b_out: float32 [768], P(('dp', 'seq'))
- grad_ln2_gain: float32 [768], P(('dp', 'seq'))
- grad_ln2_bias: float32 [768], P(('dp', 'seq'))
- grad_w_up: float32 [768, 3072], P(('dp', 'seq'))
- grad_b_up: float32 [3072], P(('dp', 'seq'))
- grad_w_down: float32 [3072, 768], P(('dp', 'seq'))
- grad_b_down: float32 [768], P(('dp', 'seq'))
Inputs may be any that keep to these rules, and one draw needn't show every extreme that they name: Every prefix length is an integer within the range stated in the table.
All inputs are finite; a program needn't handle non-finite values.
Results may differ from a plain program's by a relative error of at most 0.014.
The roundings to bfloat16 on the way count: a program that leaves them out, or rounds other values in their place, can miss the bound.
Values may be sent and summed in bfloat16 or wider, within the bound.
A program may use at most 256 MiB of HBM per device.

v0:
```python
import jax
import jax.numpy as jnp
from jax import lax
from jax.sharding import PartitionSpec as P

HEADS = 12
HEAD_DIM = 64
MB = 2


norm_eps = 1e-05
block_rows = 512


def layer_norm(features, gain, shift):
    centre = features - jnp.mean(features, axis=-1, keepdims=True)
    spread = jnp.mean(centre * centre, axis=-1, keepdims=True)
    return centre * lax.rsqrt(spread + norm_eps) * gain + shift


def gelu_tanh(values):
    return jax.nn.gelu(values, approximate=True)


def in_blocks(update, running, pieces):
    length = pieces[0].shape[1]
    blocks = length // block_rows
    blocked_pieces = tuple(
        (
            jnp.swapaxes(
                member.reshape((member.shape[0], blocks, block_rows) + member.shape[2:]), 0, 1
            )
            for member in pieces
        )
    )

    def advance(carried, element):
        return (update(carried, element[0], element[1] * block_rows), None)

    running, unused = lax.scan(
        advance, running, (blocked_pieces, jnp.arange(blocks, dtype=jnp.int32))
    )
    return running


def to_heads(flat_rows):
    return flat_rows.reshape(flat_rows.shape[0], flat_rows.shape[1], HEADS, HEAD_DIM)


def visible_mask(query_places, key_places, prefix_len):
    earlier = key_places[None, None, :] <= query_places[None, :, None]
    in_prefix = key_places[None, None, :] < prefix_len[:, None, None]
    return (earlier | in_prefix)[:, :, None, :]


def head_scores(query_heads, key_flat):
    return jnp.einsum(
        "bqhd,bkhd->bqhk", query_heads, to_heads(key_flat), preferred_element_type=jnp.float32
    ) * HEAD_DIM ** (-0.5)


def attend(query_heads, key_flat, value_flat, prefix_len):
    local_len = query_heads.shape[1]
    query_places = lax.axis_index("seq") * local_len + jnp.arange(local_len, dtype=jnp.int32)
    starting = (
        jnp.zeros(query_heads.shape, jnp.float32),
        jnp.zeros(query_heads.shape[:3], jnp.float32),
        jnp.zeros(query_heads.shape[:3], jnp.float32),
    )

    def update(running, pieces, offset):
        weighted, normaliser, ceiling = running
        key_piece, value_piece = pieces
        key_places = offset + jnp.arange(key_piece.shape[1], dtype=jnp.int32)
        scores = head_scores(query_heads, key_piece)
        visible = visible_mask(query_places, key_places, prefix_len)
        magnitude = jnp.where(visible, jnp.abs(scores), 0.0)
        new_ceiling = jnp.maximum(ceiling, jnp.max(magnitude, axis=-1))
        exponent = jnp.where(visible, jnp.exp(magnitude - new_ceiling[..., None]), 0.0)
        factor = jnp.exp(ceiling - new_ceiling)
        weights = (jnp.sign(scores) * exponent).astype(jnp.bfloat16)
        weighted = weighted * factor[..., None] + jnp.einsum(
            "bqhk,bkhd->bqhd", weights, to_heads(value_piece), preferred_element_type=jnp.float32
        )
        normaliser = normaliser * factor + jnp.sum(exponent, axis=-1)
        return (weighted, normaliser, new_ceiling)

    weighted, normaliser, ceiling = in_blocks(
        update,
        starting,
        (
            lax.all_gather(key_flat, "seq", axis=1, tiled=True),
            lax.all_gather(value_flat, "seq", axis=1, tiled=True),
        ),
    )
    return (weighted / normaliser[..., None], ceiling + jnp.log(normaliser))


def grad_terms(
    query_heads,
    grad_heads,
    key_flat,
    value_flat,
    log_total,
    delta_sum,
    query_places,
    key_places,
    prefix_len,
):
    scores = head_scores(query_heads, key_flat)
    sign_of = jnp.sign(scores)
    visible = visible_mask(query_places, key_places, prefix_len)
    shares = jnp.where(visible, jnp.exp(jnp.abs(scores) - log_total[..., None]), 0.0)
    grad_weights = jnp.einsum(
        "bqhd,bkhd->bqhk", grad_heads, to_heads(value_flat), preferred_element_type=jnp.float32
    )
    grad_scores = (shares * (grad_weights - sign_of * delta_sum[..., None])).astype(jnp.bfloat16)
    return ((sign_of * shares).astype(jnp.bfloat16), grad_scores)


def query_term(grad_scores, key_flat):
    return jnp.einsum(
        "bqhk,bkhd->bqhd", grad_scores, to_heads(key_flat), preferred_element_type=jnp.float32
    ) * HEAD_DIM ** (-0.5)


def key_value_terms(query_heads, grad_heads, shares_low, grad_scores):
    key_term = jnp.einsum(
        "bqhk,bqhd->bkhd", grad_scores, query_heads, preferred_element_type=jnp.float32
    ) * HEAD_DIM ** (-0.5)
    value_term = jnp.einsum(
        "bqhk,bqhd->bkhd", shares_low, grad_heads, preferred_element_type=jnp.float32
    )
    flat_shape = (key_term.shape[0], key_term.shape[1], key_term.shape[2] * key_term.shape[3])
    return jnp.concatenate([key_term.reshape(flat_shape), value_term.reshape(flat_shape)], axis=-1)


def attend_back(query_heads, key_flat, value_flat, grad_heads, log_total, delta_sum, prefix_len):
    seq_block, local_len = (query_heads.shape[0], query_heads.shape[1])
    width = key_flat.shape[2]
    local_places = lax.axis_index("seq") * local_len + jnp.arange(local_len, dtype=jnp.int32)
    starting = (
        jnp.zeros(query_heads.shape, jnp.float32),
        jnp.zeros((seq_block, lax.axis_size("seq") * local_len, 2 * width), jnp.float32),
    )

    def update_both(running, pieces, offset):
        grad_query, grad_keys = running
        key_piece, value_piece = pieces
        piece_len = key_piece.shape[1]
        key_places = offset + jnp.arange(piece_len, dtype=jnp.int32)
        shares_low, grad_scores = grad_terms(
            query_heads,
            grad_heads,
            key_piece,
            value_piece,
            log_total,
            delta_sum,
            local_places,
            key_places,
            prefix_len,
        )
        grad_query = grad_query + query_term(grad_scores, key_piece)
        current = lax.dynamic_slice_in_dim(grad_keys, offset, piece_len, 1)
        updated = current + key_value_terms(query_heads, grad_heads, shares_low, grad_scores)
        return (grad_query, lax.dynamic_update_slice_in_dim(grad_keys, updated, offset, 1))

    grad_query, grad_keys = in_blocks(
        update_both,
        starting,
        (
            lax.all_gather(key_flat, "seq", axis=1, tiled=True),
            lax.all_gather(value_flat, "seq", axis=1, tiled=True),
        ),
    )
    key_local = lax.psum_scatter(
        grad_keys.astype(jnp.bfloat16), "seq", scatter_dimension=1, tiled=True
    ).astype(jnp.float32)
    return (grad_query, key_local)


def forward_block(weights_in, token_part, prefix_len):
    (
        gain_one,
        shift_one,
        w_qkv,
        b_qkv,
        w_out,
        b_out,
        gain_two,
        shift_two,
        w_up,
        b_up,
        w_down,
        b_down,
    ) = weights_in
    seq_block, local_len, width = token_part.shape
    residual_in = token_part.reshape(-1, width).astype(jnp.float32)
    normed_one = layer_norm(
        residual_in, gain_one.astype(jnp.float32), shift_one.astype(jnp.float32)
    ).astype(jnp.bfloat16)
    projected = jnp.dot(normed_one, w_qkv, preferred_element_type=jnp.float32) + b_qkv.astype(
        jnp.float32
    )
    query_heads = (
        projected[:, :width].astype(jnp.bfloat16).reshape(seq_block, local_len, HEADS, HEAD_DIM)
    )
    key_flat = (
        projected[:, width : 2 * width].astype(jnp.bfloat16).reshape(seq_block, local_len, width)
    )
    value_flat = projected[:, 2 * width :].astype(jnp.bfloat16).reshape(seq_block, local_len, width)
    attended, log_total = attend(query_heads, key_flat, value_flat, prefix_len)
    attended_low = attended.reshape(-1, width).astype(jnp.bfloat16)
    residual_mid = (
        residual_in
        + jnp.dot(attended_low, w_out, preferred_element_type=jnp.float32)
        + b_out.astype(jnp.float32)
    )
    normed_two = layer_norm(
        residual_mid, gain_two.astype(jnp.float32), shift_two.astype(jnp.float32)
    ).astype(jnp.bfloat16)
    pre_gelu = jnp.dot(normed_two, w_up, preferred_element_type=jnp.float32) + b_up.astype(
        jnp.float32
    )
    hidden = gelu_tanh(pre_gelu).astype(jnp.bfloat16)
    result = (
        residual_mid
        + jnp.dot(hidden, w_down, preferred_element_type=jnp.float32)
        + b_down.astype(jnp.float32)
    )
    saved = (
        residual_in,
        normed_one,
        query_heads,
        key_flat,
        value_flat,
        attended,
        log_total,
        attended_low,
        residual_mid,
        normed_two,
        pre_gelu,
        hidden,
    )
    return (result.astype(jnp.bfloat16).reshape(token_part.shape), saved)


def backward_block(weights_in, saved, grad_part, prefix_len):
    (
        gain_one,
        shift_one,
        w_qkv,
        b_qkv,
        w_out,
        b_out,
        gain_two,
        shift_two,
        w_up,
        b_up,
        w_down,
        b_down,
    ) = weights_in
    (
        residual_in,
        normed_one,
        query_heads,
        key_flat,
        value_flat,
        attended,
        log_total,
        attended_low,
        residual_mid,
        normed_two,
        pre_gelu,
        hidden,
    ) = saved
    seq_block, local_len, width = grad_part.shape
    grad_result = grad_part.reshape(-1, width).astype(jnp.float32)
    grad_branch = grad_part.reshape(-1, width)
    grads_down = jnp.einsum("rf,rd->fd", hidden, grad_branch, preferred_element_type=jnp.float32)
    bias_down = jnp.sum(grad_branch, axis=0, dtype=jnp.float32)
    grad_hidden = jnp.einsum("rd,fd->rf", grad_branch, w_down, preferred_element_type=jnp.float32)
    gelu_pull = jax.vjp(gelu_tanh, pre_gelu)[1]
    grad_pre = gelu_pull(grad_hidden)[0].astype(jnp.bfloat16)
    grads_up = jnp.einsum("rd,rf->df", normed_two, grad_pre, preferred_element_type=jnp.float32)
    bias_up = jnp.sum(grad_pre, axis=0, dtype=jnp.float32)
    grad_normed_two = jnp.einsum("rf,df->rd", grad_pre, w_up, preferred_element_type=jnp.float32)
    norm_two_pull = jax.vjp(
        layer_norm, residual_mid, gain_two.astype(jnp.float32), shift_two.astype(jnp.float32)
    )[1]
    grad_mid, grads_gain_two, grads_shift_two = norm_two_pull(grad_normed_two)
    grad_mid = grad_mid + grad_result
    grad_attn = grad_mid.astype(jnp.bfloat16)
    grads_out = jnp.einsum("rd,re->de", attended_low, grad_attn, preferred_element_type=jnp.float32)
    bias_out = jnp.sum(grad_attn, axis=0, dtype=jnp.float32)
    grad_heads = (
        jnp.einsum("re,de->rd", grad_attn, w_out, preferred_element_type=jnp.float32)
        .astype(jnp.bfloat16)
        .reshape(seq_block, local_len, HEADS, HEAD_DIM)
    )
    delta_sum = jnp.sum(grad_heads.astype(jnp.float32) * attended, axis=-1)
    grad_query, key_local = attend_back(
        query_heads, key_flat, value_flat, grad_heads, log_total, delta_sum, prefix_len
    )
    grad_proj = jnp.concatenate(
        [grad_query.reshape(-1, width), key_local.reshape(-1, 2 * width)], axis=1
    ).astype(jnp.bfloat16)
    grads_qkv = jnp.einsum("rd,re->de", normed_one, grad_proj, preferred_element_type=jnp.float32)
    bias_qkv = jnp.sum(grad_proj, axis=0, dtype=jnp.float32)
    grad_normed_one = jnp.einsum("re,de->rd", grad_proj, w_qkv, preferred_element_type=jnp.float32)
    norm_one_pull = jax.vjp(
        layer_norm, residual_in, gain_one.astype(jnp.float32), shift_one.astype(jnp.float32)
    )[1]
    grad_in, grads_gain_one, grads_shift_one = norm_one_pull(grad_normed_one)
    grad_in = grad_in + grad_mid
    weight_grads = (
        grads_gain_one,
        grads_shift_one,
        grads_qkv,
        bias_qkv,
        grads_out,
        bias_out,
        grads_gain_two,
        grads_shift_two,
        grads_up,
        bias_up,
        grads_down,
        bias_down,
    )
    return (grad_in.astype(jnp.bfloat16).reshape(grad_part.shape), weight_grads)


def body(
    tokens,
    cotangent,
    prefix,
    ln1_gain,
    ln1_bias,
    w_qkv,
    b_qkv,
    w_out,
    b_out,
    ln2_gain,
    ln2_bias,
    w_up,
    b_up,
    w_down,
    b_down,
):
    shards = (
        ln1_gain,
        ln1_bias,
        w_qkv,
        b_qkv,
        w_out,
        b_out,
        ln2_gain,
        ln2_bias,
        w_up,
        b_up,
        w_down,
        b_down,
    )
    spread_count = lax.axis_size(("dp", "seq"))
    totals = tuple(
        (
            jnp.zeros((member.shape[0] * spread_count,) + member.shape[1:], jnp.float32)
            for member in shards
        )
    )
    seq_block = tokens.shape[0] // MB
    outputs = []
    grad_inputs = []
    for batch_index in range(MB):
        first_row = batch_index * seq_block
        token_part = tokens[first_row : first_row + seq_block]
        cotangent_part = cotangent[first_row : first_row + seq_block]
        prefix_part = prefix[first_row : first_row + seq_block]
        forward_weights = (
            lax.all_gather(shards[0], ("dp", "seq"), axis=0, tiled=True),
            lax.all_gather(shards[1], ("dp", "seq"), axis=0, tiled=True),
            lax.all_gather(shards[2], ("dp", "seq"), axis=0, tiled=True),
            lax.all_gather(shards[3], ("dp", "seq"), axis=0, tiled=True),
            lax.all_gather(shards[4], ("dp", "seq"), axis=0, tiled=True),
            lax.all_gather(shards[5], ("dp", "seq"), axis=0, tiled=True),
            lax.all_gather(shards[6], ("dp", "seq"), axis=0, tiled=True),
            lax.all_gather(shards[7], ("dp", "seq"), axis=0, tiled=True),
            lax.all_gather(shards[8], ("dp", "seq"), axis=0, tiled=True),
            lax.all_gather(shards[9], ("dp", "seq"), axis=0, tiled=True),
            lax.all_gather(shards[10], ("dp", "seq"), axis=0, tiled=True),
            lax.all_gather(shards[11], ("dp", "seq"), axis=0, tiled=True),
        )
        result, saved = forward_block(forward_weights, token_part, prefix_part)
        back_weights = (
            lax.all_gather(shards[0], ("dp", "seq"), axis=0, tiled=True),
            lax.all_gather(shards[1], ("dp", "seq"), axis=0, tiled=True),
            lax.all_gather(shards[2], ("dp", "seq"), axis=0, tiled=True),
            lax.all_gather(shards[3], ("dp", "seq"), axis=0, tiled=True),
            lax.all_gather(shards[4], ("dp", "seq"), axis=0, tiled=True),
            lax.all_gather(shards[5], ("dp", "seq"), axis=0, tiled=True),
            lax.all_gather(shards[6], ("dp", "seq"), axis=0, tiled=True),
            lax.all_gather(shards[7], ("dp", "seq"), axis=0, tiled=True),
            lax.all_gather(shards[8], ("dp", "seq"), axis=0, tiled=True),
            lax.all_gather(shards[9], ("dp", "seq"), axis=0, tiled=True),
            lax.all_gather(shards[10], ("dp", "seq"), axis=0, tiled=True),
            lax.all_gather(shards[11], ("dp", "seq"), axis=0, tiled=True),
        )
        grad_piece, weight_grads = backward_block(back_weights, saved, cotangent_part, prefix_part)
        totals = tuple(
            (running_sum + new_term for running_sum, new_term in zip(totals, weight_grads))
        )
        outputs.append(result)
        grad_inputs.append(grad_piece)
    reduced = (
        lax.psum_scatter(totals[0], ("dp", "seq"), scatter_dimension=0, tiled=True),
        lax.psum_scatter(totals[1], ("dp", "seq"), scatter_dimension=0, tiled=True),
        lax.psum_scatter(totals[2], ("dp", "seq"), scatter_dimension=0, tiled=True),
        lax.psum_scatter(totals[3], ("dp", "seq"), scatter_dimension=0, tiled=True),
        lax.psum_scatter(totals[4], ("dp", "seq"), scatter_dimension=0, tiled=True),
        lax.psum_scatter(totals[5], ("dp", "seq"), scatter_dimension=0, tiled=True),
        lax.psum_scatter(totals[6], ("dp", "seq"), scatter_dimension=0, tiled=True),
        lax.psum_scatter(totals[7], ("dp", "seq"), scatter_dimension=0, tiled=True),
        lax.psum_scatter(totals[8], ("dp", "seq"), scatter_dimension=0, tiled=True),
        lax.psum_scatter(totals[9], ("dp", "seq"), scatter_dimension=0, tiled=True),
        lax.psum_scatter(totals[10], ("dp", "seq"), scatter_dimension=0, tiled=True),
        lax.psum_scatter(totals[11], ("dp", "seq"), scatter_dimension=0, tiled=True),
    )
    return (
        jnp.concatenate(outputs, axis=0),
        jnp.concatenate(grad_inputs, axis=0),
        reduced[0],
        reduced[1],
        reduced[2],
        reduced[3],
        reduced[4],
        reduced[5],
        reduced[6],
        reduced[7],
        reduced[8],
        reduced[9],
        reduced[10],
        reduced[11],
    )


def solution(mesh):
    in_specs = (
        P("dp", "seq", None),
        P("dp", "seq", None),
        P("dp"),
        P(("dp", "seq")),
        P(("dp", "seq")),
        P(("dp", "seq"), None),
        P(("dp", "seq")),
        P(("dp", "seq"), None),
        P(("dp", "seq")),
        P(("dp", "seq")),
        P(("dp", "seq")),
        P(("dp", "seq"), None),
        P(("dp", "seq")),
        P(("dp", "seq"), None),
        P(("dp", "seq")),
    )
    out_specs = (
        P("dp", "seq", None),
        P("dp", "seq", None),
        P(("dp", "seq")),
        P(("dp", "seq")),
        P(("dp", "seq"), None),
        P(("dp", "seq")),
        P(("dp", "seq"), None),
        P(("dp", "seq")),
        P(("dp", "seq")),
        P(("dp", "seq")),
        P(("dp", "seq"), None),
        P(("dp", "seq")),
        P(("dp", "seq"), None),
        P(("dp", "seq")),
    )
    return jax.shard_map(body, mesh=mesh, in_specs=in_specs, out_specs=out_specs, check_vma=False)
```

profile of v0, /device:TPU:0, one launch (start us, length us, event | category | flops | bytes accessed | tf_op | source)
XLA Modules:
  0.0 1022.3 jit_solution(3153697958548902397)
XLA Ops:
  14.7 42.8 %all-reduce.17 = (bf16[2304]{0:T(1024)(128)(2,1)S(1)}, bf16[768]{0:T(1024)(128)(2,1)S(1)}, bf16[768]{0:T(1024)(128)(2,1)S(1)}, bf16[768]{0:T(1024)(128)(2,1)S(1)...) all-reduce(bf16[2304]{0:T(1024)(128)(2,1)S(1)} %dynamic-update-slic, ...), channel_id=1, replica_groups=mesh['dp'=8,'seq'=4] {'dp','seq'}, use_global_device_ids=true, to_apply=%add.2 | all-reduce | flops 9984 | bytes 39936
  60.4 13.4 %all-gather.13.cloned.1.call-done = bf16[768,2304]{1,0:T(8,128)(2,1)} async-done(((bf16[24,2304]{1,0:T(8,128)(2,1)}), bf16[768,2304]{1,0:T(8,128)(2,1)}) %all-gather.13.cloned.1.call-update) | async-done | bytes 3538960 | tf_op jit(solution)/shard_map/all_gather | solution.py:382
  73.8 3.3 fusion.111
  90.6 6.2 all-gather.27.cloned.1.call-done
  98.5 19.5 %all-gather.25.cloned.1.call-done = bf16[1024,768]{1,0:T(8,128)(2,1)} async-done(((bf16[256,768]{1,0:T(8,128)(2,1)}), bf16[1024,768]{1,0:T(8,128)(2,1)}) %all-gather.25.cloned.1.call-update) | async-done | bytes 1572880 | tf_op jit(solution)/shard_map/all_gather | solution.py:92
  120.3 21.1 %while.57 = (s32[]{:T(128)}, f32[1,256,12,64]{1,3,2,0:T(8,128)}, f32[1,256,12]{1,2,0:T(8,128)}, f32[1,256,12]{1,2,0:T(8,128)}, s32[2]{0:T(128)}, /*index=5*/s32[...) while((s32[]{:T(128)}, f32[1,256,12,64]{1,3,2,0:T(8,128)}, ...), condition=%wide.region_13.14_spmd.clone, body=%wide.region_10.13_spmd.clone.sunk | while | flops 431836928 | bytes 32726344 | solution.py:40
  124.6 3.8 fusion.304
  135.2 3.8 fusion.304
  143.9 31.0 %all-gather.15.cloned.1.call-done = bf16[768,768]{1,0:T(8,128)(2,1)} async-done(((bf16[24,768]{1,0:T(8,128)(2,1)}), bf16[768,768]{1,0:T(8,128)(2,1)}) %all-gather.15.cloned.1.call-update) | async-done | bytes 1179664 | tf_op jit(solution)/shard_map/all_gather | solution.py:384
  174.9 3.5 fusion.204
  178.4 16.6 %all-gather.23.cloned.1.call-done = bf16[1024,768]{1,0:T(8,128)(2,1)} async-done(((bf16[256,768]{1,0:T(8,128)(2,1)}), bf16[1024,768]{1,0:T(8,128)(2,1)}) %all-gather.23.cloned.1.call-update) | async-done | bytes 1572880 | tf_op jit(solution)/shard_map/all_gather | solution.py:93
  197.5 18.5 %all-gather.21.cloned.1.call-done = bf16[1024,768]{1,0:T(8,128)(2,1)} async-done(((bf16[256,768]{1,0:T(8,128)(2,1)}), bf16[1024,768]{1,0:T(8,128)(2,1)}) %all-gather.21.cloned.1.call-update) | async-done | bytes 1572880 | tf_op jit(solution)/shard_map/all_gather | solution.py:92
  221.7 21.4 %while.56 = (s32[]{:T(128)}, f32[1,256,12,64]{1,3,2,0:T(8,128)}, f32[1,256,12]{1,2,0:T(8,128)}, f32[1,256,12]{1,2,0:T(8,128)S(1)}, s32[2]{0:T(128)}, /*index=5*/...) while((s32[]{:T(128)}, f32[1,256,12,64]{1,3,2,0:T(8,128)}, ...), condition=%wide.region_5.6_spmd.clone, body=%wide.region_2.5_spmd.clone.sunk | while | flops 431836928 | bytes 32677164 | solution.py:40
  226.2 3.8 fusion.297
  236.7 3.8 fusion.297
  250.0 32.6 %all-gather.17.cloned.1.call-done = bf16[768,3072]{1,0:T(8,128)(2,1)} async-done(((bf16[24,3072]{1,0:T(8,128)(2,1)}), bf16[768,3072]{1,0:T(8,128)(2,1)}) %all-gather.17.cloned.1.call-update) | async-done | bytes 4718608 | tf_op jit(solution)/shard_map/all_gather | solution.py:388
  282.6 5.8 convolution_add_fusion.6
  288.4 3.2 convolution_add_fusion.5
  291.7 56.2 %all-gather.19.cloned.1.call-done = bf16[3072,768]{1,0:T(8,128)(2,1)} async-done(((bf16[96,768]{1,0:T(8,128)(2,1)}), bf16[3072,768]{1,0:T(8,128)(2,1)}) %all-gather.19.cloned.1.call-update) | async-done | bytes 4718608 | tf_op jit(solution)/shard_map/all_gather | solution.py:390
  347.9 6.9 convert_reduce_fusion.1
  354.9 3.8 convert_reduce_fusion
  379.2 3.4 broadcast.473.clone.1
  382.7 34.4 %while.58 = (s32[]{:T(128)}, f32[1,256,12,64]{1,3,2,0:T(8,128)}, f32[1,1024,1536]{1,2,0:T(8,128)}, bf16[2,1,512,768]{2,3,1,0:T(8,128)(2,1)S(1)}, s32[2]{0:T(128)...) while((s32[]{:T(128)}, f32[1,256,12,64]{1,3,2,0:T(8,128)}, ...), condition=%wide.region_20.21_spmd.clone, body=%wide.region_19.20_spmd.clone.sunk | while | flops 1034618624 | bytes 101936560 | solution.py:40
  387.1 3.6 fusion.319
  390.8 4.0 fusion.317
  404.1 3.6 fusion.319
  407.7 4.0 fusion.317
  417.1 5.0 convert_element_type.219
  422.7 3.6 broadcast.473.clone
  426.3 34.2 %while.59 = (s32[]{:T(128)}, f32[1,256,12,64]{1,3,2,0:T(8,128)}, f32[1,1024,1536]{1,2,0:T(8,128)}, bf16[2,1,512,768]{2,3,1,0:T(8,128)(2,1)S(1)}, s32[2]{0:T(128)...) while((s32[]{:T(128)}, f32[1,256,12,64]{1,3,2,0:T(8,128)}, ...), condition=%wide.region_28.29_spmd.clone, body=%wide.region_27.28_spmd.clone.sunk | while | flops 1034618624 | bytes 101936560 | solution.py:40
  430.5 3.6 fusion.335
  434.1 4.0 fusion.333
  447.5 3.6 fusion.335
  451.1 4.0 fusion.333
  460.5 5.0 convert_element_type.226
  469.1 4.3 fusion.167
  473.5 6.0 convolution_add_fusion.1
  483.0 5.2 convolution_add_fusion.2
  490.3 5.4 fusion.174
  495.7 6.5 reduce-scatter.9.cloned.1.call-done
  502.2 7.5 convolution_add_fusion
  512.9 5.5 fusion.133
  518.4 4.5 fusion.132
  530.0 40.9 %all-reduce.16 = (f32[768]{0:T(1024)S(1)}, f32[768]{0:T(1024)S(1)}, f32[2304]{0:T(1024)S(1)}, f32[768]{0:T(1024)S(1)}, f32[768]{0:T(1024)S(1)}, /*index=5*/f32[7...) all-reduce(f32[768]{0:T(1024)} %add.386, ...), channel_id=8, replica_groups=mesh['dp'=8,'seq'=4] {'dp','seq'}, use_global_device_ids=true, to_apply=%region_34.35.clone | all-reduce | flops 9984 | bytes 79872
  579.9 27.2 %reduce-scatter.13.cloned.1.call-done = f32[24,768]{1,0:T(8,128)} async-done(((f32[768,768]{1,0:T(8,128)}), f32[24,768]{1,0:T(8,128)}) %reduce-scatter.13.cloned.1.call-update) | async-done | bytes 73744 | tf_op jit(solution)/shard_map/reduce_scatter | solution.py:419
  607.1 142.0 %reduce-scatter.17.cloned.1.call-done = f32[96,768]{1,0:T(8,128)} async-done(((f32[3072,768]{1,0:T(8,128)}), f32[96,768]{1,0:T(8,128)}) %reduce-scatter.17.cloned.1.call-update) | async-done | bytes 294928 | tf_op jit(solution)/shard_map/reduce_scatter | solution.py:425
  749.2 141.1 %reduce-scatter.15.cloned.1.call-done = f32[24,3072]{1,0:T(8,128)} async-done(((f32[768,3072]{1,0:T(8,128)}), f32[24,3072]{1,0:T(8,128)}) %reduce-scatter.15.cloned.1.call-update) | async-done | bytes 294928 | tf_op jit(solution)/shard_map/reduce_scatter | solution.py:423
  890.2 125.1 %reduce-scatter.11.cloned.1.call-done = f32[24,2304]{1,0:T(8,128)} async-done(((f32[768,2304]{1,0:T(8,128)}), f32[24,2304]{1,0:T(8,128)}) %reduce-scatter.11.cloned.1.call-update) | async-done | bytes 221200 | tf_op jit(solution)/shard_map/reduce_scatter | solution.py:417
  (543 shorter events, 152.0 us)
Async XLA Ops:
  7.2 66.6 %all-gather.13.cloned.1.call-start = ((), (), s32[]{:S(2)}) async-start(), calls=%async_computation.6 | async-start | bytes 3649536 | tf_op jit(solution)/shard_map/all_gather | solution.py:382
  7.9 88.9 %all-gather.27.cloned.1.call-start = ((), (), s32[]{:S(2)}) async-start(), calls=%async_computation.19 | async-start | bytes 1966080 | tf_op jit(solution)/shard_map/all_gather | solution.py:93
  57.5 22.0 %copy-start.71 = (f32[768]{0:T(1024)}, f32[768]{0:T(1024)S(1)}, u32[]{:S(2)}) copy-start(f32[768]{0:T(1024)S(1)} %convert_element_type.192) | copy-start | bytes 9220
  57.5 22.0 %copy-start.73 = (f32[768]{0:T(1024)}, f32[768]{0:T(1024)S(1)}, u32[]{:S(2)}) copy-start(f32[768]{0:T(1024)S(1)} %convert_element_type.193) | copy-start | bytes 9220
  58.9 15.0 %copy-start.84 = (f32[256]{0:T(256)}, f32[256]{0:T(256)S(1)}, u32[]{:S(2)}) copy-start(f32[256]{0:T(256)S(1)} %get-tuple-element.725) | copy-start | bytes 3076
  58.9 20.7 %copy-start.75 = (f32[256]{0:T(256)}, f32[256]{0:T(256)S(1)}, u32[]{:S(2)}) copy-start(f32[256]{0:T(256)S(1)} %get-tuple-element.726) | copy-start | bytes 3076
  60.4 13.5 %copy-start.112 = (f32[256]{0:T(256)}, f32[256]{0:T(256)S(1)}, u32[]{:S(2)}) copy-start(f32[256]{0:T(256)S(1)} %get-tuple-element.565) | copy-start | bytes 3076
  60.4 19.1 %copy-start.114 = (f32[256]{0:T(256)}, f32[256]{0:T(256)S(1)}, u32[]{:S(2)}) copy-start(f32[256]{0:T(256)S(1)} %get-tuple-element.564) | copy-start | bytes 3076
  60.4 13.4 %copy-start.100 = (f32[256]{0:T(256)}, f32[256]{0:T(256)S(1)}, u32[]{:S(2)}) copy-start(f32[256]{0:T(256)S(1)} %fusion.184) | copy-start | bytes 3076
  78.2 39.9 %all-gather.25.cloned.1.call-start = ((), (), s32[]{:S(2)}) async-start(), calls=%async_computation.18 | async-start | bytes 1966080 | tf_op jit(solution)/shard_map/all_gather | solution.py:92
  78.9 96.0 %all-gather.15.cloned.1.call-start = ((), (), s32[]{:S(2)}) async-start(), calls=%async_computation.7 | async-start | bytes 1216512 | tf_op jit(solution)/shard_map/all_gather | solution.py:384
  79.5 115.5 %all-gather.23.cloned.1.call-start = ((), (), s32[]{:S(2)}) async-start(), calls=%async_computation.17 | async-start | bytes 1966080 | tf_op jit(solution)/shard_map/all_gather | solution.py:93
  83.8 132.3 %all-gather.21.cloned.1.call-start = ((), (), s32[]{:S(2)}) async-start(), calls=%async_computation.16 | async-start | bytes 1966080 | tf_op jit(solution)/shard_map/all_gather | solution.py:92
  84.4 198.2 %all-gather.17.cloned.1.call-start = ((), (), s32[]{:S(2)}) async-start(), calls=%async_computation.8 | async-start | bytes 4866048 | tf_op jit(solution)/shard_map/all_gather | solution.py:388
  85.1 262.8 %all-gather.19.cloned.1.call-start = ((), (), s32[]{:S(2)}) async-start(), calls=%async_computation.9 | async-start | bytes 4866048 | tf_op jit(solution)/shard_map/all_gather | solution.py:390
  85.9 404.3 %reduce-scatter.7.cloned.1.call-start = ((), (), s32[]{:S(2)}) async-start(), calls=%async_computation.10 | async-start | bytes 3932160 | tf_op jit(solution)/shard_map/reduce_scatter | solution.py:176
  141.3 56.2 %copy-start.2 = (bf16[2,1,512,768]{2,3,1,0:T(8,128)(2,1)}, bf16[2,1,512,768]{2,3,1,0:T(8,128)(2,1)S(1)}, u32[]{:S(2)}) copy-start(bf16[2,1,512,768]{2,3,1,0:T(8,128)(2,1)S(1)} %get-tuple-element.1219) | copy-start | bytes 4718596
  141.3 56.2 %copy-start.4 = (bf16[2,1,512,768]{2,3,1,0:T(8,128)(2,1)}, bf16[2,1,512,768]{2,3,1,0:T(8,128)(2,1)S(1)}, u32[]{:S(2)}) copy-start(bf16[2,1,512,768]{2,3,1,0:T(8,128)(2,1)S(1)} %get-tuple-element.1220) | copy-start | bytes 4718596
  141.3 56.2 %copy-start.7 = (bf16[1,256,12,64]{1,3,2,0:T(8,128)(2,1)}, bf16[1,256,12,64]{1,3,2,0:T(8,128)(2,1)S(1)}, u32[]{:S(2)}) copy-start(bf16[1,256,12,64]{1,3,2,0:T(8,128)(2,1)S(1)} %get-tuple-element.1223) | copy-start | bytes 1179652
  243.1 6.3 copy-start.62
  250.0 38.4 %copy-start.67 = (f32[768]{0:T(1024)S(1)}, f32[768]{0:T(1024)}, u32[]{:S(2)}) copy-start(f32[768]{0:T(1024)} %convert_element_type.199) | copy-start | bytes 9220
  250.0 38.4 %copy-start.69 = (f32[768]{0:T(1024)S(1)}, f32[768]{0:T(1024)}, u32[]{:S(2)}) copy-start(f32[768]{0:T(1024)} %convert_element_type.200) | copy-start | bytes 9220
  250.0 38.4 %copy-start.88 = (f32[256]{0:T(256)S(1)}, f32[256]{0:T(256)}, u32[]{:S(2)}) copy-start(f32[256]{0:T(256)} %copy-done.87) | copy-start | bytes 3076
  250.0 38.4 %copy-start.103 = (f32[256]{0:T(256)S(1)}, f32[256]{0:T(256)}, u32[]{:S(2)}) copy-start(f32[256]{0:T(256)} %fusion.185) | copy-start | bytes 3076
  282.6 5.8 copy-start.21
  282.6 5.8 copy-start.105
  282.6 5.8 copy-start.127
  347.9 7.0 copy-start.18
  347.9 7.0 copy-start.32
  347.9 7.0 copy-start.126
  347.9 10.7 %slice-start.4 = ((s8[4718592]{0:T(1024)(128)(4,1)}), s8[4194304]{0:T(1024)(128)(4,1)S(1)}, s32[]{:S(2)}) async-start(s8[4718592]{0:T(1024)(128)(4,1)} %bitcast.676), calls=%async_computation.24 | async-start | bytes 8388608
  367.0 9.7 copy-start.63
  387.1 9.4 slice-start.2
  404.1 9.4 slice-start.2
  407.7 5.8 slice-start.3
  422.1 80.1 %reduce-scatter.9.cloned.1.call-start = ((), (), s32[]{:S(2)}) async-start(), calls=%async_computation.11 | async-start | bytes 3932160 | tf_op jit(solution)/shard_map/reduce_scatter | solution.py:176
  430.5 9.4 slice-start
  447.5 9.4 slice-start
  465.5 141.6 %reduce-scatter.13.cloned.1.call-start = ((), (), s32[]{:S(2)}) async-start(), calls=%async_computation.13 | async-start | bytes 2433024 | tf_op jit(solution)/shard_map/reduce_scatter | solution.py:419
  469.0 280.1 %reduce-scatter.17.cloned.1.call-start = ((), (), s32[]{:S(2)}) async-start(), calls=%async_computation.15 | async-start | bytes 9732096 | tf_op jit(solution)/shard_map/reduce_scatter | solution.py:425
  479.6 410.7 %reduce-scatter.15.cloned.1.call-start = ((), (), s32[]{:S(2)}) async-start(), calls=%async_computation.14 | async-start | bytes 9732096 | tf_op jit(solution)/shard_map/reduce_scatter | solution.py:423
  488.3 527.1 %reduce-scatter.11.cloned.1.call-start = ((), (), s32[]{:S(2)}) async-start(), calls=%async_computation.12 | async-start | bytes 7299072 | tf_op jit(solution)/shard_map/reduce_scatter | solution.py:417
  490.3 12.0 %copy-start.39 = (bf16[1,256,12,64]{1,3,2,0:T(8,128)(2,1)S(1)}, bf16[1,256,12,64]{1,3,2,0:T(8,128)(2,1)}, u32[]{:S(2)}) copy-start(bf16[1,256,12,64]{1,3,2,0:T(8,128)(2,1)} %convert.25) | copy-start | bytes 1179652
  490.3 12.0 %copy-start.85 = (f32[256]{0:T(256)S(1)}, f32[256]{0:T(256)}, u32[]{:S(2)}) copy-start(f32[256]{0:T(256)} %copy-done.84) | copy-start | bytes 3076
  490.3 12.0 %copy-start.101 = (f32[256]{0:T(256)S(1)}, f32[256]{0:T(256)}, u32[]{:S(2)}) copy-start(f32[256]{0:T(256)} %copy-done.100) | copy-start | bytes 3076
  526.6 50.3 %copy-start.25 = (f32[256,768]{1,0:T(8,128)S(1)}, f32[256,768]{1,0:T(8,128)}, u32[]{:S(2)}) copy-start(f32[256,768]{1,0:T(8,128)} %copy-done.24) | copy-start | bytes 2359300
  526.6 50.3 %copy-start.27 = (f32[256,768]{1,0:T(8,128)S(1)}, f32[256,768]{1,0:T(8,128)}, u32[]{:S(2)}) copy-start(f32[256,768]{1,0:T(8,128)} %copy-done.26) | copy-start | bytes 2359300
  526.6 50.3 %copy-start.34 = (bf16[2,256,768]{2,1,0:T(8,128)(2,1)S(1)}, bf16[2,256,768]{2,1,0:T(8,128)(2,1)}, u32[]{:S(2)}) copy-start(bf16[2,256,768]{2,1,0:T(8,128)(2,1)} %param.24) | copy-start | bytes 2359300
  (124 other events, 294.4 us)
Sparse Core Ops, SparseCore 0:
  10.9 62.8 all-gather.12
  78.3 18.4 all-gather.26
  98.3 19.6 all-gather.24
  120.8 54.0 all-gather.14
  176.3 18.5 all-gather.22
  196.4 19.6 all-gather.20
  219.0 63.5 all-gather.16
  285.5 62.3 all-gather.18
  422.2 36.7 reduce-scatter.6
  465.6 36.5 reduce-scatter.8
  508.1 98.9 reduce-scatter.12
  614.4 134.6 reduce-scatter.16
  755.6 134.5 reduce-scatter.14
  897.3 117.9 reduce-scatter.10
where the time goes:
time: 1030 us; the launch traced here: 1020 us
  waiting for transfers between devices  640 us (62%)
  matrix products  147 us (14%)
  blocking collectives  83.7 us (8%)
  local copies, waits for them, and re-layouts  67.5 us (7%)
  other arithmetic  59.7 us (6%)
  between operations  15.6 us (2%)
    reduce_scatter x1, waiting for transfers between devices, body(): lax.psum_scatter(totals[10], ('dp', 'seq'), scatter_dimension=0, tiled=True)  142 us
    reduce_scatter x1, waiting for transfers between devices, body(): lax.psum_scatter(totals[8], ('dp', 'seq'), scatter_dimension=0, tiled=True)  141 us
    reduce_scatter x1, waiting for transfers between devices, body(): lax.psum_scatter(totals[2], ('dp', 'seq'), scatter_dimension=0, tiled=True)  125 us
    unnamed x2, blocking collectives  83.7 us
    all_gather x1, waiting for transfers between devices, body(): lax.all_gather(shards[10], ('dp', 'seq'), axis=0, tiled=True)  56.2 us
    all_gather x2, waiting for transfers between devices, attend(): lax.all_gather(key_flat, 'seq', axis=1, tiled=True)  38.1 us
    all_gather x1, waiting for transfers between devices, body(): lax.all_gather(shards[8], ('dp', 'seq'), axis=0, tiled=True)  32.6 us
    all_gather x1, waiting for transfers between devices, body(): lax.all_gather(shards[4], ('dp', 'seq'), axis=0, tiled=True)  31 us
  transfers between devices with their start and end apart: 14, of which 13 were waited for; matrix products, arithmetic and copies ran while one was open for 18% of the time, Pallas kernels for 0%

commit v1 on v0

--- a/solution.py
+++ b/solution.py
@@ -1,11 +1,809 @@
+import functools
+import numpy as np
 import jax
 import jax.numpy as jnp
 from jax import lax
+from jax.experimental import pallas as pl
+from jax.experimental.pallas import tpu as pltpu
 from jax.sharding import PartitionSpec as P
+
 
 HEADS = 12
 HEAD_DIM = 64
 MB = 2
+
+F32 = jnp.float32
+BF = jnp.bfloat16
+EPS = 1e-05
+MESH = pl.DeviceIdType.MESH
+NEG = -1e30
+ANY = pl.BlockSpec(memory_space=pl.ANY)
+VM = pl.BlockSpec(memory_space=pltpu.VMEM)
+SM = pl.BlockSpec(memory_space=pltpu.SMEM)
+WIDTHS = (24, 24, 72, 24, 24, 24, 96, 24)
+
+
+def places():
+    dp = lax.axis_index("dp")
+    sq = lax.axis_index("seq")
+    return dp // 2, dp % 2, sq // 2, sq % 2
+
+
+def device(z, x, y, c):
+    return (z * 2 + x, y * 2 + c)
+
+
+def spread_row(gathered, index, width):
+    total = 32 * width
+    owner = lax.broadcasted_iota(jnp.int32, (32, 256), 0)
+    place = lax.broadcasted_iota(jnp.int32, (32, 256), 1)
+    pick = jnp.where(place == owner * 8 + index, 1.0, 0.0).astype(BF)
+    mine = jnp.dot(pick, gathered, preferred_element_type=F32).astype(BF)
+    column = lax.broadcasted_iota(jnp.int32, (1, total), 1).astype(F32)
+    row_of = jnp.floor((column + 0.5) * (1.0 / width))
+    rest = (column - row_of * width).astype(jnp.int32)
+    row_of = row_of.astype(jnp.int32)
+    spread = jnp.where(lax.broadcasted_iota(jnp.int32, (128, total), 0) == rest, 1.0, 0.0).astype(BF)
+    full = jnp.dot(mine, spread, preferred_element_type=F32)
+    keep = lax.broadcasted_iota(jnp.int32, (32, total), 0) == row_of
+    return jnp.sum(jnp.where(keep, full, 0.0), axis=0, keepdims=True)
+
+
+def forward_kernel(
+    prefix, tok, cot, vec_s, wq_s, wo_s, wu_s, wd_s,
+    wq, wo, wu, wd, gv, cots, attl_out, xs, n1t_out, qs_out, qst_out, k_out, v_out, att_out, lt_out, vrows,
+    tok_all, gvm, wqm, vt, attl, n1, ssem, rsem, lsem,
+):
+    z, x, y, c = places()
+    x2, y2, c2 = 1 - x, 1 - y, 1 - c
+    px, py, pc = device(z, x2, y, c), device(z, x, y2, c), device(z, x, y, c2)
+    zs = [lax.rem(z + d, 4) for d in (1, 2, 3)]
+    pz = [device(zz, x, y, c) for zz in zs]
+
+    sent = []
+    counts = [0, 0]
+
+    def remote(src, dst, dev):
+        i = counts[0]
+        counts[0] += 1
+        copy = pltpu.make_async_remote_copy(
+            src_ref=src, dst_ref=dst, send_sem=ssem.at[i], recv_sem=rsem.at[i],
+            device_id=dev, device_id_type=MESH)
+        copy.start()
+        sent.append(copy)
+        return copy
+
+    def local(src, dst):
+        i = counts[1]
+        counts[1] += 1
+        copy = pltpu.make_async_copy(src, dst, lsem.at[i])
+        copy.start()
+        return copy
+
+    def arrive(copies):
+        for copy in copies:
+            copy.wait_recv()
+
+    def landed(copies):
+        for copy in copies:
+            copy.wait()
+
+    barrier = pltpu.get_barrier_semaphore()
+    for dev in [px, py, pc] + pz:
+        pl.semaphore_signal(barrier, inc=1, device_id=dev, device_id_type=MESH)
+    pl.semaphore_wait(barrier, 6)
+
+    width = 768
+    third = 384
+
+    def shard(xx, yy, cc):
+        return pl.ds(pl.multiple_of(((xx * 2 + yy) * 2 + cc) * 24, 8), 24)
+
+    own_vec = [local(vec_s, gv.at[z, x, y, c])]
+    vec_c = [remote(vec_s, gv.at[z, x, y, c], pc)]
+    tok_y = [remote(tok.at[y2], tok_all.at[y, c], py)]
+    own_tok = [local(tok.at[y], tok_all.at[y, c])]
+    own_wq, wq_c = [], []
+    for kind in range(3):
+        there = pl.ds(kind * third, third)
+        mine_cols = pl.ds(pl.multiple_of(kind * width + c * third, 128), third)
+        peer_cols = pl.ds(pl.multiple_of(kind * width + c2 * third, 128), third)
+        own_wq.append(local(wq_s.at[:, mine_cols], wq.at[z, shard(x, y, c), there]))
+        wq_c.append(remote(wq_s.at[:, peer_cols], wq.at[z, shard(x, y, c), there], pc))
+    own_w = [local(s, w.at[z, x, y, c]) for s, w in ((wo_s, wo), (wu_s, wu), (wd_s, wd))]
+    own_cot = [local(cot.at[y], cots.at[y])]
+
+    landed(own_vec)
+    arrive(vec_c)
+    vec_z = [remote(gv.at[z, x, y], gv.at[z, x, y], dev) for dev in pz]
+    landed(own_wq)
+    arrive(wq_c)
+    both = pl.ds(pl.multiple_of((x * 2 + y) * 48, 16), 48)
+    wq_z = [remote(wq.at[z, both], wq.at[z, both], dev) for dev in pz]
+    landed(own_tok)
+    arrive(tok_y)
+    own_xs = local(tok_all.at[:, c], xs)
+    tok_c = [remote(tok_all.at[:, c], tok_all.at[:, c], pc)]
+    arrive(vec_z)
+    vec_x = [remote(gv.at[:, x, y], gv.at[:, x, y], px)]
+    arrive(vec_x)
+    vec_y = [remote(gv.at[:, :, y], gv.at[:, :, y], py)]
+    arrive(tok_c)
+    arrive(vec_y)
+    gcopy = local(gv, gvm)
+    gcopy.wait()
+    table = gvm[...].reshape(256, 128)
+    for index, wide in enumerate(WIDTHS):
+        vrows[index : index + 1, 0 : 32 * wide] = spread_row(table, index, wide)
+    gain = vrows[0:1, 0:width]
+    shift = vrows[1:2, 0:width]
+
+    def norm_block(b, carry):
+        yy, cc = b // 2, lax.rem(b, 2)
+        rows = tok_all[yy, cc].astype(F32)
+        centre = rows - jnp.mean(rows, axis=-1, keepdims=True)
+        spread = jnp.mean(centre * centre, axis=-1, keepdims=True)
+        normed = (centre * lax.rsqrt(spread + EPS) * gain + shift).astype(BF)
+        rows_at = pl.ds(pl.multiple_of(b * 256, 256), 256)
+        n1[rows_at, :] = normed
+        n1t_out[:, rows_at] = normed.astype(F32).T.astype(BF)
+        return carry
+
+    lax.fori_loop(0, 4, norm_block, 0)
+
+    arrive(wq_z)
+    wq_1 = [remote(wq.at[:, shard(x, y, 0)], wq.at[:, shard(x, y, 0)], px),
+            remote(wq.at[:, shard(x, y, 1)], wq.at[:, shard(x, y, 1)], py)]
+    landed(own_w)
+    wo_z = [remote(wo_s, wo.at[z, x, y, c], dev) for dev in pz]
+    wu_z = [remote(wu_s, wu.at[z, x, y, c], dev) for dev in pz]
+
+    def spread_1(w):
+        half = w.shape[5] // 2
+        return [remote(w.at[:, x, y, c, :, 0:half], w.at[:, x, y, c, :, 0:half], px),
+                remote(w.at[:, x, y, c, :, half:], w.at[:, x, y, c, :, half:], py)]
+
+    def spread_2(w):
+        half = w.shape[5] // 2
+        return [remote(w.at[:, :, y, c, :, 0:half], w.at[:, :, y, c, :, 0:half], py),
+                remote(w.at[:, x, :, c, :, half:], w.at[:, x, :, c, :, half:], px)]
+
+    def spread_3(w):
+        return [remote(w.at[:, :, :, c], w.at[:, :, :, c], pc)]
+
+    arrive(wq_1)
+    wq_2 = [remote(wq.at[:, shard(i, y, 0)], wq.at[:, shard(i, y, 0)], py) for i in range(2)]
+    wq_2 += [remote(wq.at[:, shard(x, i, 1)], wq.at[:, shard(x, i, 1)], px) for i in range(2)]
+    wd_z = [remote(wd_s, wd.at[z, x, y, c], dev) for dev in pz]
+    arrive(wq_2)
+    arrive(wo_z)
+    wo_1 = spread_1(wo)
+    arrive(wu_z)
+    wu_1 = spread_1(wu)
+    gather_q = local(wq.reshape(width, 3 * third), wqm)
+    gather_q.wait()
+
+    def project(b, carry):
+        rows = pl.ds(pl.multiple_of(b * 256, 256), 256)
+        block = n1[rows, :]
+        parts = []
+        for kind in range(3):
+            bias = vrows[2:3, pl.ds(pl.multiple_of(kind * width + c * third, 128), third)]
+            value = jnp.dot(block, wqm[:, kind * third : (kind + 1) * third], preferred_element_type=F32)
+            parts.append((value + bias).astype(BF))
+        qs = (parts[0].astype(F32) * 0.125)
+        qs_out[rows, :] = qs.astype(BF)
+        qst_out[:, rows] = qs.T.astype(BF)
+        k_out[rows, :] = parts[1]
+        v_out[rows, :] = parts[2]
+        vt[:, rows] = parts[2].astype(F32).T.astype(BF)
+        return carry
+
+    lax.fori_loop(0, 4, project, 0)
+
+    limit = prefix[y] - 1
+    sub = lax.broadcasted_iota(jnp.int32, (128, 256), 0)
+
+    def attend(block):
+        rows = min(4, max(block + 1, 2)) * 256
+        qcols = pl.ds(block * 256, 256)
+
+        def unit(u, carry):
+            cols = pl.ds(pl.multiple_of(u * 128, 128), 128)
+            keys = k_out[0:rows, cols]
+            queries = qst_out[cols, qcols]
+            qpos = block * 256 + lax.broadcasted_iota(jnp.int32, (1, 256), 1)
+            bound = jnp.maximum(qpos, limit)
+            seen = lax.broadcasted_iota(jnp.int32, (rows, 256), 0) <= bound
+            for half in range(2):
+                chosen = jnp.where(sub // 64 == half, queries, jnp.zeros_like(queries))
+                scores = jnp.dot(keys, chosen, preferred_element_type=F32)
+                size = jnp.where(seen, jnp.abs(scores), NEG)
+                top = jnp.max(size, axis=0, keepdims=True)
+                exponent = jnp.exp(size - top)
+                total = jnp.sum(exponent, axis=0, keepdims=True)
+                weights = jnp.where(scores > 0, exponent, jnp.where(scores < 0, -exponent, 0.0)).astype(BF)
+                values = vt[pl.ds(pl.multiple_of(u * 128 + half * 64, 64), 64), 0:rows]
+                result = jnp.dot(values, weights, preferred_element_type=F32) / total
+                att_out[pl.ds(pl.multiple_of(u * 128 + half * 64, 64), 64), qcols] = result
+                lt_out[pl.ds(u * 2 + half, 1), qcols] = top + jnp.log(total)
+            both = att_out[cols, qcols]
+            attl[block // 2, block % 2, :, cols] = both.T.astype(BF)
+            return carry
+
+        lax.fori_loop(0, 3, unit, 0)
+
+    lt_out[...] = jnp.zeros_like(lt_out)
+    attend(3)
+    arrive(wo_1)
+    wo_2 = spread_2(wo)
+    arrive(wu_1)
+    wu_2 = spread_2(wu)
+    arrive(wd_z)
+    wd_1 = spread_1(wd)
+    cot_y = [remote(cot.at[y2], cots.at[y], py)]
+    attend(2)
+    arrive(wo_2)
+    wo_3 = spread_3(wo)
+    attend(1)
+    attend(0)
+    mine_cols = pl.ds(pl.multiple_of(c * third, 128), third)
+    own_att = local(attl.at[:, c], attl_out.at[:, :, mine_cols])
+    att_c = [remote(attl.at[:, c2], attl_out.at[:, :, mine_cols], pc)]
+    arrive(wu_2)
+    wu_3 = spread_3(wu)
+    arrive(wd_1)
+    wd_2 = spread_2(wd)
+    arrive(wd_2)
+    wd_3 = spread_3(wd)
+    own_att.wait()
+    own_xs.wait()
+    landed(own_cot)
+    arrive(att_c + cot_y + wo_3 + wu_3 + wd_3)
+    for copy in sent:
+        copy.wait_send()
+
+
+N_REMOTE = 64
+N_LOCAL = 24
+
+
+def forward_call(prefix, tok, cot, vec_s, wq_s, wo_s, wu_s, wd_s):
+    sds = jax.ShapeDtypeStruct
+    out_shape = (
+        sds((4, 192, 1152), BF), sds((4, 2, 2, 2, 24, 768), BF), sds((4, 2, 2, 2, 24, 3072), BF),
+        sds((4, 2, 2, 2, 96, 768), BF), sds((4, 2, 2, 2, 8, 128), BF), sds((2, 256, 768), BF), sds((2, 256, 768), BF), sds((2, 256, 768), BF),
+        sds((768, 1024), BF), sds((1024, 384), BF), sds((384, 1024), BF), sds((1024, 384), BF), sds((1024, 384), BF),
+        sds((384, 1024), F32), sds((8, 1024), F32), sds((8, 3072), F32),
+    )
+    return pl.pallas_call(
+        forward_kernel,
+        out_shape=out_shape,
+        in_specs=[SM] + [ANY] * 7,
+        out_specs=(ANY,) * 8 + (VM,) * 8,
+        scratch_shapes=[
+            pltpu.VMEM((2, 2, 256, 768), BF), pltpu.VMEM((4, 2, 2, 2, 8, 128), BF), pltpu.VMEM((768, 1152), BF),
+            pltpu.VMEM((384, 1024), BF), pltpu.VMEM((2, 2, 256, 384), BF), pltpu.VMEM((1024, 768), BF),
+            pltpu.SemaphoreType.DMA((N_REMOTE,)), pltpu.SemaphoreType.DMA((N_REMOTE,)),
+            pltpu.SemaphoreType.DMA((N_LOCAL,)),
+        ],
+        compiler_params=pltpu.CompilerParams(
+            collective_id=0, has_side_effects=True, vmem_limit_bytes=56 * 2**20),
+    )(prefix, tok, cot, vec_s, wq_s, wo_s, wu_s, wd_s)
+
+
+def pack_vectors(vectors):
+    return jnp.stack([jnp.pad(v, (0, 128 - v.shape[0])) for v in vectors])
+
+
+def collect_rows(vector, wide):
+    total = 32 * wide
+    column = lax.broadcasted_iota(jnp.int32, (1, total), 1).astype(F32)
+    row_of = jnp.floor((column + 0.5) * (1.0 / wide))
+    rest = (column - row_of * wide).astype(jnp.int32)
+    row_of = row_of.astype(jnp.int32)
+    gather = jnp.where(lax.broadcasted_iota(jnp.int32, (128, total), 0) == rest, 1.0, 0.0).astype(BF)
+    keep = lax.broadcasted_iota(jnp.int32, (32, total), 0) == row_of
+    high = vector.astype(BF).astype(F32)
+    low = vector - high
+    dims = (((1,), (1,)), ((), ()))
+    out = None
+    for part in (high, low):
+        placed = jnp.where(keep, part, 0.0).astype(BF)
+        term = lax.dot_general(placed, gather, dims, preferred_element_type=F32)
+        out = term if out is None else out + term
+    return out
+
+
+def add_into(ref, at, other):
+    ref[at] = (ref[at].astype(F32) + other.astype(F32)).astype(BF)
+
+
+def backward_kernel(
+    prefix, gd, gu, go, bo, ga, wq, n1t, xs, gmid, qs, qst, k, v, att, lt, vrows,
+    vb_out, vg2, vb2, vb_up, vb_down,
+    out_bo, out_gt, out_q, out_o, out_u, out_d, out_vec,
+    ld, lu, lo, r0d, r0u, r0o, r1ad, r1bd, r1au, r1bu, r1ao, r1bo, r2ad, r2bd, r2au, r2bu, r2ao, r2bo, r3d, r3u, r3o,
+    ga_all, gt, kt, dk, dv, gp, gpu, qbuf, qr1a, qr1b, qr2a, qr2b, qr3, qsend, qrecv,
+    wqm, n1m, gmm, part_send, part_own, part_recv, gtb, vsum, vbq, vtab, vr0, vr1, vr2, vr3,
+    ssem, rsem, lsem,
+):
+    z, x, y, c = places()
+    x2, y2, c2 = 1 - x, 1 - y, 1 - c
+    px, py, pc = device(z, x2, y, c), device(z, x, y2, c), device(z, x, y, c2)
+    zs = [lax.rem(z + d, 4) for d in (1, 2, 3)]
+    pz = [device(zz, x, y, c) for zz in zs]
+    third = 384
+    width = 768
+
+    def remote(i, src, dst, dev):
+        return pltpu.make_async_remote_copy(
+            src_ref=src, dst_ref=dst, send_sem=ssem.at[i], recv_sem=rsem.at[i],
+            device_id=dev, device_id_type=MESH)
+
+    ids = [0]
+
+    def fresh(count=1):
+        first = ids[0]
+        ids[0] += count
+        return first
+
+    def start(copies):
+        for copy in copies:
+            copy.start()
+
+    def arrive(copies):
+        for copy in copies:
+            copy.wait_recv()
+
+    def gone(copies):
+        for copy in copies:
+            copy.wait_send()
+
+    barrier = pltpu.get_barrier_semaphore()
+    for dev in [px, py, pc] + pz:
+        pl.semaphore_signal(barrier, inc=1, device_id=dev, device_id_type=MESH)
+    pl.semaphore_wait(barrier, 6)
+
+    locals_used = [0]
+
+    def local(src, dst):
+        i = locals_used[0]
+        locals_used[0] += 1
+        return pltpu.make_async_copy(src, dst, lsem.at[i])
+
+    mine_cols = pl.ds(pl.multiple_of(c * third, 128), third)
+    peer_cols = pl.ds(pl.multiple_of(c2 * third, 128), third)
+    ga_own = local(ga.at[:, :, mine_cols], ga_all.at[:, c])
+    ga_own.start()
+    ga_c = [remote(fresh(), ga.at[:, :, peer_cols], ga_all.at[:, c], pc)]
+    start(ga_c)
+    bo_own = local(bo.at[y], out_bo.at[y])
+    bo_own.start()
+    bo_y = [remote(fresh(), bo.at[y2], out_bo.at[y], py)]
+    start(bo_y)
+
+    class Scatter:
+        def __init__(self, grad, held, r0, r1a, r1b, r2a, r2b, r3, out):
+            half = out.shape[1] // 2
+            self.half, self.held, self.out = half, held, out
+            self.r0, self.r1a, self.r1b, self.r2a, self.r2b, self.r3 = r0, r1a, r1b, r2a, r2b, r3
+            self.mine = local(grad.at[:, :, :, c], held)
+            self.c0 = [remote(fresh(), grad.at[:, :, :, c2], r0, pc)]
+            self.c1 = [remote(fresh(), held.at[:, :, y2, :, 0:half], r1a, py),
+                       remote(fresh(), held.at[:, x2, :, :, half:], r1b, px)]
+            self.c2 = [remote(fresh(), held.at[:, x2, y, :, 0:half], r2a, px),
+                       remote(fresh(), held.at[:, x, y2, :, half:], r2b, py)]
+            self.c3 = [remote(fresh(), held.at[zs[d], x, y], r3.at[d], pz[d]) for d in range(3)]
+
+        def s0(self):
+            self.mine.start()
+            start(self.c0)
+
+        def s1(self):
+            self.mine.wait()
+            arrive(self.c0)
+
+            def add(i, carry):
+                zz, xx, yy = i // 4, lax.rem(i // 2, 2), lax.rem(i, 2)
+                add_into(self.held, (zz, xx, yy), self.r0[zz, xx, yy])
+                return carry
+
+            lax.fori_loop(0, 16, add, 0)
+            start(self.c1)
+
+        def s2(self):
+            arrive(self.c1)
+
+            def add(i, carry):
+                zz, other = i // 2, lax.rem(i, 2)
+                add_into(self.held, (zz, other, y, slice(None), slice(0, self.half)), self.r1a[zz, other])
+                add_into(self.held, (zz, x, other, slice(None), slice(self.half, None)), self.r1b[zz, other])
+                return carry
+
+            lax.fori_loop(0, 8, add, 0)
+            start(self.c2)
+
+        def s3(self):
+            arrive(self.c2)
+
+            def add(zz, carry):
+                add_into(self.held, (zz, x, y, slice(None), slice(0, self.half)), self.r2a[zz])
+                add_into(self.held, (zz, x, y, slice(None), slice(self.half, None)), self.r2b[zz])
+                return carry
+
+            lax.fori_loop(0, 4, add, 0)
+            start(self.c3)
+
+        def s4(self):
+            arrive(self.c3)
+            self.out[...] = (self.held[z, x, y].astype(F32) + self.r3[0].astype(F32)
+                             + self.r3[1].astype(F32) + self.r3[2].astype(F32))
+
+        def sends(self):
+            return self.c0 + self.c1 + self.c2 + self.c3
+
+    down = Scatter(gd, ld, r0d, r1ad, r1bd, r2ad, r2bd, r3d, out_d)
+    up = Scatter(gu, lu, r0u, r1au, r1bu, r2au, r2bu, r3u, out_u)
+    outp = Scatter(go, lo, r0o, r1ao, r1bo, r2ao, r2bo, r3o, out_o)
+    down.s0()
+    up.s0()
+    outp.s0()
+    late = [local(wq, wqm), local(n1t, n1m), local(gmid, gmm)]
+    start(late)
+
+    q1a, q1b, q2a, q2b = fresh(3), fresh(3), fresh(3), fresh(3)
+    q3 = [fresh(3) for d in range(3)]
+    q4 = fresh(3)
+
+    class QScatter:
+        def __init__(self, u):
+            self.u = u
+            buf = qbuf.at[u]
+            self.buf = buf
+            self.c1 = [remote(q1a + u, buf.at[:, :, y2, 0], qr1a.at[u], py),
+                       remote(q1b + u, buf.at[:, x2, :, 1], qr1b.at[u], px)]
+            self.c2 = [remote(q2a + u, buf.at[:, x2, y, 0], qr2a.at[u], px),
+                       remote(q2b + u, buf.at[:, x, y2, 1], qr2b.at[u], py)]
+            self.c3 = [remote(q3[d] + u, buf.at[zs[d], x, y], qr3.at[u, d], pz[d]) for d in range(3)]
+            self.c4 = [remote(q4 + u, qsend.at[u], qrecv.at[u], pc)]
+
+        def s1(self):
+            start(self.c1)
+
+        def s2(self):
+            u = self.u
+            arrive(self.c1)
+
+            def add(i, carry):
+                zz, other = i // 2, lax.rem(i, 2)
+                add_into(qbuf, (u, zz, other, y, 0), qr1a[u, zz, other])
+                add_into(qbuf, (u, zz, x, other, 1), qr1b[u, zz, other])
+                return carry
+
+            lax.fori_loop(0, 8, add, 0)
+            start(self.c2)
+
+        def s3(self):
+            u = self.u
+            arrive(self.c2)
+
+            def add(zz, carry):
+                add_into(qbuf, (u, zz, x, y, 0), qr2a[u, zz])
+                add_into(qbuf, (u, zz, x, y, 1), qr2b[u, zz])
+                return carry
+
+            lax.fori_loop(0, 4, add, 0)
+            start(self.c3)
+
+        def total(self, cs):
+            u = self.u
+            return (qbuf[u, z, x, y, cs].astype(F32) + qr3[u, 0, cs].astype(F32)
+                    + qr3[u, 1, cs].astype(F32) + qr3[u, 2, cs].astype(F32))
+
+        def put(self, value, core):
+            for kind in range(3):
+                cols = pl.ds(pl.multiple_of(kind * width + core * third + self.u * 128, 128), 128)
+                out_q[:, cols] = value[:, kind * 128 : (kind + 1) * 128]
+
+        def s4(self):
+            arrive(self.c3)
+            qsend[self.u] = self.total(c2)
+            start(self.c4)
+            self.put(self.total(c), c)
+
+        def s5(self):
+            arrive(self.c4)
+            self.put(qrecv[self.u], c2)
+
+        def sends(self):
+            return self.c1 + self.c2 + self.c3 + self.c4
+
+    queue = [QScatter(u) for u in range(3)]
+    slots = {
+        (0, 3): [down.s1], (0, 2): [up.s1], (0, 1): [outp.s1], (0, 0): [down.s2],
+        (1, 3): [], (1, 2): [up.s2], (1, 1): [outp.s2, down.s3], (1, 0): [up.s3],
+        (2, 3): [queue[0].s2, outp.s3], (2, 2): [down.s4], (2, 1): [queue[0].s3], (2, 0): [],
+    }
+
+    ga_own.wait()
+    arrive(ga_c)
+    limit = prefix[y] - 1
+    sub = lax.broadcasted_iota(jnp.int32, (128, 256), 0)
+    lane = lax.broadcasted_iota(jnp.int32, (256, 128), 1)
+    vbq[...] = jnp.zeros_like(vbq)
+
+    def unit(u, carry):
+        cols = pl.ds(pl.multiple_of(u * 128, 128), 128)
+        for b in range(4):
+            rows = slice(b * 256, (b + 1) * 256)
+            gt[:, rows] = ga_all[b // 2, b % 2, :, cols].astype(F32).T.astype(BF)
+            kt[:, rows] = k[rows, cols].astype(F32).T.astype(BF)
+        dk[...] = jnp.zeros_like(dk)
+        dv[...] = jnp.zeros_like(dv)
+        for block in (3, 2, 1, 0):
+            rows = min(4, max(block + 1, 2)) * 256
+            qrange = slice(block * 256, (block + 1) * 256)
+            keys = k[0:rows, cols]
+            values = v[0:rows, cols]
+            queries_t = qst[cols, qrange]
+            grads_t = gt[:, qrange]
+            queries = qs[qrange, cols]
+            grads = ga_all[block // 2, block % 2, :, cols]
+            qpos = block * 256 + lax.broadcasted_iota(jnp.int32, (1, 256), 1)
+            bound = jnp.maximum(qpos, limit)
+            seen = lax.broadcasted_iota(jnp.int32, (rows, 256), 0) <= bound
+            prod = grads_t.astype(F32) * att[cols, qrange]
+            dqs, dks, dvs = [], None, None
+            for half in range(2):
+                part = slice(half * 64, half * 64 + 64)
+                in_sub = sub // 64 == half
+                in_lane = lane // 64 == half
+                delta = jnp.sum(prod[part], axis=0, keepdims=True)
+                total = lt[pl.ds(u * 2 + half, 1), qrange]
+                zero = jnp.zeros((), BF)
+                scores = jnp.dot(keys, jnp.where(in_sub, queries_t, zero), preferred_element_type=F32)
+                pull = jnp.dot(values, jnp.where(in_sub, grads_t, zero), preferred_element_type=F32)
+                share = jnp.exp(jnp.where(seen, jnp.abs(scores) - total, NEG))
+                signed = jnp.where(scores > 0, share, jnp.where(scores < 0, -share, 0.0))
+                grad_scores = (share * pull - signed * delta).astype(BF)
+                signed = signed.astype(BF)
+                dvt = jnp.dot(signed, jnp.where(in_lane, grads, zero), preferred_element_type=F32)
+                dkt = jnp.dot(grad_scores, jnp.where(in_lane, queries, zero), preferred_element_type=F32)
+                dvs = dvt if dvs is None else dvs + dvt
+                dks = dkt if dks is None else dks + dkt
+                dqs.append(jnp.dot(kt[part, 0:rows], grad_scores, preferred_element_type=F32))
+            dk[0:rows, :] += dks
+            dv[0:rows, :] += dvs
+            gpu[qrange, 0:128] = (jnp.concatenate(dqs, axis=0).T * 0.125).astype(BF)
+            for which in range(3):
+                if slots[which, block]:
+                    @pl.when(u == which)
+                    def _():
+                        for step in slots[which, block]:
+                            step()
+        gpu[:, 128:256] = dk[...].astype(BF)
+        gpu[:, 256:384] = dv[...].astype(BF)
+        sums = jnp.sum(gpu[...].astype(F32), axis=0, keepdims=True)
+        for kind in range(3):
+            part = slice(kind * 128, (kind + 1) * 128)
+            vbq[0:1, pl.ds(pl.multiple_of(kind * width + c * third + u * 128, 128), 128)] = sums[:, part]
+            gp[:, pl.ds(pl.multiple_of(kind * third + u * 128, 128), 128)] = gpu[:, part]
+
+        @pl.when(u == 0)
+        def _():
+            late[1].wait()
+
+        def weights(i, inner):
+            zz, xx = i // 2, lax.rem(i, 2)
+            block = jnp.dot(n1m[pl.ds(pl.multiple_of(i * 96, 32), 96), :], gpu[...], preferred_element_type=F32)
+            for j in range(4):
+                qbuf[u, zz, xx, j // 2, j % 2] = block[j * 24 : (j + 1) * 24].astype(BF)
+            return inner
+
+        lax.fori_loop(0, 8, weights, 0)
+        QScatter(u).s1()
+        return carry
+
+    lax.fori_loop(0, 3, unit, 0)
+
+    late[0].wait()
+    late[2].wait()
+    dims = (((1,), (1,)), ((), ()))
+
+    def back_rows(b):
+        return lax.dot_general(gp[pl.ds(pl.multiple_of(b * 256, 256), 256), :], wqm[...], dims,
+                               preferred_element_type=F32)
+
+    def back_peer(yy, carry):
+        part_send[yy] = back_rows(yy * 2 + c2)
+        return carry
+
+    lax.fori_loop(0, 2, back_peer, 0)
+    part_c = [remote(fresh(), part_send, part_recv, pc)]
+    start(part_c)
+    queue[1].s2()
+
+    def back_own(yy, carry):
+        part_own[yy] = back_rows(yy * 2 + c)
+        return carry
+
+    lax.fori_loop(0, 2, back_own, 0)
+    queue[2].s2()
+    up.s4()
+    outp.s4()
+    queue[0].s4()
+    gain = vrows[0:1, 0:width]
+    vsum[...] = jnp.zeros_like(vsum)
+    arrive(part_c)
+
+    def norm_back(yy, carry):
+        rows = xs[yy].astype(F32)
+        centre = rows - jnp.mean(rows, axis=-1, keepdims=True)
+        scale = lax.rsqrt(jnp.mean(centre * centre, axis=-1, keepdims=True) + EPS)
+        unit_rows = centre * scale
+        grad = part_own[yy] + part_recv[yy]
+        vsum[0:1, :] += jnp.sum(grad * unit_rows, axis=0, keepdims=True)
+        vsum[1:2, :] += jnp.sum(grad, axis=0, keepdims=True)
+        grad = grad * gain
+        inner = (grad - jnp.mean(grad, axis=-1, keepdims=True)
+                 - unit_rows * jnp.mean(grad * unit_rows, axis=-1, keepdims=True))
+        gtb[yy] = (gmm[yy] + scale * inner).astype(BF)
+        return carry
+
+    lax.fori_loop(0, 2, norm_back, 0)
+    gt_own = local(gtb.at[y], out_gt.at[y])
+    gt_own.start()
+    gt_y = [remote(fresh(), gtb.at[y2], out_gt.at[y], py)]
+    start(gt_y)
+    queue[1].s3()
+    vectors = (vsum[0:1, :], vsum[1:2, :], vbq[...], vb_out[...], vg2[...], vb2[...], vb_up[...], vb_down[...])
+    for index, wide in enumerate(WIDTHS):
+        vtab[pl.ds(index, 32, stride=8), :] = collect_rows(vectors[index], wide)
+    table = vtab.reshape(4, 2, 2, 2, 8, 128)
+    v0 = [remote(fresh(), table.at[:, :, :, c2], vr0, pc)]
+    v1 = [remote(fresh(), table.at[:, :, y2, c], vr1, py)]
+    v2 = [remote(fresh(), table.at[:, x2, y, c], vr2, px)]
+    v3 = [remote(fresh(), table.at[zs[d], x, y, c], vr3.at[d], pz[d]) for d in range(3)]
+
+    def tile(zz, xx, yy):
+        return pl.ds(pl.multiple_of((((zz * 2 + xx) * 2 + yy) * 2 + c) * 8, 8), 8)
+
+    start(v0)
+    queue[2].s3()
+    arrive(v0)
+
+    def add_core(i, carry):
+        zz, xx, yy = i // 4, lax.rem(i // 2, 2), lax.rem(i, 2)
+        vtab[tile(zz, xx, yy), :] += vr0[zz, xx, yy]
+        return carry
+
+    lax.fori_loop(0, 16, add_core, 0)
+    start(v1)
+    queue[1].s4()
+    queue[0].s5()
+    arrive(v1)
+
+    def add_y(i, carry):
+        vtab[tile(i // 2, lax.rem(i, 2), y), :] += vr1[i // 2, lax.rem(i, 2)]
+        return carry
+
+    lax.fori_loop(0, 8, add_y, 0)
+    start(v2)
+    queue[2].s4()
+    arrive(v2)
+
+    def add_x(zz, carry):
+        vtab[tile(zz, x, y), :] += vr2[zz]
+        return carry
+
+    lax.fori_loop(0, 4, add_x, 0)
+    start(v3)
+    queue[1].s5()
+    queue[2].s5()
+    arrive(v3)
+    out_vec[...] = vtab[tile(z, x, y), :] + vr3[0] + vr3[1] + vr3[2]
+    gt_own.wait()
+    bo_own.wait()
+    arrive(gt_y + bo_y)
+    gone(ga_c + bo_y + down.sends() + up.sends() + outp.sends() + part_c + gt_y + v0 + v1 + v2 + v3)
+    for u in range(3):
+        gone(queue[u].sends())
+
+
+def backward_call(*operands):
+    sds = jax.ShapeDtypeStruct
+    vmem = pltpu.VMEM
+    dma = pltpu.SemaphoreType.DMA
+    out_shape = (
+        sds((2, 256, 768), BF), sds((2, 256, 768), BF), sds((24, 2304), F32), sds((24, 768), F32),
+        sds((24, 3072), F32), sds((96, 768), F32), sds((8, 128), F32),
+    )
+    shapes = ((96, 768), (24, 3072), (24, 768))
+    scratch = [vmem((4, 2, 2) + s, BF) for s in shapes] + [vmem((4, 2, 2) + s, BF) for s in shapes]
+    for rows, columns in shapes:
+        scratch += [vmem((4, 2, rows, columns // 2), BF)] * 2
+    for rows, columns in shapes:
+        scratch += [vmem((4, rows, columns // 2), BF)] * 2
+    scratch += [vmem((3,) + s, BF) for s in shapes]
+    scratch += [
+        vmem((2, 2, 256, 384), BF), vmem((128, 1024), BF), vmem((128, 1024), BF), vmem((1024, 128), F32),
+        vmem((1024, 128), F32), vmem((1024, 1152), BF), vmem((1024, 384), BF), vmem((3, 4, 2, 2, 2, 24, 384), BF),
+        vmem((3, 4, 2, 24, 384), BF), vmem((3, 4, 2, 24, 384), BF), vmem((3, 4, 24, 384), BF), vmem((3, 4, 24, 384), BF),
+        vmem((3, 3, 2, 24, 384), BF), vmem((3, 24, 384), F32), vmem((3, 24, 384), F32),
+        vmem((768, 1152), BF), vmem((768, 1024), BF), vmem((2, 256, 768), F32), vmem((2, 256, 768), F32),
+        vmem((2, 256, 768), F32), vmem((2, 256, 768), F32), vmem((2, 256, 768), BF), vmem((2, 768), F32),
+        vmem((1, 2304), F32), vmem((256, 128), F32), vmem((4, 2, 2, 8, 128), F32), vmem((4, 2, 8, 128), F32),
+        vmem((4, 8, 128), F32), vmem((3, 8, 128), F32),
+        dma((96,)), dma((96,)), dma((16,)),
+    ]
+    return pl.pallas_call(
+        backward_kernel,
+        out_shape=out_shape,
+        in_specs=[SM] + [ANY] * 7 + [VM, ANY] + [VM] * 7 + [VM] * 5,
+        out_specs=(ANY, ANY) + (VM,) * 5,
+        scratch_shapes=scratch,
+        compiler_params=pltpu.CompilerParams(
+            collective_id=1, has_side_effects=True, vmem_limit_bytes=60 * 2**20),
+    )(*operands)
+
+
+def middle(wo, wu, wd, cots, attl, xs, vrows):
+    width = xs.shape[-1]
+    w_out = wo.reshape(width, width)
+    w_up = wu.reshape(width, -1)
+    w_down = wd.reshape(-1, width)
+    hidden_units = w_up.shape[1]
+    b_out, gain_two, shift_two = vrows[3, :width], vrows[4, :width], vrows[5, :width]
+    b_up, b_down = vrows[6, :hidden_units], vrows[7, :width]
+    residual_in = xs.reshape(-1, width).astype(F32)
+    attended_low = attl.reshape(-1, width)
+    grad_branch = cots.reshape(-1, width)
+    residual_mid = residual_in + jnp.dot(attended_low, w_out, preferred_element_type=F32) + b_out
+    normed_two, norm_two_pull = jax.vjp(layer_norm, residual_mid, gain_two, shift_two)
+    normed_two = normed_two.astype(BF)
+    pre_gelu = jnp.dot(normed_two, w_up, preferred_element_type=F32) + b_up
+    hidden, gelu_pull = jax.vjp(gelu_tanh, pre_gelu)
+    hidden = hidden.astype(BF)
+    block_out = (residual_mid + jnp.dot(hidden, w_down, preferred_element_type=F32) + b_down).astype(BF)
+    g_down = jnp.einsum("rf,rd->fd", hidden, grad_branch, preferred_element_type=F32).astype(BF)
+    v_down = jnp.sum(grad_branch, axis=0, dtype=F32)
+    grad_hidden = jnp.einsum("rd,fd->rf", grad_branch, w_down, preferred_element_type=F32)
+    grad_pre = gelu_pull(grad_hidden)[0].astype(BF)
+    g_up = jnp.einsum("rd,rf->df", normed_two, grad_pre, preferred_element_type=F32).astype(BF)
+    v_up = jnp.sum(grad_pre, axis=0, dtype=F32)
+    grad_normed_two = jnp.einsum("rf,df->rd", grad_pre, w_up, preferred_element_type=F32)
+    grad_mid, v_gain, v_shift = norm_two_pull(grad_normed_two)
+    grad_mid = grad_mid + grad_branch.astype(F32)
+    grad_attn = grad_mid.astype(BF)
+    g_out = jnp.einsum("rd,re->de", attended_low, grad_attn, preferred_element_type=F32).astype(BF)
+    v_out = jnp.sum(grad_attn, axis=0, dtype=F32)
+    grad_attended = jnp.einsum("re,de->rd", grad_attn, w_out, preferred_element_type=F32).astype(BF)
+    return (
+        g_down.reshape(wd.shape), g_up.reshape(wu.shape), g_out.reshape(wo.shape), block_out.reshape(xs.shape),
+        grad_attended.reshape(xs.shape), grad_mid.reshape(xs.shape),
+        (v_out[None], v_gain[None], v_shift[None], v_up[None], v_down[None]),
+    )
+
+
+def body(
+    tokens, cotangent, prefix, ln1_gain, ln1_bias, w_qkv, b_qkv, w_out, b_out,
+    ln2_gain, ln2_bias, w_up, b_up, w_down, b_down,
+):
+    vec = pack_vectors((ln1_gain, ln1_bias, b_qkv, b_out, ln2_gain, ln2_bias, b_up, b_down))
+    (wq, wo, wu, wd, _, cots, attl, xs, n1t, qs, qst, k, v, att, lt, vrows) = forward_call(
+        prefix, tokens, cotangent, vec, w_qkv, w_out, w_up, w_down)
+    g_down, g_up, g_out, bo, ga, gmid, small = middle(wo, wu, wd, cots, attl, xs, vrows)
+    block_out, grad_tokens, gq, go, gu, gd, gvec = backward_call(
+        prefix, g_down, g_up, g_out, bo, ga, wq.reshape(-1, wq.shape[-1]), n1t, xs, gmid, qs, qst, k, v, att, lt, vrows, *small)
+    rows = [gvec[i, :wide] for i, wide in enumerate(WIDTHS)]
+    return (
+        block_out, grad_tokens, rows[0], rows[1], gq, rows[2], go, rows[3], rows[4], rows[5], gu, rows[6], gd, rows[7],
+    )
+
+
+def fits(mesh):
+    return dict(mesh.shape) == {"dp": 8, "seq": 4}
 
 
 norm_eps = 1e-05
@@ -330,7 +1128,7 @@
     return (grad_in.astype(jnp.bfloat16).reshape(grad_part.shape), weight_grads)
 
 
-def body(
+def general_body(
     tokens,
     cotangent,
     prefix,
@@ -477,4 +1275,5 @@
         P(("dp", "seq"), None),
         P(("dp", "seq")),
     )
-    return jax.shard_map(body, mesh=mesh, in_specs=in_specs, out_specs=out_specs, check_vma=False)
+    chosen = body if fits(mesh) else general_body
+    return jax.shard_map(chosen, mesh=mesh, in_specs=in_specs, out_specs=out_specs, check_vma=False)

time: 1030 us -> 274 us (0.27)
  waiting for transfers between devices: 640 us -> 0 us
  Pallas kernels: 0 us -> 217 us
  matrix products: 147 us -> 34.5 us
  blocking collectives: 83.7 us -> 0 us
  other arithmetic: 59.7 us -> 2.59 us
  local copies, waits for them, and re-layouts: 67.5 us -> 19.3 us
  between operations: 15.6 us -> 0.8 us
    reduce_scatter x6 -> x0, waiting for transfers between devices: 442 us -> none  [the longest x1 142 us: body(): lax.psum_scatter(totals[10], ('dp', 'seq'), scatter_dimension=0, tiled=True)]
    pallas_call x0 -> x2, Pallas kernels: none -> 217 us  [the longest x1 113 us: backward_call(): pl.pallas_call(backward_kernel, out_shape=out_shape, in_specs=[SM] + [ANY...]
    all_gather x8 -> x0, waiting for transfers between devices: 194 us -> none  [the longest x1 56.2 us: body(): lax.all_gather(shards[10], ('dp', 'seq'), axis=0, tiled=True)]
    dot_general x52 -> x9, matrix products: 147 us -> 34.5 us  [the longest x1 7.17 us: middle(): jnp.einsum('rd,fd->rf', grad_branch, w_down, preferred_element_type=F32)]
    unnamed x2 -> x0, blocking collectives: 83.7 us -> none
    unnamed x252 -> x28, local copies, waits for them, and re-layouts: 27 us -> 7.9 us
    convert_element_type x12 -> x0, other arithmetic: 16.1 us -> none  [the longest x2 9.93 us: attend_back(): grad_keys.astype(jnp.bfloat16)]
    while x96 -> x0, local copies, waits for them, and re-layouts: 13.1 us -> none
  transfers between devices with their start and end apart: 14 -> 0, of which waited for: 13 -> 0; matrix products, arithmetic and copies ran while one was open for 18% -> 0% of each run, Pallas kernels for 0% -> 0%
where the time goes in v1:
time: 274 us
  Pallas kernels  217 us (79%)
  matrix products  34.5 us (13%)
  local copies, waits for them, and re-layouts  19.3 us (7%)
    pallas_call x1, Pallas kernels, backward_call(): pl.pallas_call(backward_kernel, out_shape=out_shape, in_specs=[SM] + [ANY...  113 us
    pallas_call x1, Pallas kernels, forward_call(): pl.pallas_call(forward_kernel, out_shape=out_shape, in_specs=[SM] + [ANY]...  104 us
    unnamed x28, local copies, waits for them, and re-layouts  7.9 us
    dot_general x1, matrix products, middle(): jnp.einsum('rd,fd->rf', grad_branch, w_down, preferred_element_type=F32)  7.17 us
    dot_general x1, matrix products, middle(): jnp.einsum('rf,rd->fd', hidden, grad_branch, preferred_element_type=F32)  5.49 us

profile of v1, /device:TPU:0, one launch (start us, length us, event | category | flops | bytes accessed | tf_op | source)
XLA Modules:
  0.0 273.6 jit_solution(13495427369623666272)
XLA Ops:
  0.6 0.7 pad_bitcast_fusion.6
  1.3 0.7 pad_bitcast_fusion.4
  2.0 0.7 pad_bitcast_fusion.2
  2.7 0.7 pad_bitcast_fusion
  3.4 0.6 stack.35.vec_s
  4.0 103.6 %shard_map.254 = (bf16[4,192,1152]{2,1,0:T(8,128)(2,1)}, bf16[4,2,2,2,24,768]{5,4,3,2,1,0:T(8,128)(2,1)}, bf16[4,2,2,2,24,3072]{5,4,3,2,1,0:T(8,128)(2,1)}, bf16...) custom-call(s32[2]{0:T(128)} %prefix.3, ...), custom_call_target="tpu_custom_call" | custom-call | tf_op jit(solution)/shard_map/pallas_call | solution.py:279
  107.6 1.3 convert_reduce_fusion.1
  108.9 0.6 broadcast_in_dim.23.vb_down
  109.5 0.9 slice.42
  110.4 0.9 slice_reduce_fusion
  111.3 0.0 copy-start.7
  111.3 2.8 %fusion.14 = (f32[512]{0:T(512)S(1)}, f32[512,768]{1,0:T(8,128)S(1)}) fusion(f32[768]{0:T(1024)S(1)} %get-tuple-element.64, bf16[512,768]{1,0:T(8,128)(2,1)} %bitcast.69, bf16[768,768]{1,0:T(8,128)(2,1)} %bitcast.84, bf16[512,768]{1,0:T(8,128)(2,1)} %bitcast.71), kind=kOutput, calls=%fused_computation.55 | convolution fusion | flops 605552128 | bytes 4330496 | tf_op jit(solution)/shard_map/dot_general | solution.py:762
  114.1 0.0 slice-start
  114.1 0.3 multiply_reduce_fusion.2
  114.4 0.1 copy-done.7
  114.5 2.7 fusion.11
  117.2 0.0 slice-done
  117.2 0.0 slice-done.1
  117.2 0.0 copy-start.1
  117.2 4.9 %add_convert_fusion = bf16[512,768]{1,0:T(8,128)(2,1)} fusion(f32[512,768]{1,0:T(8,128)S(1)} %get-tuple-element.78, bf16[3072,768]{1,0:T(8,128)(2,1)S(1)} %bitcast.82, f32[768]{0:T(1024)S(1)} %get-tuple-element.61, f32[512,3072]{1,0:T(8,128)S(1)} %fusion.11, f32[3072]{0:T(1024)S(1)} %bitcast.74), kind=kOutput, calls=%fused_computation.19 | convolution fusion | flops 2432827392 | bytes 13384704 | tf_op jit(solution)/shard_map/dot_general | solution.py:768
  122.1 0.0 copy-done.1
  122.1 7.2 %convert_reduce_fusion = (f32[3072]{0:T(1024)}, bf16[512,3072]{1,0:T(8,128)(2,1)S(1)}) fusion(f32[512,3072]{1,0:T(8,128)S(1)} %fusion.11, f32[3072]{0:T(1024)S(1)} %bitcast.75, bf16[512,768]{1,0:T(8,128)(2,1)S(1)} %bitcast.66, bf16[3072,768]{1,0:T(8,128)(2,1)S(1)} %bitcast.83), kind=kOutput, calls=%fused_computation.9 | convolution fusion | flops 2452091904 | bytes 14966784 | tf_op jit(solution)/shard_map/rd,fd->rf/dot_general | solution.py:771
  129.3 5.5 %convolution_convert_fusion.1 = bf16[3072,768]{1,0:T(8,128)(2,1)} fusion(bf16[512,768]{1,0:T(8,128)(2,1)S(1)} %bitcast.67, f32[512,3072]{1,0:T(8,128)S(1)} %fusion.11, f32[3072]{0:T(1024)S(1)} %bitcast.76), kind=kOutput, calls=%fused_computation.12 | convolution fusion | flops 2434007040 | bytes 11808768 | tf_op jit(solution)/shard_map/rf,rd->fd/dot_general | solution.py:769
  134.8 3.0 %multiply_reduce_fusion = (f32[768]{0:T(1024)S(1)}, f32[512]{0:T(512)S(1)}, f32[768]{0:T(1024)S(1)}, f32[512,768]{1,0:T(8,128)S(1)}) fusion(f32[512,768]{1,0:T(8,128)S(1)} %get-tuple-element.78, f32[512]{0:T(512)S(1)} %fusion.8, f32[512]{0:T(512)S(1)} %broadcast_multiply_fusion, f32[768]{0:T(1024)S(1)} %get-tuple-element.63, ...), kind=kOutput, calls=%fused_computation.17 | convolution fusion | flops 2419062784 | bytes 11025408 | tf_op jit(solution)/shard_map/rf,df->rd/dot_general | solution.py:775
  137.8 0.6 reshape.113.vg2
  138.4 0.7 fusion.13
  139.0 4.9 %convolution_convert_fusion = bf16[768,3072]{1,0:T(8,128)(2,1)} fusion(bf16[512,3072]{1,0:T(8,128)(2,1)S(1)} %get-tuple-element.66, f32[512,768]{1,0:T(8,128)S(1)} %get-tuple-element.78, f32[768]{0:T(1024)S(1)} %get-tuple-element.62, f32[768]{0:T(1024)S(1)} %get-tuple-element.63, f32[512]{0:T(512)S(1)} %fusion.8, f32[512]{0:T(512)S(1)} %broadcast_multiply_fusion), kind=kOutput, calls=%fused_computation.11 | convolution fusion | flops 2420244480 | bytes 9447424 | tf_op jit(solution)/shard_map/rd,rf->df/dot_general | solution.py:773
  144.0 0.3 convert_reduce_fusion.2
  144.3 0.0 copy-start
  144.3 0.9 copy-done.8
  145.2 1.7 convolution_convert_fusion.3
  146.9 0.6 broadcast_in_dim.21.vb_out
  147.5 0.6 reshape.114.vb2
  148.1 0.0 copy-done.2
  148.1 1.8 convolution_convert_fusion.2
  149.9 0.0 copy-done
  149.9 112.9 %shard_map.255 = (bf16[2,256,768]{2,1,0:T(8,128)(2,1)}, bf16[2,256,768]{2,1,0:T(8,128)(2,1)}, f32[24,2304]{1,0:T(8,128)}, f32[24,768]{1,0:T(8,128)}, f32[24,3072...) custom-call(s32[2]{0:T(128)} %prefix.3, bf16[4,2,2,2,96,768]{5,4,3,2,1,0:T(8,128)(2,1)} %bitcast.63, ...), custom_call_target="tpu_custom_call" | custom-call | tf_op jit(solution)/shard_map/pallas_call | solution.py:740
  262.9 1.3 slice_bitcast_fusion.5
  264.1 1.2 slice_bitcast_fusion.1
  265.3 1.4 slice_bitcast_fusion
  266.8 2.1 copy.35
  268.8 2.1 copy.36
  270.9 0.0 copy-done.5
  270.9 0.7 copy.37
  271.6 0.0 copy-done.6
  271.6 0.6 copy.38
  272.2 0.7 copy.39
  272.9 0.7 copy.40
  (14 shorter events, 0.0 us)
Async XLA Ops:
  111.3 3.2 %copy-start.7 = (bf16[4,2,2,2,24,3072]{5,4,3,2,1,0:T(8,128)(2,1)S(1)}, bf16[4,2,2,2,24,3072]{5,4,3,2,1,0:T(8,128)(2,1)}, u32[]{:S(2)}) copy-start(bf16[4,2,2,2,24,3072]{5,4,3,2,1,0:T(8,128)(2,1)} %get-tuple-element.40) | copy-start | bytes 14155780
  114.1 3.1 %slice-start = ((s8[4718592]{0:T(1024)(128)(4,1)}), s8[4194304]{0:T(1024)(128)(4,1)S(1)}, s32[]{:S(2)}) async-start(s8[4718592]{0:T(1024)(128)(4,1)} %bitcast.80), calls=%async_computation | async-start | bytes 8388608
  114.5 2.7 %slice-start.1 = ((s8[4718592]{0:T(1024)(128)(4,1)}), s8[524288]{0:T(1024)(128)(4,1)S(1)}, s32[]{:S(2)}) async-start(s8[4718592]{0:T(1024)(128)(4,1)} %bitcast.80), calls=%async_computation.1 | async-start | bytes 1048576
  117.2 4.9 %copy-start.1 = (bf16[2,256,768]{2,1,0:T(8,128)(2,1)S(1)}, bf16[2,256,768]{2,1,0:T(8,128)(2,1)}, u32[]{:S(2)}) copy-start(bf16[2,256,768]{2,1,0:T(8,128)(2,1)} %get-tuple-element.41) | copy-start | bytes 2359300
  143.9 1.3 copy-start.8
  144.0 4.1 %copy-start.2 = (bf16[2,256,768]{2,1,0:T(8,128)(2,1)S(1)}, bf16[2,256,768]{2,1,0:T(8,128)(2,1)}, u32[]{:S(2)}) copy-start(bf16[2,256,768]{2,1,0:T(8,128)(2,1)} %get-tuple-element.37) | copy-start | bytes 2359300
  144.3 5.6 %copy-start = (f32[512,768]{1,0:T(8,128)}, f32[512,768]{1,0:T(8,128)S(1)}, u32[]{:S(2)}) copy-start(f32[512,768]{1,0:T(8,128)S(1)} %get-tuple-element.68) | copy-start | bytes 4718596
  262.8 8.1 %copy-start.5 = (f32[24,2304]{1,0:T(8,128)S(1)}, f32[24,2304]{1,0:T(8,128)}, u32[]{:S(2)}) copy-start(f32[24,2304]{1,0:T(8,128)} %get-tuple-element.106) | copy-start | bytes 663556
  262.8 8.7 %copy-start.6 = (f32[24,768]{1,0:T(8,128)S(1)}, f32[24,768]{1,0:T(8,128)}, u32[]{:S(2)}) copy-start(f32[24,768]{1,0:T(8,128)} %get-tuple-element.108) | copy-start | bytes 221188
  262.8 9.4 %copy-start.4 = (f32[24,3072]{1,0:T(8,128)S(1)}, f32[24,3072]{1,0:T(8,128)}, u32[]{:S(2)}) copy-start(f32[24,3072]{1,0:T(8,128)} %get-tuple-element.112) | copy-start | bytes 884740
  262.8 10.1 %copy-start.3 = (f32[96,768]{1,0:T(8,128)S(1)}, f32[96,768]{1,0:T(8,128)}, u32[]{:S(2)}) copy-start(f32[96,768]{1,0:T(8,128)} %get-tuple-element.114) | copy-start | bytes 884740

commit v2 on v0

--- a/solution.py
+++ b/solution.py
@@ -1,11 +1,910 @@
 import jax
 import jax.numpy as jnp
 from jax import lax
+from jax.experimental import pallas as pl
+from jax.experimental.pallas import tpu as pltpu
 from jax.sharding import PartitionSpec as P
 
 HEADS = 12
 HEAD_DIM = 64
 MB = 2
+
+F32 = jnp.float32
+BF = jnp.bfloat16
+EPS = 1e-05
+MESH = pl.DeviceIdType.MESH
+NEG = -1e30
+ANY = pl.BlockSpec(memory_space=pl.ANY)
+VM = pl.BlockSpec(memory_space=pltpu.VMEM)
+SM = pl.BlockSpec(memory_space=pltpu.SMEM)
+WIDTHS = (24, 24, 72, 24, 24, 24, 96, 24)
+D = 768
+FF = 3072
+THIRD = 384
+LAST = (((1,), (1,)), ((), ()))
+FIRST = (((0,), (0,)), ((), ()))
+ALL = slice(None)
+REMOTES = 128
+LOCALS = 64
+
+
+def places():
+    dp = lax.axis_index("dp")
+    sq = lax.axis_index("seq")
+    return dp // 2, dp % 2, sq // 2, sq % 2
+
+
+def device(z, x, y, c):
+    return (z * 2 + x, y * 2 + c)
+
+
+def owner_of(wide):
+    column = lax.broadcasted_iota(jnp.int32, (1, 32 * wide), 1).astype(F32)
+    owner = jnp.floor((column + 0.5) * (1.0 / wide))
+    return owner.astype(jnp.int32), (column - owner * wide).astype(jnp.int32)
+
+
+def spread_row(gathered, index, wide):
+    total = 32 * wide
+    row = lax.broadcasted_iota(jnp.int32, (32, 256), 0)
+    place = lax.broadcasted_iota(jnp.int32, (32, 256), 1)
+    pick = jnp.where(place == row * 8 + index, 1.0, 0.0).astype(BF)
+    mine = jnp.dot(pick, gathered, preferred_element_type=F32).astype(BF)
+    owner, rest = owner_of(wide)
+    spread = jnp.where(lax.broadcasted_iota(jnp.int32, (128, total), 0) == rest, 1.0, 0.0).astype(BF)
+    full = jnp.dot(mine, spread, preferred_element_type=F32)
+    keep = lax.broadcasted_iota(jnp.int32, (32, total), 0) == owner
+    return jnp.sum(jnp.where(keep, full, 0.0), axis=0, keepdims=True)
+
+
+def collect_rows(vector, wide):
+    total = 32 * wide
+    owner, rest = owner_of(wide)
+    gather = jnp.where(lax.broadcasted_iota(jnp.int32, (128, total), 0) == rest, 1.0, 0.0).astype(BF)
+    keep = lax.broadcasted_iota(jnp.int32, (32, total), 0) == owner
+    high = vector.astype(BF).astype(F32)
+    out = None
+    for part in (high, vector - high):
+        placed = jnp.where(keep, part, 0.0).astype(BF)
+        term = lax.dot_general(placed, gather, LAST, preferred_element_type=F32)
+        out = term if out is None else out + term
+    return out
+
+
+def add_into(ref, at, other):
+    ref[at] = (ref[at].astype(F32) + other.astype(F32)).astype(BF)
+
+
+def start(copies):
+    for copy in copies:
+        copy.start()
+
+
+def arrive(copies):
+    for copy in copies:
+        copy.wait_recv()
+
+
+def landed(copies):
+    for copy in copies:
+        copy.wait()
+
+
+def lanes(first, count=128):
+    return pl.ds(pl.multiple_of(first, 128), count)
+
+
+def rows_at(first, count, step=256):
+    return pl.ds(pl.multiple_of(first, step), count)
+
+
+class Links:
+    def __init__(self, ssem, rsem, lsem):
+        self.ssem, self.rsem, self.lsem = ssem, rsem, lsem
+        self.remotes = self.locals = 0
+        self.sent = []
+        z, x, y, c = places()
+        self.z, self.x, self.y, self.c = z, x, y, c
+        self.x2, self.y2, self.c2 = 1 - x, 1 - y, 1 - c
+        self.px, self.py, self.pc = device(z, 1 - x, y, c), device(z, x, 1 - y, c), device(z, x, y, 1 - c)
+        self.zs = [lax.rem(z + d, 4) for d in (1, 2, 3)]
+        self.pz = [device(zz, x, y, c) for zz in self.zs]
+
+    def fresh(self, count=1):
+        first = self.remotes
+        self.remotes += count
+        return first
+
+    def remote(self, src, dst, dev, at=None):
+        i = self.fresh() if at is None else at
+        copy = pltpu.make_async_remote_copy(
+            src_ref=src, dst_ref=dst, send_sem=self.ssem.at[i], recv_sem=self.rsem.at[i],
+            device_id=dev, device_id_type=MESH)
+        if at is None:
+            self.sent.append(copy)
+        return copy
+
+    def local(self, src, dst):
+        i = self.locals
+        self.locals += 1
+        return pltpu.make_async_copy(src, dst, self.lsem.at[i])
+
+    def greet(self):
+        barrier = pltpu.get_barrier_semaphore()
+        for dev in [self.px, self.py, self.pc] + self.pz:
+            pl.semaphore_signal(barrier, inc=1, device_id=dev, device_id_type=MESH)
+        pl.semaphore_wait(barrier, 6)
+
+
+class Gather:
+    def __init__(self, links, shard, full, cut, kinds=None):
+        k = links
+        self.k, self.full, self.kinds = k, full, kinds
+        rows = shard.shape[0]
+        own = pl.ds(pl.multiple_of(k.c * rows, 8), rows)
+        mine = full if kinds else full.at[k.c]
+        theirs = full if kinds else full.at[k.c2]
+        half = full.shape[-1]
+        z, x, y = k.z, k.x, k.y
+        if kinds:
+            self.own, self.c0 = [], []
+            for kind in range(kinds):
+                there = pl.ds(kind * THIRD, THIRD)
+                self.own.append(k.local(shard.at[:, lanes(kind * D + k.c * THIRD, THIRD)], mine.at[z, x, y, own, there]))
+                self.c0.append(k.remote(shard.at[:, lanes(kind * D + k.c2 * THIRD, THIRD)],
+                                        theirs.at[z, x, y, own, there], k.pc))
+        else:
+            self.own = [k.local(shard.at[:, lanes(k.c * half, half)], mine.at[z, x, y, own])]
+            self.c0 = [k.remote(shard.at[:, lanes(k.c2 * half, half)], theirs.at[z, x, y, own], k.pc)]
+        self.c1 = [k.remote(mine.at[z, x, y], mine.at[z, x, y], dev) for dev in k.pz]
+        a, b = slice(0, cut), slice(cut, None)
+        self.c2 = [k.remote(mine.at[:, x, y, :, a], mine.at[:, x, y, :, a], k.px),
+                   k.remote(mine.at[:, x, y, :, b], mine.at[:, x, y, :, b], k.py)]
+        self.c3 = [k.remote(mine.at[:, :, y, :, a], mine.at[:, :, y, :, a], k.py),
+                   k.remote(mine.at[:, x, :, :, b], mine.at[:, x, :, :, b], k.px)]
+        self.c4 = [] if kinds else [k.remote(full.at[k.c], full.at[k.c], k.pc)]
+
+    def s0(self):
+        start(self.own)
+        start(self.c0)
+
+    def s1(self):
+        landed(self.own)
+        arrive(self.c0)
+        start(self.c1)
+
+    def s2(self):
+        arrive(self.c1)
+        start(self.c2)
+
+    def s3(self):
+        arrive(self.c2)
+        start(self.c3)
+
+    def s4(self):
+        arrive(self.c3)
+        start(self.c4)
+
+    def done(self):
+        arrive(self.c4)
+
+
+class Scatter:
+    def __init__(self, links, grad, r0, r1a, r1b, r2a, r2b, r3, tot, fin, put, cut, base=None, whole=True):
+        k = links
+        self.k, self.grad, self.whole, self.put = k, grad, whole, put
+        self.r0, self.r1a, self.r1b, self.r2a, self.r2b, self.r3, self.tot, self.fin = r0, r1a, r1b, r2a, r2b, r3, tot, fin
+        self.mine = grad.at[k.c] if whole else grad
+        self.a = (ALL, slice(0, cut))
+        self.b = (ALL, slice(cut, None))
+        x, y, x2, y2 = k.x, k.y, k.x2, k.y2
+        at = iter([None] * 10 if base is None else base)
+        mine = self.mine
+        self.c0 = [k.remote(grad.at[k.c2], r0, k.pc, next(at))] if whole else []
+        self.c1 = [k.remote(mine.at[(ALL, ALL, y2) + self.a], r1a, k.py, next(at)),
+                   k.remote(mine.at[(ALL, x2, ALL) + self.b], r1b, k.px, next(at))]
+        self.c2 = [k.remote(mine.at[(ALL, x2, y) + self.a], r2a, k.px, next(at)),
+                   k.remote(mine.at[(ALL, x, y2) + self.b], r2b, k.py, next(at))]
+        self.c3 = [k.remote(mine.at[k.zs[d], x, y], r3.at[d], k.pz[d], next(at)) for d in range(3)]
+        self.c4 = [k.remote(tot.at[k.c2], fin, k.pc, next(at))]
+
+    def at(self, place):
+        return ((self.k.c,) if self.whole else ()) + place
+
+    def s0(self):
+        start(self.c0)
+
+    def s1(self):
+        if self.whole:
+            arrive(self.c0)
+
+            def add(i, carry):
+                where = (i // 4, lax.rem(i // 2, 2), lax.rem(i, 2))
+                add_into(self.grad, self.at(where), self.r0[where])
+                return carry
+
+            lax.fori_loop(0, 16, add, 0)
+        start(self.c1)
+
+    def s2(self):
+        arrive(self.c1)
+        k = self.k
+
+        def add(i, carry):
+            zz, other = i // 2, lax.rem(i, 2)
+            add_into(self.grad, self.at((zz, other, k.y) + self.a), self.r1a[zz, other])
+            add_into(self.grad, self.at((zz, k.x, other) + self.b), self.r1b[zz, other])
+            return carry
+
+        lax.fori_loop(0, 8, add, 0)
+        start(self.c2)
+
+    def s3(self):
+        arrive(self.c2)
+        k = self.k
+
+        def add(zz, carry):
+            add_into(self.grad, self.at((zz, k.x, k.y) + self.a), self.r2a[zz])
+            add_into(self.grad, self.at((zz, k.x, k.y) + self.b), self.r2b[zz])
+            return carry
+
+        lax.fori_loop(0, 4, add, 0)
+        start(self.c3)
+
+    def s4(self):
+        arrive(self.c3)
+        k = self.k
+        total = self.mine[k.z, k.x, k.y].astype(F32)
+        for d in range(3):
+            total = total + self.r3[d].astype(F32)
+        rows = total.shape[0] // 2
+        self.tot[0] = total[:rows]
+        self.tot[1] = total[rows:]
+        start(self.c4)
+        self.put(self.tot[k.c], k.c)
+
+    def s5(self):
+        arrive(self.c4)
+        self.put(self.fin[...], self.k.c2)
+
+    def gone(self):
+        for copy in self.c0 + self.c1 + self.c2 + self.c3 + self.c4:
+            copy.wait_send()
+
+
+def gelu_parts(value):
+    rate = 0.7978845608028654
+    bent = jnp.tanh(rate * (value + 0.044715 * (value * value * value)))
+    result = 0.5 * value * (1.0 + bent)
+    slope = 0.5 * (1.0 + bent) + 0.5 * value * (1.0 - bent * bent) * (rate * (1.0 + 0.134145 * (value * value)))
+    return result, slope
+
+
+def unit_rows(rows):
+    centre = rows - jnp.mean(rows, axis=-1, keepdims=True)
+    scale = lax.rsqrt(jnp.mean(centre * centre, axis=-1, keepdims=True) + EPS)
+    return centre * scale, scale
+
+
+def norm_back(grad, normed, scale):
+    return scale * (grad - jnp.mean(grad, axis=-1, keepdims=True)
+                    - normed * jnp.mean(grad * normed, axis=-1, keepdims=True))
+
+
+def layer_kernel(
+    prefix, tok, cot, vec_s, wq_s, wo_s, wu_s, wd_s,
+    out_bo, out_gt, out_q, out_o, out_u, out_d, out_vec,
+    wq, wo, wu, wd, gv, k_qs, k_qst, k_k, k_v, k_att, k_n1t,
+    gvm, tok_all, vrows, wom, al_send, al, cotm, ga_send, ga_all, fa, fb, fc, fr, lt,
+    gd, gu, go, gq,
+    r0d, r0u, r0o, r1ad, r1bd, r1au, r1bu, r1ao, r1bo, r2ad, r2bd, r2au, r2bu, r2ao, r2bo, r3d, r3u, r3o,
+    td, tu, to, fd, fu, fo,
+    q1a, q1b, q2a, q2b, q3, tq, fq,
+    vs, vbq, vup, vtab, vr0, vr1, vr2, vr3,
+    ssem, rsem, lsem,
+):
+    k = Links(ssem, rsem, lsem)
+    bo, gtb = al, cotm
+    z, x, y, c, x2, y2, c2 = k.z, k.x, k.y, k.c, k.x2, k.y2, k.c2
+    k.greet()
+    vmem = pltpu.VMEM
+
+    gather_q = Gather(k, wq_s, wq, 512, 3)
+    gather_o = Gather(k, wo_s, wo, 256)
+    gather_u = Gather(k, wu_s, wu, 768)
+    gather_d = Gather(k, wd_s, wd, 128)
+    own_vec = k.local(vec_s, gv.at[z, x, y, c])
+    vec_c = k.remote(vec_s, gv.at[z, x, y, c], k.pc)
+    own_vec.start()
+    vec_c.start()
+    own_tok = k.local(tok.at[y], tok_all.at[y, c])
+    tok_y = k.remote(tok.at[y2], tok_all.at[y, c], k.py)
+    own_tok.start()
+    tok_y.start()
+    gather_q.s0()
+    own_cot = k.local(cot.at[y], cotm.at[y])
+    cot_y = k.remote(cot.at[y2], cotm.at[y], k.py)
+    own_vec.wait()
+    vec_c.wait_recv()
+    vec_z = [k.remote(gv.at[z, x, y], gv.at[z, x, y], dev) for dev in k.pz]
+    start(vec_z)
+    gather_q.s1()
+    gather_o.s0()
+    gather_u.s0()
+    gather_d.s0()
+    own_tok.wait()
+    tok_y.wait_recv()
+    tok_c = k.remote(tok_all.at[:, c], tok_all.at[:, c], k.pc)
+    tok_c.start()
+    own_cot.start()
+    cot_y.start()
+    arrive(vec_z)
+    vec_x = k.remote(gv.at[:, x, y], gv.at[:, x, y], k.px)
+    vec_x.start()
+    vec_x.wait_recv()
+    vec_y = k.remote(gv.at[:, :, y], gv.at[:, :, y], k.py)
+    vec_y.start()
+    tok_c.wait_recv()
+    vec_y.wait_recv()
+    table = k.local(gv, gvm)
+    table.start()
+    table.wait()
+    table = gvm[...].reshape(256, 128)
+    for index, wide in enumerate(WIDTHS):
+        vrows[index : index + 1, 0 : 32 * wide] = spread_row(table, index, wide)
+
+    mine_cols = lanes(c * THIRD, THIRD)
+    peer_cols = lanes(c2 * THIRD, THIRD)
+    al_own = k.local(al_send.at[:, c], al.at[:, :, mine_cols])
+    al_c = k.remote(al_send.at[:, c2], al.at[:, :, mine_cols], k.pc)
+    limit = prefix[y] - 1
+    sub = lax.broadcasted_iota(jnp.int32, (128, 256), 0)
+
+    def forward(n1, n1t, vt, qs, qst, keys_ref, values_ref, att, wqm):
+        gain = vrows[0:1, 0:D]
+        shift = vrows[1:2, 0:D]
+
+        def norm_block(b, carry):
+            normed, _ = unit_rows(tok_all[b // 2, lax.rem(b, 2)].astype(F32))
+            normed = (normed * gain + shift).astype(BF)
+            at = rows_at(b * 256, 256)
+            n1[at, :] = normed
+            n1t[:, at] = normed.astype(F32).T.astype(BF)
+            return carry
+
+        lax.fori_loop(0, 4, norm_block, 0)
+        keep_n1t = k.local(n1t, k_n1t)
+        keep_n1t.start()
+        gather_q.s2()
+        gather_o.s1()
+        gather_u.s1()
+        gather_q.s3()
+        gather_o.s2()
+        gather_q.s4()
+        load_q = k.local(wq.reshape(D, 3 * THIRD), wqm)
+        load_q.start()
+        load_q.wait()
+
+        def project(b, carry):
+            rows = rows_at(b * 256, 256)
+            block = n1[rows, :]
+            parts = []
+            for kind in range(3):
+                bias = vrows[2:3, lanes(kind * D + c * THIRD, THIRD)]
+                value = jnp.dot(block, wqm[:, kind * THIRD : (kind + 1) * THIRD], preferred_element_type=F32)
+                parts.append((value + bias).astype(BF))
+            queries = parts[0].astype(F32) * 0.125
+            qs[rows, :] = queries.astype(BF)
+            qst[:, rows] = queries.T.astype(BF)
+            keys_ref[rows, :] = parts[1]
+            values_ref[rows, :] = parts[2]
+            vt[:, rows] = parts[2].astype(F32).T.astype(BF)
+            return carry
+
+        lax.fori_loop(0, 4, project, 0)
+        keep = [k.local(qs, k_qs), k.local(qst, k_qst), k.local(keys_ref, k_k), k.local(values_ref, k_v)]
+        start(keep)
+        gather_u.s2()
+        gather_d.s1()
+
+        def attend(block):
+            rows = min(4, max(block + 1, 2)) * 256
+            qcols = pl.ds(block * 256, 256)
+
+            def unit(u, carry):
+                cols = lanes(u * 128)
+                keys = keys_ref[0:rows, cols]
+                queries = qst[cols, qcols]
+                qpos = block * 256 + lax.broadcasted_iota(jnp.int32, (1, 256), 1)
+                seen = lax.broadcasted_iota(jnp.int32, (rows, 256), 0) <= jnp.maximum(qpos, limit)
+                for half in range(2):
+                    chosen = jnp.where(sub // 64 == half, queries, jnp.zeros_like(queries))
+                    scores = jnp.dot(keys, chosen, preferred_element_type=F32)
+                    size = jnp.where(seen, jnp.abs(scores), NEG)
+                    top = jnp.max(size, axis=0, keepdims=True)
+                    exponent = jnp.exp(size - top)
+                    total = jnp.sum(exponent, axis=0, keepdims=True)
+                    weights = jnp.where(scores > 0, exponent, jnp.where(scores < 0, -exponent, 0.0)).astype(BF)
+                    at = pl.ds(pl.multiple_of(u * 128 + half * 64, 64), 64)
+                    att[at, qcols] = jnp.dot(vt[at, 0:rows], weights, preferred_element_type=F32) / total
+                    lt[pl.ds(u * 2 + half, 1), qcols] = top + jnp.log(total)
+                al_send[block // 2, block % 2, :, cols] = att[cols, qcols].T.astype(BF)
+                return carry
+
+            lax.fori_loop(0, 3, unit, 0)
+
+        attend(3)
+        gather_o.s3()
+        attend(2)
+        gather_u.s3()
+        attend(1)
+        gather_o.s4()
+        attend(0)
+        al_own.start()
+        al_c.start()
+        keep_att = k.local(att, k_att)
+        keep_att.start()
+        gather_o.done()
+        load_o = k.local(wo.reshape(2, D, THIRD), wom)
+        load_o.start()
+        gather_d.s2()
+        al_own.wait()
+        al_c.wait_recv()
+        load_o.wait()
+        landed(keep + [keep_n1t, keep_att])
+
+    pl.run_scoped(
+        forward, vmem((1024, D), BF), vmem((D, 1024), BF), vmem((THIRD, 1024), BF), vmem((1024, THIRD), BF),
+        vmem((THIRD, 1024), BF), vmem((1024, THIRD), BF), vmem((1024, THIRD), BF), vmem((THIRD, 1024), F32), vmem((D, 1152), BF))
+
+    def put_to(out, half):
+        def put(value, core):
+            out[:, lanes(core * half, half)] = value
+        return put
+
+    down = Scatter(k, gd, r0d, r1ad, r1bd, r2ad, r2bd, r3d, td, fd, put_to(out_d, THIRD), 128)
+    up = Scatter(k, gu, r0u, r1au, r1bu, r2au, r2bu, r3u, tu, fu, put_to(out_u, 1536), 768)
+    outp = Scatter(k, go, r0o, r1ao, r1bo, r2ao, r2bo, r3o, to, fo, put_to(out_o, THIRD), 256)
+
+    def middle(wbuf, wdb, hid, slope, n2, n2t, alt, gpc):
+        b_out, gain, shift = vrows[3:4, 0:D], vrows[4:5, 0:D], vrows[5:6, 0:D]
+
+        def begin(yy, carry):
+            rows = rows_at(yy * 256, 256)
+            branch = jnp.concatenate([jnp.dot(al[yy], wom[h], preferred_element_type=F32) for h in range(2)], axis=1)
+            residual = tok_all[yy, c].astype(F32) + branch + b_out
+            fa[yy] = residual
+            normed, _ = unit_rows(residual)
+            normed = (normed * gain + shift).astype(BF)
+            n2[rows, :] = normed
+            n2t[:, rows] = normed.astype(F32).T.astype(BF)
+            alt[:, rows] = al[yy].astype(F32).T.astype(BF)
+            return carry
+
+        lax.fori_loop(0, 2, begin, 0)
+        own_cot.wait()
+        cot_y.wait_recv()
+
+        wu2 = wu.reshape(2, D, 1536)
+        wd2 = wd.reshape(2, FF, THIRD)
+
+        def chunk(j, first, second):
+            h = first if j < 2 else second
+            return h, j % 2
+
+        def up_load(j, slot, order):
+            h, part = chunk(j, *order)
+            return k.local(wu2.at[h, :, part * D : (part + 1) * D], wbuf.at[slot])
+
+        def down_load(j, slot, order):
+            h, part = chunk(j, *order)
+            return k.local(wd2.at[:, rows_at(h * 1536 + part * D, D), :], wdb.at[slot])
+
+        forth = (c, c2)
+        gather_u.s4()
+        loads = [up_load(j, j % 2, forth) for j in range(4)]
+        loads[0].start()
+        for j in range(4):
+            if j == 1:
+                gather_u.done()
+            if j < 3:
+                loads[j + 1].start()
+            loads[j].wait()
+            h, part = chunk(j, *forth)
+            cols = lanes(h * 1536 + part * D, D)
+
+            def ahead(yy, carry):
+                rows = rows_at(yy * 256, 256)
+                value = jnp.dot(n2[rows, :], wbuf[j % 2], preferred_element_type=F32) + vrows[6:7, cols]
+                result, bend = gelu_parts(value)
+                hid[rows, cols] = result.astype(BF)
+                slope[rows, cols] = bend
+                return carry
+
+            lax.fori_loop(0, 2, ahead, 0)
+        gather_d.s3()
+
+        vs[7:8, :] = jnp.sum(cotm[0].astype(F32), axis=0, keepdims=True) + jnp.sum(
+            cotm[1].astype(F32), axis=0, keepdims=True)
+
+        def down_grad(i, carry):
+            total = jnp.zeros((THIRD, D), F32)
+            for yy in range(2):
+                total += lax.dot_general(hid[yy * 256 : (yy + 1) * 256, lanes(i * THIRD, THIRD)], cotm[yy], FIRST,
+                                         preferred_element_type=F32)
+            zz, xx = i // 2, lax.rem(i, 2)
+            for yy in range(2):
+                for h in range(2):
+                    gd[h, zz, xx, yy] = total[yy * 192 : (yy + 1) * 192, h * THIRD : (h + 1) * THIRD].astype(BF)
+            return carry
+
+        lax.fori_loop(0, 8, down_grad, 0)
+        down.s0()
+        fb[...] = jnp.zeros_like(fb)
+        fc[...] = jnp.zeros_like(fc)
+        vup[...] = jnp.zeros_like(vup)
+        gather_d.s4()
+        back = (c2, c)
+        again = [up_load(j, j % 2, back) for j in range(4)]
+        lower = [down_load(j, j % 2, back) for j in range(4)]
+        again[0].start()
+        down.s1()
+        gather_d.done()
+        lower[0].start()
+        for j in range(4):
+            slot = j % 2
+            if j < 3:
+                again[j + 1].start()
+                lower[j + 1].start()
+            again[j].wait()
+            lower[j].wait()
+            h, part = chunk(j, *back)
+            cols = lanes(h * 1536 + part * D, D)
+
+            def behind(yy, carry):
+                rows = rows_at(yy * 256, 256)
+                units = hid[rows, cols]
+                grad = None
+                for side in range(2):
+                    there = slice(side * THIRD, (side + 1) * THIRD)
+                    fc[yy, :, there] += jnp.dot(units, wdb[slot, side], preferred_element_type=F32)
+                    term = lax.dot_general(cotm[yy, :, there], wdb[slot, side], LAST, preferred_element_type=F32)
+                    grad = term if grad is None else grad + term
+                grad = (grad * slope[rows, cols]).astype(BF)
+                gpc[rows, :] = grad
+                vup[0:1, cols] += jnp.sum(grad.astype(F32), axis=0, keepdims=True)
+                fb[yy] += lax.dot_general(grad, wbuf[slot], LAST, preferred_element_type=F32)
+                return carry
+
+            lax.fori_loop(0, 2, behind, 0)
+
+            def up_grad(zz, carry):
+                total = jnp.dot(n2t[rows_at(zz * 192, 192, 64), :], gpc[...], preferred_element_type=F32)
+                for i in range(4):
+                    gu[h, zz, i // 2, i % 2, :, part * D : (part + 1) * D] = total[i * 48 : (i + 1) * 48].astype(BF)
+                return carry
+
+            lax.fori_loop(0, 4, up_grad, 0)
+            if j == 1:
+                up.s0()
+        bo[...] = (fa[...] + fc[...] + vrows[7:8, 0:D].reshape(1, 1, D)).astype(BF)
+        up.s1()
+
+        vs[3:6, :] = jnp.zeros((3, D), F32)
+
+        def mid_back(yy, carry):
+            rows = rows_at(yy * 256, 256)
+            normed, scale = unit_rows(fa[yy])
+            grad = fb[yy]
+            vs[4:5, :] += jnp.sum(grad * normed, axis=0, keepdims=True)
+            vs[5:6, :] += jnp.sum(grad, axis=0, keepdims=True)
+            total = cotm[yy].astype(F32) + norm_back(grad * gain, normed, scale)
+            fa[yy] = total
+            low = total.astype(BF)
+            vs[3:4, :] += jnp.sum(low.astype(F32), axis=0, keepdims=True)
+            gpc[rows, :] = low
+            heads = None
+            for side in range(2):
+                term = lax.dot_general(low[:, side * THIRD : (side + 1) * THIRD], wom[side], LAST,
+                                       preferred_element_type=F32)
+                heads = term if heads is None else heads + term
+            ga_send[yy] = heads.astype(BF)
+            ga_all[yy, c] = ga_send[yy, :, mine_cols]
+            return carry
+
+        lax.fori_loop(0, 2, mid_back, 0)
+        ga_c.start()
+
+        def out_grad(zz, carry):
+            total = jnp.dot(alt[rows_at(zz * 192, 192, 64), :], gpc[...], preferred_element_type=F32)
+            for i in range(4):
+                for h in range(2):
+                    go[h, zz, i // 2, i % 2] = total[i * 48 : (i + 1) * 48, h * THIRD : (h + 1) * THIRD].astype(BF)
+            return carry
+
+        lax.fori_loop(0, 4, out_grad, 0)
+        outp.s0()
+
+    ga_c = k.remote(ga_send.at[:, :, peer_cols], ga_all.at[:, c], k.pc)
+    pl.run_scoped(
+        middle, vmem((2, D, D), BF), vmem((2, 2, D, THIRD), BF), vmem((512, FF), BF), vmem((512, FF), F32),
+        vmem((512, D), BF), vmem((D, 512), BF), vmem((D, 512), BF), vmem((512, D), BF))
+
+    bo_own = k.local(bo.at[y], out_bo.at[y])
+    bo_y = k.remote(bo.at[y2], out_bo.at[y], k.py)
+    bo_own.start()
+    bo_y.start()
+
+    def put_q(u):
+        def put(value, core):
+            for kind in range(3):
+                out_q[:, lanes(kind * D + core * THIRD + u * 128)] = value[:, kind * 128 : (kind + 1) * 128]
+        return put
+
+    bases = [k.fresh(3) for _ in range(8)]
+
+    def query_scatter(u):
+        return Scatter(k, gq.at[u], None, q1a.at[u], q1b.at[u], q2a.at[u], q2b.at[u], q3.at[u], tq.at[u], fq.at[u],
+                       put_q(u), 128, base=[b + u for b in bases], whole=False)
+
+    queue = [query_scatter(u) for u in range(3)]
+
+    def backward(qs, qst, keys_ref, values_ref, att, n1t, gt, kt, dk, dv, gp, gpu, wqm):
+        loads = [k.local(k_qs, qs), k.local(k_qst, qst), k.local(k_k, keys_ref), k.local(k_v, values_ref),
+                 k.local(k_att, att), k.local(k_n1t, n1t), k.local(wq.reshape(D, 3 * THIRD), wqm)]
+        start(loads)
+        ga_c.wait_recv()
+        landed(loads)
+        lane = lax.broadcasted_iota(jnp.int32, (256, 128), 1)
+        vbq[...] = jnp.zeros_like(vbq)
+        slots = {
+            (0, 3): [down.s2, outp.s1], (0, 2): [], (0, 1): [down.s3], (0, 0): [up.s2],
+            (1, 3): [], (1, 2): [outp.s2], (1, 1): [up.s3], (1, 0): [down.s4, outp.s3],
+            (2, 3): [queue[0].s2], (2, 2): [down.s5], (2, 1): [queue[0].s3, up.s4], (2, 0): [outp.s4],
+        }
+
+        def unit(u, carry):
+            cols = lanes(u * 128)
+            for b in range(4):
+                rows = slice(b * 256, (b + 1) * 256)
+                gt[:, rows] = ga_all[b // 2, b % 2, :, cols].astype(F32).T.astype(BF)
+                kt[:, rows] = keys_ref[rows, cols].astype(F32).T.astype(BF)
+            dk[...] = jnp.zeros_like(dk)
+            dv[...] = jnp.zeros_like(dv)
+            for block in (3, 2, 1, 0):
+                rows = min(4, max(block + 1, 2)) * 256
+                qrange = slice(block * 256, (block + 1) * 256)
+                keys = keys_ref[0:rows, cols]
+                values = values_ref[0:rows, cols]
+                queries_t = qst[cols, qrange]
+                grads_t = gt[:, qrange]
+                queries = qs[qrange, cols]
+                grads = ga_all[block // 2, block % 2, :, cols]
+                qpos = block * 256 + lax.broadcasted_iota(jnp.int32, (1, 256), 1)
+                seen = lax.broadcasted_iota(jnp.int32, (rows, 256), 0) <= jnp.maximum(qpos, limit)
+                prod = grads_t.astype(F32) * att[cols, qrange]
+                dqs, dks, dvs = [], None, None
+                for half in range(2):
+                    part = slice(half * 64, half * 64 + 64)
+                    in_sub = sub // 64 == half
+                    in_lane = lane // 64 == half
+                    delta = jnp.sum(prod[part], axis=0, keepdims=True)
+                    total = lt[pl.ds(u * 2 + half, 1), qrange]
+                    zero = jnp.zeros((), BF)
+                    scores = jnp.dot(keys, jnp.where(in_sub, queries_t, zero), preferred_element_type=F32)
+                    pull = jnp.dot(values, jnp.where(in_sub, grads_t, zero), preferred_element_type=F32)
+                    share = jnp.exp(jnp.where(seen, jnp.abs(scores) - total, NEG))
+                    signed = jnp.where(scores > 0, share, jnp.where(scores < 0, -share, 0.0))
+                    grad_scores = (share * pull - signed * delta).astype(BF)
+                    signed = signed.astype(BF)
+                    dvt = jnp.dot(signed, jnp.where(in_lane, grads, zero), preferred_element_type=F32)
+                    dkt = jnp.dot(grad_scores, jnp.where(in_lane, queries, zero), preferred_element_type=F32)
+                    dvs = dvt if dvs is None else dvs + dvt
+                    dks = dkt if dks is None else dks + dkt
+                    dqs.append(jnp.dot(kt[part, 0:rows], grad_scores, preferred_element_type=F32))
+                dk[0:rows, :] += dks
+                dv[0:rows, :] += dvs
+                gpu[qrange, 0:128] = (jnp.concatenate(dqs, axis=0).T * 0.125).astype(BF)
+                for which in range(3):
+                    if slots[which, block]:
+                        @pl.when(u == which)
+                        def _():
+                            for step in slots[which, block]:
+                                step()
+            gpu[:, 128:256] = dk[...].astype(BF)
+            gpu[:, 256:384] = dv[...].astype(BF)
+            sums = jnp.sum(gpu[...].astype(F32), axis=0, keepdims=True)
+            for kind in range(3):
+                part = slice(kind * 128, (kind + 1) * 128)
+                vbq[0:1, lanes(kind * D + c * THIRD + u * 128)] = sums[:, part]
+                gp[:, lanes(kind * THIRD + u * 128)] = gpu[:, part]
+
+            def weights(zz, inner):
+                block = jnp.dot(n1t[rows_at(zz * 192, 192, 64), :], gpu[...], preferred_element_type=F32)
+                for i in range(4):
+                    gq[u, zz, i // 2, i % 2] = block[i * 48 : (i + 1) * 48].astype(BF)
+                return inner
+
+            lax.fori_loop(0, 4, weights, 0)
+            for which in range(3):
+                @pl.when(u == which)
+                def _():
+                    queue[which].s1()
+            return carry
+
+        lax.fori_loop(0, 3, unit, 0)
+
+        def back_rows(b):
+            return lax.dot_general(gp[rows_at(b * 256, 256), :], wqm[...], LAST, preferred_element_type=F32)
+
+        def back_peer(yy, carry):
+            fb[yy] = back_rows(yy * 2 + c2)
+            return carry
+
+        lax.fori_loop(0, 2, back_peer, 0)
+        part_c.start()
+        queue[1].s2()
+
+        def back_own(yy, carry):
+            fc[yy] = back_rows(yy * 2 + c)
+            return carry
+
+        lax.fori_loop(0, 2, back_own, 0)
+        queue[2].s2()
+        queue[0].s4()
+
+    part_c = k.remote(fb, fr, k.pc)
+    pl.run_scoped(
+        backward, vmem((1024, THIRD), BF), vmem((THIRD, 1024), BF), vmem((1024, THIRD), BF), vmem((1024, THIRD), BF),
+        vmem((THIRD, 1024), F32), vmem((D, 1024), BF), vmem((128, 1024), BF), vmem((128, 1024), BF),
+        vmem((1024, 128), F32), vmem((1024, 128), F32), vmem((1024, 3 * THIRD), BF), vmem((1024, THIRD), BF),
+        vmem((D, 1152), BF))
+
+    gain = vrows[0:1, 0:D]
+    vs[0:2, :] = jnp.zeros((2, D), F32)
+    part_c.wait_recv()
+
+    def last_back(yy, carry):
+        normed, scale = unit_rows(tok_all[yy, c].astype(F32))
+        grad = fc[yy] + fr[yy]
+        vs[0:1, :] += jnp.sum(grad * normed, axis=0, keepdims=True)
+        vs[1:2, :] += jnp.sum(grad, axis=0, keepdims=True)
+        gtb[yy] = (fa[yy] + norm_back(grad * gain, normed, scale)).astype(BF)
+        return carry
+
+    lax.fori_loop(0, 2, last_back, 0)
+    gt_own = k.local(gtb.at[y], out_gt.at[y])
+    gt_y = k.remote(gtb.at[y2], out_gt.at[y], k.py)
+    gt_own.start()
+    gt_y.start()
+    queue[1].s3()
+    for index, wide in enumerate(WIDTHS):
+        if index == 2:
+            row = vbq[...]
+        elif index == 6:
+            row = vup[...]
+        else:
+            row = vs[index : index + 1, :]
+        vtab[pl.ds(index, 32, stride=8), :] = collect_rows(row, wide)
+    table = vtab.reshape(4, 2, 2, 2, 8, 128)
+    v0 = k.remote(table.at[:, :, :, c2], vr0, k.pc)
+    v1 = k.remote(table.at[:, :, y2, c], vr1, k.py)
+    v2 = k.remote(table.at[:, x2, y, c], vr2, k.px)
+    v3 = [k.remote(table.at[k.zs[d], x, y, c], vr3.at[d], k.pz[d]) for d in range(3)]
+
+    def tile(zz, xx, yy):
+        return rows_at((((zz * 2 + xx) * 2 + yy) * 2 + c) * 8, 8, 8)
+
+    v0.start()
+    queue[2].s3()
+    up.s5()
+    outp.s5()
+    v0.wait_recv()
+
+    def add_core(i, carry):
+        zz, xx, yy = i // 4, lax.rem(i // 2, 2), lax.rem(i, 2)
+        vtab[tile(zz, xx, yy), :] += vr0[zz, xx, yy]
+        return carry
+
+    lax.fori_loop(0, 16, add_core, 0)
+    v1.start()
+    queue[1].s4()
+    queue[0].s5()
+    v1.wait_recv()
+
+    def add_y(i, carry):
+        vtab[tile(i // 2, lax.rem(i, 2), y), :] += vr1[i // 2, lax.rem(i, 2)]
+        return carry
+
+    lax.fori_loop(0, 8, add_y, 0)
+    v2.start()
+    queue[2].s4()
+    v2.wait_recv()
+
+    def add_x(zz, carry):
+        vtab[tile(zz, x, y), :] += vr2[zz]
+        return carry
+
+    lax.fori_loop(0, 4, add_x, 0)
+    start(v3)
+    queue[1].s5()
+    queue[2].s5()
+    arrive(v3)
+    out_vec[...] = vtab[tile(z, x, y), :] + vr3[0] + vr3[1] + vr3[2]
+    landed([gt_own, bo_own])
+    arrive([gt_y, bo_y])
+    for copy in k.sent:
+        copy.wait_send()
+    for scatter in queue:
+        scatter.gone()
+
+
+def layer_call(*operands):
+    sds = jax.ShapeDtypeStruct
+    vmem = pltpu.VMEM
+    dma = pltpu.SemaphoreType.DMA
+    results = (
+        sds((2, 256, D), BF), sds((2, 256, D), BF), sds((24, 3 * D), F32), sds((24, D), F32), sds((24, FF), F32),
+        sds((96, D), F32), sds((8, 128), F32),
+    )
+    held = (
+        sds((4, 2, 2, 48, 1152), BF), sds((2, 4, 2, 2, 48, 384), BF), sds((2, 4, 2, 2, 48, 1536), BF),
+        sds((2, 4, 2, 2, 192, 384), BF), sds((4, 2, 2, 2, 8, 128), BF), sds((1024, THIRD), BF), sds((THIRD, 1024), BF),
+        sds((1024, THIRD), BF), sds((1024, THIRD), BF), sds((THIRD, 1024), F32), sds((D, 1024), BF),
+    )
+    scratch = [
+        vmem((4, 2, 2, 2, 8, 128), BF), vmem((2, 2, 256, D), BF), vmem((8, FF), F32),
+        vmem((2, D, THIRD), BF), vmem((2, 2, 256, THIRD), BF), vmem((2, 256, D), BF), vmem((2, 256, D), BF),
+        vmem((2, 256, D), BF), vmem((2, 2, 256, THIRD), BF), vmem((2, 256, D), F32), vmem((2, 256, D), F32),
+        vmem((2, 256, D), F32), vmem((2, 256, D), F32), vmem((8, 1024), F32),
+    ]
+    kinds = ((192, 384, 128), (48, 1536, 768), (48, 384, 256))
+    scratch += [vmem((2, 4, 2, 2, r, n), BF) for r, n, _ in kinds] + [vmem((3, 4, 2, 2, 48, 384), BF)]
+    scratch += [vmem((4, 2, 2, r, n), BF) for r, n, _ in kinds]
+    for r, n, cut in kinds:
+        scratch += [vmem((4, 2, r, cut), BF), vmem((4, 2, r, n - cut), BF)]
+    for r, n, cut in kinds:
+        scratch += [vmem((4, r, cut), BF), vmem((4, r, n - cut), BF)]
+    scratch += [vmem((3, r, n), BF) for r, n, _ in kinds]
+    scratch += [vmem((2, r // 2, n), F32) for r, n, _ in kinds]
+    scratch += [vmem((r // 2, n), F32) for r, n, _ in kinds]
+    scratch += [
+        vmem((3, 4, 2, 48, 128), BF), vmem((3, 4, 2, 48, 256), BF), vmem((3, 4, 48, 128), BF), vmem((3, 4, 48, 256), BF),
+        vmem((3, 3, 48, 384), BF), vmem((3, 2, 24, 384), F32), vmem((3, 24, 384), F32),
+        vmem((8, D), F32), vmem((1, 3 * D), F32), vmem((1, FF), F32), vmem((256, 128), F32), vmem((4, 2, 2, 8, 128), F32),
+        vmem((4, 2, 8, 128), F32), vmem((4, 8, 128), F32), vmem((3, 8, 128), F32),
+        dma((REMOTES,)), dma((REMOTES,)), dma((LOCALS,)),
+    ]
+    return pl.pallas_call(
+        layer_kernel,
+        out_shape=results + held,
+        in_specs=[SM] + [ANY] * 7,
+        out_specs=(ANY, ANY) + (VM,) * 5 + (ANY,) * len(held),
+        scratch_shapes=scratch,
+        compiler_params=pltpu.CompilerParams(
+            collective_id=0, has_side_effects=True, vmem_limit_bytes=63 * 2**20),
+    )(*operands)[: len(results)]
+
+
+def pack_vectors(vectors):
+    return jnp.stack([jnp.pad(v, (0, 128 - v.shape[0])) for v in vectors])
+
+
+def body(
+    tokens, cotangent, prefix, ln1_gain, ln1_bias, w_qkv, b_qkv, w_out, b_out,
+    ln2_gain, ln2_bias, w_up, b_up, w_down, b_down,
+):
+    vec = pack_vectors((ln1_gain, ln1_bias, b_qkv, b_out, ln2_gain, ln2_bias, b_up, b_down))
+    block_out, grad_tokens, gq, go, gu, gd, gvec = layer_call(
+        prefix, tokens, cotangent, vec, w_qkv, w_out, w_up, w_down)
+    rows = [gvec[i, :wide] for i, wide in enumerate(WIDTHS)]
+    return (
+        block_out, grad_tokens, rows[0], rows[1], gq, rows[2], go, rows[3], rows[4], rows[5], gu, rows[6], gd, rows[7],
+    )
+
+
+def fits(mesh):
+    return dict(mesh.shape) == {"dp": 8, "seq": 4}
 
 
 norm_eps = 1e-05
@@ -330,7 +1229,7 @@
     return (grad_in.astype(jnp.bfloat16).reshape(grad_part.shape), weight_grads)
 
 
-def body(
+def general_body(
     tokens,
     cotangent,
     prefix,
@@ -477,4 +1376,5 @@
         P(("dp", "seq"), None),
         P(("dp", "seq")),
     )
-    return jax.shard_map(body, mesh=mesh, in_specs=in_specs, out_specs=out_specs, check_vma=False)
+    chosen = body if fits(mesh) else general_body
+    return jax.shard_map(chosen, mesh=mesh, in_specs=in_specs, out_specs=out_specs, check_vma=False)

time: 1030 us -> 238 us (0.23)
  waiting for transfers between devices: 640 us -> 0 us
  Pallas kernels: 0 us -> 224 us
  matrix products: 147 us -> 0 us
  blocking collectives: 83.7 us -> 0 us
  other arithmetic: 59.7 us -> 0 us
  local copies, waits for them, and re-layouts: 67.5 us -> 12.9 us
  between operations: 15.6 us -> 0.69 us
    reduce_scatter x6 -> x0, waiting for transfers between devices: 442 us -> none  [the longest x1 142 us: body(): lax.psum_scatter(totals[10], ('dp', 'seq'), scatter_dimension=0, tiled=True)]
    pallas_call x0 -> x1, Pallas kernels: none -> 224 us  [layer_call(): pl.pallas_call(layer_kernel, out_shape=results + held, in_specs=[SM] + [A...]
    all_gather x8 -> x0, waiting for transfers between devices: 194 us -> none  [the longest x1 56.2 us: body(): lax.all_gather(shards[10], ('dp', 'seq'), axis=0, tiled=True)]
    dot_general x52 -> x0, matrix products: 147 us -> none  [the longest x4 15.9 us: grad_terms(): jnp.einsum('bqhd,bkhd->bqhk', grad_heads, to_heads(value_flat), preferred...]
    unnamed x2 -> x0, blocking collectives: 83.7 us -> none
    unnamed x252 -> x16, local copies, waits for them, and re-layouts: 27 us -> 5.76 us
    reduce_sum x15 -> x0, other arithmetic: 20 us -> none  [the longest x4 6.72 us: update(): normaliser = normaliser * factor + jnp.sum(exponent, axis=-1)]
    convert_element_type x12 -> x0, other arithmetic: 16.1 us -> none  [the longest x2 9.93 us: attend_back(): grad_keys.astype(jnp.bfloat16)]
  transfers between devices with their start and end apart: 14 -> 0, of which waited for: 13 -> 0; matrix products, arithmetic and copies ran while one was open for 18% -> 0% of each run, Pallas kernels for 0% -> 0%
where the time goes in v2:
time: 238 us; the launch traced here: 237 us
  Pallas kernels  224 us (94%)
  local copies, waits for them, and re-layouts  12.9 us (5%)
    pallas_call x1, Pallas kernels, layer_call(): pl.pallas_call(layer_kernel, out_shape=results + held, in_specs=[SM] + [A...  224 us
    unnamed x16, local copies, waits for them, and re-layouts  5.76 us

profile of v2, /device:TPU:0, one launch (start us, length us, event | category | flops | bytes accessed | tf_op | source)
XLA Modules:
  0.0 237.2 jit_solution(5544046815137351)
XLA Ops:
  0.6 0.7 pad_bitcast_fusion.6
  1.3 0.7 pad_bitcast_fusion.4
  2.0 0.7 pad_bitcast_fusion.2
  2.7 0.7 pad_bitcast_fusion
  3.4 0.6 stack.35.vec_s
  4.0 223.5 %shard_map.254 = (bf16[2,256,768]{2,1,0:T(8,128)(2,1)}, bf16[2,256,768]{2,1,0:T(8,128)(2,1)}, f32[24,2304]{1,0:T(8,128)}, f32[24,768]{1,0:T(8,128)}, f32[24,3072...) custom-call(s32[2]{0:T(128)} %prefix.1, ...), custom_call_target="tpu_custom_call" | custom-call | tf_op jit(solution)/shard_map/pallas_call | solution.py:878
  227.5 0.0 copy-start
  227.5 0.0 copy-start.3
  227.5 1.3 slice_bitcast_fusion.5
  228.8 1.2 slice_bitcast_fusion.1
  230.0 1.4 slice_bitcast_fusion
  231.4 0.0 copy-start.4
  231.4 0.0 copy-start.2
  231.4 2.1 copy.35
  233.5 0.0 copy-done
  233.5 0.0 copy-start.1
  233.5 0.9 copy.36
  234.4 0.0 copy-done.3
  234.4 0.7 copy.37
  235.1 0.0 copy-done.4
  235.1 0.6 copy.38
  235.7 0.0 copy-done.2
  235.7 0.7 copy.39
  236.5 0.0 copy-done.1
  236.5 0.7 copy.40
Async XLA Ops:
  227.5 6.0 %copy-start = (bf16[2,256,768]{2,1,0:T(8,128)(2,1)S(1)}, bf16[2,256,768]{2,1,0:T(8,128)(2,1)}, u32[]{:S(2)}) copy-start(bf16[2,256,768]{2,1,0:T(8,128)(2,1)} %get-tuple-element.57) | copy-start | bytes 2359300
  227.5 6.9 %copy-start.3 = (f32[24,2304]{1,0:T(8,128)S(1)}, f32[24,2304]{1,0:T(8,128)}, u32[]{:S(2)}) copy-start(f32[24,2304]{1,0:T(8,128)} %get-tuple-element.60) | copy-start | bytes 663556
  231.4 3.7 %copy-start.4 = (f32[24,768]{1,0:T(8,128)S(1)}, f32[24,768]{1,0:T(8,128)}, u32[]{:S(2)}) copy-start(f32[24,768]{1,0:T(8,128)} %get-tuple-element.62) | copy-start | bytes 221188
  231.4 4.3 %copy-start.2 = (f32[24,3072]{1,0:T(8,128)S(1)}, f32[24,3072]{1,0:T(8,128)}, u32[]{:S(2)}) copy-start(f32[24,3072]{1,0:T(8,128)} %get-tuple-element.66) | copy-start | bytes 884740
  233.5 2.9 %copy-start.1 = (f32[96,768]{1,0:T(8,128)S(1)}, f32[96,768]{1,0:T(8,128)}, u32[]{:S(2)}) copy-start(f32[96,768]{1,0:T(8,128)} %get-tuple-element.68) | copy-start | bytes 884740

commit v3 on v2

--- a/solution.py
+++ b/solution.py
@@ -1,3 +1,5 @@
+import functools
+
 import jax
 import jax.numpy as jnp
 from jax import lax
@@ -133,39 +135,28 @@
         barrier = pltpu.get_barrier_semaphore()
         for dev in [self.px, self.py, self.pc] + self.pz:
             pl.semaphore_signal(barrier, inc=1, device_id=dev, device_id_type=MESH)
-        pl.semaphore_wait(barrier, 6)
+
+    def greeted(self):
+        pl.semaphore_wait(pltpu.get_barrier_semaphore(), 6)
 
 
 class Gather:
-    def __init__(self, links, shard, full, cut, kinds=None):
+    def __init__(self, links, own, other, mine, theirs, cut, full=None):
         k = links
-        self.k, self.full, self.kinds = k, full, kinds
-        rows = shard.shape[0]
-        own = pl.ds(pl.multiple_of(k.c * rows, 8), rows)
-        mine = full if kinds else full.at[k.c]
-        theirs = full if kinds else full.at[k.c2]
-        half = full.shape[-1]
+        rows = own.shape[0]
+        at = pl.ds(pl.multiple_of(k.c * rows, 8), rows)
         z, x, y = k.z, k.x, k.y
-        if kinds:
-            self.own, self.c0 = [], []
-            for kind in range(kinds):
-                there = pl.ds(kind * THIRD, THIRD)
-                self.own.append(k.local(shard.at[:, lanes(kind * D + k.c * THIRD, THIRD)], mine.at[z, x, y, own, there]))
-                self.c0.append(k.remote(shard.at[:, lanes(kind * D + k.c2 * THIRD, THIRD)],
-                                        theirs.at[z, x, y, own, there], k.pc))
-        else:
-            self.own = [k.local(shard.at[:, lanes(k.c * half, half)], mine.at[z, x, y, own])]
-            self.c0 = [k.remote(shard.at[:, lanes(k.c2 * half, half)], theirs.at[z, x, y, own], k.pc)]
+        self.own = [k.local(own, mine.at[z, x, y, at])]
+        self.c0 = [k.remote(other, theirs.at[z, x, y, at], k.pc)]
         self.c1 = [k.remote(mine.at[z, x, y], mine.at[z, x, y], dev) for dev in k.pz]
         a, b = slice(0, cut), slice(cut, None)
         self.c2 = [k.remote(mine.at[:, x, y, :, a], mine.at[:, x, y, :, a], k.px),
                    k.remote(mine.at[:, x, y, :, b], mine.at[:, x, y, :, b], k.py)]
         self.c3 = [k.remote(mine.at[:, :, y, :, a], mine.at[:, :, y, :, a], k.py),
                    k.remote(mine.at[:, x, :, :, b], mine.at[:, x, :, :, b], k.px)]
-        self.c4 = [] if kinds else [k.remote(full.at[k.c], full.at[k.c], k.pc)]
+        self.c4 = [] if full is None else [k.remote(full.at[k.c], full.at[k.c], k.pc)]
 
     def s0(self):
-        start(self.own)
         start(self.c0)
 
     def s1(self):
@@ -292,10 +283,10 @@
 
 
 def layer_kernel(
-    prefix, tok, cot, vec_s, wq_s, wo_s, wu_s, wd_s,
+    prefix, tok, cot, v0_s, v1_s, v2_s, v3_s, v4_s, v5_s, v6_s, v7_s, wq_s, wo_s, wu_s, wd_s,
     out_bo, out_gt, out_q, out_o, out_u, out_d, out_vec,
     wq, wo, wu, wd, gv, k_qs, k_qst, k_k, k_v, k_att, k_n1t,
-    gvm, tok_all, vrows, wom, al_send, al, cotm, ga_send, ga_all, fa, fb, fc, fr, lt,
+    vec_s, wq_p, gvm, tok_all, vrows, wom, al_send, al, cotm, ga_send, ga_all, fa, fb, fc, fr, lt,
     gd, gu, go, gq,
     r0d, r0u, r0o, r1ad, r1bd, r1au, r1bu, r1ao, r1bo, r2ad, r2bd, r2au, r2bu, r2ao, r2bo, r3d, r3u, r3o,
     td, tu, to, fd, fu, fo,
@@ -309,49 +300,75 @@
     k.greet()
     vmem = pltpu.VMEM
 
-    gather_q = Gather(k, wq_s, wq, 512, 3)
-    gather_o = Gather(k, wo_s, wo, 256)
-    gather_u = Gather(k, wu_s, wu, 768)
-    gather_d = Gather(k, wd_s, wd, 128)
+    vec_s[...] = jnp.zeros_like(vec_s)
+    for index, (wide, ref) in enumerate(zip(WIDTHS, (v0_s, v1_s, v2_s, v3_s, v4_s, v5_s, v6_s, v7_s))):
+        vec_s[index : index + 1, 0:wide] = ref[...].astype(F32).reshape(1, wide)
+    for core in range(2):
+        for u in range(3):
+            for kind in range(3):
+                first = kind * D + core * THIRD + u * 128
+                wq_p[core, u, :, kind * 128 : (kind + 1) * 128] = wq_s[:, first : first + 128]
+    cuts = (128, 256, 128)
+    gather_q = [Gather(k, wq_p.at[c, u], wq_p.at[c2, u], wq.at[u], wq.at[u], cuts[u]) for u in range(3)]
+
+    def halves(shard, full, cut):
+        half = full.shape[-1]
+        return Gather(k, shard.at[:, lanes(c * half, half)], shard.at[:, lanes(c2 * half, half)], full.at[c], full.at[c2],
+                      cut, full)
+
+    gather_o = halves(wo_s, wo, 256)
+    gather_u = halves(wu_s, wu, 768)
+    gather_d = halves(wd_s, wd, 128)
     own_vec = k.local(vec_s, gv.at[z, x, y, c])
+    own_tok = k.local(tok.at[y], tok_all.at[y, c])
+    own_cot = k.local(cot.at[y], cotm.at[y])
+    own_vec.start()
+    start(gather_q[0].own)
+    own_tok.start()
+    start(gather_q[1].own + gather_q[2].own + gather_o.own + gather_u.own + gather_d.own)
+    own_cot.start()
+    k.greeted()
+
     vec_c = k.remote(vec_s, gv.at[z, x, y, c], k.pc)
-    own_vec.start()
+    tok_y = k.remote(tok.at[y2], tok_all.at[y, c], k.py)
+    cot_y = k.remote(cot.at[y2], cotm.at[y], k.py)
+    gather_q[0].s0()
     vec_c.start()
-    own_tok = k.local(tok.at[y], tok_all.at[y, c])
-    tok_y = k.remote(tok.at[y2], tok_all.at[y, c], k.py)
-    own_tok.start()
     tok_y.start()
-    gather_q.s0()
-    own_cot = k.local(cot.at[y], cotm.at[y])
-    cot_y = k.remote(cot.at[y2], cotm.at[y], k.py)
+    for gather in (gather_q[1], gather_q[2], gather_o, gather_u, gather_d):
+        gather.s0()
+    gather_q[0].s1()
     own_vec.wait()
     vec_c.wait_recv()
     vec_z = [k.remote(gv.at[z, x, y], gv.at[z, x, y], dev) for dev in k.pz]
     start(vec_z)
-    gather_q.s1()
-    gather_o.s0()
-    gather_u.s0()
-    gather_d.s0()
+    gather_q[1].s1()
     own_tok.wait()
+    arrive(vec_z)
+    vec_x = k.remote(gv.at[:, x, y], gv.at[:, x, y], k.px)
+    vec_x.start()
+    gather_q[0].s2()
+    gather_q[2].s1()
     tok_y.wait_recv()
     tok_c = k.remote(tok_all.at[:, c], tok_all.at[:, c], k.pc)
     tok_c.start()
-    own_cot.start()
     cot_y.start()
-    arrive(vec_z)
-    vec_x = k.remote(gv.at[:, x, y], gv.at[:, x, y], k.px)
-    vec_x.start()
     vec_x.wait_recv()
     vec_y = k.remote(gv.at[:, :, y], gv.at[:, :, y], k.py)
     vec_y.start()
-    tok_c.wait_recv()
+    gather_q[1].s2()
+    gather_o.s1()
+    gather_q[0].s3()
+    gather_q[2].s2()
+    gather_u.s1()
     vec_y.wait_recv()
     table = k.local(gv, gvm)
     table.start()
     table.wait()
-    table = gvm[...].reshape(256, 128)
+    table = gvm[...].reshape(256, 128).astype(BF)
     for index, wide in enumerate(WIDTHS):
         vrows[index : index + 1, 0 : 32 * wide] = spread_row(table, index, wide)
+    tok_c.wait_recv()
 
     mine_cols = lanes(c * THIRD, THIRD)
     peer_cols = lanes(c2 * THIRD, THIRD)
@@ -359,6 +376,7 @@
     al_c = k.remote(al_send.at[:, c2], al.at[:, :, mine_cols], k.pc)
     limit = prefix[y] - 1
     sub = lax.broadcasted_iota(jnp.int32, (128, 256), 0)
+    wq3 = wq.reshape(3, D, THIRD)
 
     def forward(n1, n1t, vt, qs, qst, keys_ref, values_ref, att, wqm):
         gain = vrows[0:1, 0:D]
@@ -373,89 +391,93 @@
             return carry
 
         lax.fori_loop(0, 4, norm_block, 0)
-        keep_n1t = k.local(n1t, k_n1t)
-        keep_n1t.start()
-        gather_q.s2()
-        gather_o.s1()
-        gather_u.s1()
-        gather_q.s3()
-        gather_o.s2()
-        gather_q.s4()
-        load_q = k.local(wq.reshape(D, 3 * THIRD), wqm)
-        load_q.start()
-        load_q.wait()
-
-        def project(b, carry):
-            rows = rows_at(b * 256, 256)
-            block = n1[rows, :]
-            parts = []
-            for kind in range(3):
-                bias = vrows[2:3, lanes(kind * D + c * THIRD, THIRD)]
-                value = jnp.dot(block, wqm[:, kind * THIRD : (kind + 1) * THIRD], preferred_element_type=F32)
-                parts.append((value + bias).astype(BF))
-            queries = parts[0].astype(F32) * 0.125
-            qs[rows, :] = queries.astype(BF)
-            qst[:, rows] = queries.T.astype(BF)
-            keys_ref[rows, :] = parts[1]
-            values_ref[rows, :] = parts[2]
-            vt[:, rows] = parts[2].astype(F32).T.astype(BF)
+        keep = [k.local(n1t, k_n1t), k.local(qs, k_qs), k.local(qst, k_qst), k.local(keys_ref, k_k),
+                k.local(values_ref, k_v), k.local(att, k_att)]
+        keep[0].start()
+        gather_q[1].s3()
+        load_q = [k.local(wq3.at[u], wqm.at[u]) for u in range(3)]
+        load_o = k.local(wo.reshape(2, D, THIRD), wom)
+
+        def head(u):
+            gather_q[u].s4()
+            load_q[u].start()
+            load_q[u].wait()
+
+        slots = {
+            (0, 3): [gather_q[2].s3, gather_o.s2], (0, 2): [gather_u.s2, gather_d.s1], (0, 1): [gather_o.s3], (0, 0): [],
+            (1, 3): [], (1, 2): [gather_u.s3], (1, 1): [gather_o.s4, gather_d.s2], (1, 0): [],
+            (2, 3): [], (2, 2): [gather_o.done, load_o.start], (2, 1): [], (2, 0): [],
+        }
+
+        def unit(u, carry):
+            cols = lanes(u * 128)
+            for which in range(3):
+                @pl.when(u == which)
+                def _():
+                    head(which)
+
+            def project(b, inner):
+                rows = rows_at(b * 256, 256)
+                value = jnp.dot(n1[rows, :], wqm[u], preferred_element_type=F32)
+                parts = []
+                for kind in range(3):
+                    bias = vrows[2:3, lanes(kind * D + c * THIRD + u * 128)]
+                    parts.append((value[:, kind * 128 : (kind + 1) * 128] + bias).astype(BF))
+                queries = parts[0].astype(F32) * 0.125
+                qs[rows, cols] = queries.astype(BF)
+                qst[cols, rows] = queries.T.astype(BF)
+                keys_ref[rows, cols] = parts[1]
+                values_ref[rows, cols] = parts[2]
+                vt[cols, rows] = parts[2].astype(F32).T.astype(BF)
+                return inner
+
+            lax.fori_loop(0, 4, project, 0)
+            for block in (3, 2, 1, 0):
+                attend(u, block)
+                for which in range(3):
+                    if slots[which, block]:
+                        @pl.when(u == which)
+                        def _():
+                            for step in slots[which, block]:
+                                step()
             return carry
 
-        lax.fori_loop(0, 4, project, 0)
-        keep = [k.local(qs, k_qs), k.local(qst, k_qst), k.local(keys_ref, k_k), k.local(values_ref, k_v)]
-        start(keep)
-        gather_u.s2()
-        gather_d.s1()
-
-        def attend(block):
+        def attend(u, block):
             rows = min(4, max(block + 1, 2)) * 256
-            qcols = pl.ds(block * 256, 256)
-
-            def unit(u, carry):
-                cols = lanes(u * 128)
-                keys = keys_ref[0:rows, cols]
-                queries = qst[cols, qcols]
-                qpos = block * 256 + lax.broadcasted_iota(jnp.int32, (1, 256), 1)
-                seen = lax.broadcasted_iota(jnp.int32, (rows, 256), 0) <= jnp.maximum(qpos, limit)
-                for half in range(2):
-                    chosen = jnp.where(sub // 64 == half, queries, jnp.zeros_like(queries))
-                    scores = jnp.dot(keys, chosen, preferred_element_type=F32)
-                    size = jnp.where(seen, jnp.abs(scores), NEG)
-                    top = jnp.max(size, axis=0, keepdims=True)
-                    exponent = jnp.exp(size - top)
-                    total = jnp.sum(exponent, axis=0, keepdims=True)
-                    weights = jnp.where(scores > 0, exponent, jnp.where(scores < 0, -exponent, 0.0)).astype(BF)
-                    at = pl.ds(pl.multiple_of(u * 128 + half * 64, 64), 64)
-                    att[at, qcols] = jnp.dot(vt[at, 0:rows], weights, preferred_element_type=F32) / total
-                    lt[pl.ds(u * 2 + half, 1), qcols] = top + jnp.log(total)
-                al_send[block // 2, block % 2, :, cols] = att[cols, qcols].T.astype(BF)
-                return carry
-
-            lax.fori_loop(0, 3, unit, 0)
-
-        attend(3)
-        gather_o.s3()
-        attend(2)
-        gather_u.s3()
-        attend(1)
-        gather_o.s4()
-        attend(0)
+            qcols = slice(block * 256, (block + 1) * 256)
+            cols = lanes(u * 128)
+            keys = keys_ref[0:rows, cols]
+            queries = qst[cols, qcols]
+            qpos = block * 256 + lax.broadcasted_iota(jnp.int32, (1, 256), 1)
+            seen = lax.broadcasted_iota(jnp.int32, (rows, 256), 0) <= jnp.maximum(qpos, limit)
+            for half in range(2):
+                chosen = jnp.where(sub // 64 == half, queries, jnp.zeros_like(queries))
+                scores = jnp.dot(keys, chosen, preferred_element_type=F32)
+                size = jnp.where(seen, jnp.abs(scores), NEG)
+                top = jnp.max(size, axis=0, keepdims=True)
+                exponent = jnp.exp(size - top)
+                total = jnp.sum(exponent, axis=0, keepdims=True)
+                weights = jnp.where(scores > 0, exponent, jnp.where(scores < 0, -exponent, 0.0)).astype(BF)
+                at = pl.ds(pl.multiple_of(u * 128 + half * 64, 64), 64)
+                att[at, qcols] = jnp.dot(vt[at, 0:rows], weights, preferred_element_type=F32) / total
+                lt[pl.ds(u * 2 + half, 1), qcols] = top + jnp.log(total)
+            al_send[block // 2, block % 2, :, cols] = att[cols, qcols].T.astype(BF)
+
+        lax.fori_loop(0, 3, unit, 0)
         al_own.start()
         al_c.start()
-        keep_att = k.local(att, k_att)
-        keep_att.start()
-        gather_o.done()
-        load_o = k.local(wo.reshape(2, D, THIRD), wom)
-        load_o.start()
-        gather_d.s2()
+        start(keep[1:])
+        gather_u.s4()
+        gather_d.s3()
+        load_o.wait()
         al_own.wait()
         al_c.wait_recv()
-        load_o.wait()
-        landed(keep + [keep_n1t, keep_att])
+        landed(keep)
 
     pl.run_scoped(
         forward, vmem((1024, D), BF), vmem((D, 1024), BF), vmem((THIRD, 1024), BF), vmem((1024, THIRD), BF),
-        vmem((THIRD, 1024), BF), vmem((1024, THIRD), BF), vmem((1024, THIRD), BF), vmem((THIRD, 1024), F32), vmem((D, 1152), BF))
+        vmem((THIRD, 1024), BF), vmem((1024, THIRD), BF), vmem((1024, THIRD), BF), vmem((THIRD, 1024), F32),
+        vmem((3, D, THIRD), BF))
 
     def put_to(out, half):
         def put(value, core):
@@ -466,7 +488,7 @@
     up = Scatter(k, gu, r0u, r1au, r1bu, r2au, r2bu, r3u, tu, fu, put_to(out_u, 1536), 768)
     outp = Scatter(k, go, r0o, r1ao, r1bo, r2ao, r2bo, r3o, to, fo, put_to(out_o, THIRD), 256)
 
-    def middle(wbuf, wdb, hid, slope, n2, n2t, alt, gpc):
+    def feed(wbuf, wdb, hid, slope, n2, n2t, alt, gpc):
         b_out, gain, shift = vrows[3:4, 0:D], vrows[4:5, 0:D], vrows[5:6, 0:D]
 
         def begin(yy, carry):
@@ -501,7 +523,6 @@
             return k.local(wd2.at[:, rows_at(h * 1536 + part * D, D), :], wdb.at[slot])
 
         forth = (c, c2)
-        gather_u.s4()
         loads = [up_load(j, j % 2, forth) for j in range(4)]
         loads[0].start()
         for j in range(4):
@@ -522,8 +543,6 @@
                 return carry
 
             lax.fori_loop(0, 2, ahead, 0)
-        gather_d.s3()
-
         vs[7:8, :] = jnp.sum(cotm[0].astype(F32), axis=0, keepdims=True) + jnp.sum(
             cotm[1].astype(F32), axis=0, keepdims=True)
 
@@ -587,9 +606,14 @@
             lax.fori_loop(0, 4, up_grad, 0)
             if j == 1:
                 up.s0()
+            if j == 2:
+                down.s2()
         bo[...] = (fa[...] + fc[...] + vrows[7:8, 0:D].reshape(1, 1, D)).astype(BF)
         up.s1()
 
+    ga_c = k.remote(ga_send.at[:, :, peer_cols], ga_all.at[:, c], k.pc)
+    def turn(alt, gpc):
+        gain = vrows[4:5, 0:D]
         vs[3:6, :] = jnp.zeros((3, D), F32)
 
         def mid_back(yy, carry):
@@ -625,16 +649,6 @@
         lax.fori_loop(0, 4, out_grad, 0)
         outp.s0()
 
-    ga_c = k.remote(ga_send.at[:, :, peer_cols], ga_all.at[:, c], k.pc)
-    pl.run_scoped(
-        middle, vmem((2, D, D), BF), vmem((2, 2, D, THIRD), BF), vmem((512, FF), BF), vmem((512, FF), F32),
-        vmem((512, D), BF), vmem((D, 512), BF), vmem((D, 512), BF), vmem((512, D), BF))
-
-    bo_own = k.local(bo.at[y], out_bo.at[y])
-    bo_y = k.remote(bo.at[y2], out_bo.at[y], k.py)
-    bo_own.start()
-    bo_y.start()
-
     def put_q(u):
         def put(value, core):
             for kind in range(3):
@@ -648,19 +662,28 @@
                        put_q(u), 128, base=[b + u for b in bases], whole=False)
 
     queue = [query_scatter(u) for u in range(3)]
-
-    def backward(qs, qst, keys_ref, values_ref, att, n1t, gt, kt, dk, dv, gp, gpu, wqm):
+    bo_own = k.local(bo.at[y], out_bo.at[y])
+    bo_y = k.remote(bo.at[y2], out_bo.at[y], k.py)
+
+    def send_out():
+        bo_own.start()
+        bo_y.start()
+
+    def backward(alt, gpc, qs, qst, keys_ref, values_ref, att, n1t, gt, kt, dk, dv, gpu, wqm):
         loads = [k.local(k_qs, qs), k.local(k_qst, qst), k.local(k_k, keys_ref), k.local(k_v, values_ref),
-                 k.local(k_att, att), k.local(k_n1t, n1t), k.local(wq.reshape(D, 3 * THIRD), wqm)]
+                 k.local(k_att, att), k.local(k_n1t, n1t), k.local(wq3, wqm)]
         start(loads)
+        turn(alt, gpc)
+        fb[...] = jnp.zeros_like(fb)
+        fc[...] = jnp.zeros_like(fc)
         ga_c.wait_recv()
         landed(loads)
         lane = lax.broadcasted_iota(jnp.int32, (256, 128), 1)
         vbq[...] = jnp.zeros_like(vbq)
         slots = {
-            (0, 3): [down.s2, outp.s1], (0, 2): [], (0, 1): [down.s3], (0, 0): [up.s2],
-            (1, 3): [], (1, 2): [outp.s2], (1, 1): [up.s3], (1, 0): [down.s4, outp.s3],
-            (2, 3): [queue[0].s2], (2, 2): [down.s5], (2, 1): [queue[0].s3, up.s4], (2, 0): [outp.s4],
+            (0, 3): [outp.s1, down.s3], (0, 2): [], (0, 1): [up.s2], (0, 0): [send_out],
+            (1, 3): [outp.s2], (1, 2): [down.s4], (1, 1): [up.s3], (1, 0): [outp.s3, down.s5],
+            (2, 3): [queue[0].s2], (2, 2): [], (2, 1): [queue[0].s3], (2, 0): [outp.s4],
         }
 
         def unit(u, carry):
@@ -717,7 +740,6 @@
             for kind in range(3):
                 part = slice(kind * 128, (kind + 1) * 128)
                 vbq[0:1, lanes(kind * D + c * THIRD + u * 128)] = sums[:, part]
-                gp[:, lanes(kind * THIRD + u * 128)] = gpu[:, part]
 
             def weights(zz, inner):
                 block = jnp.dot(n1t[rows_at(zz * 192, 192, 64), :], gpu[...], preferred_element_type=F32)
@@ -730,61 +752,61 @@
                 @pl.when(u == which)
                 def _():
                     queue[which].s1()
+
+            def back_rows(b):
+                return lax.dot_general(gpu[rows_at(b * 256, 256), :], wqm[u], LAST, preferred_element_type=F32)
+
+            def back_peer(yy, inner):
+                fb[yy] += back_rows(yy * 2 + c2)
+                return inner
+
+            def back_own(yy, inner):
+                fc[yy] += back_rows(yy * 2 + c)
+                return inner
+
+            lax.fori_loop(0, 2, back_peer, 0)
+
+            @pl.when(u == 2)
+            def _():
+                part_c.start()
+
+            lax.fori_loop(0, 2, back_own, 0)
             return carry
 
         lax.fori_loop(0, 3, unit, 0)
 
-        def back_rows(b):
-            return lax.dot_general(gp[rows_at(b * 256, 256), :], wqm[...], LAST, preferred_element_type=F32)
-
-        def back_peer(yy, carry):
-            fb[yy] = back_rows(yy * 2 + c2)
-            return carry
-
-        lax.fori_loop(0, 2, back_peer, 0)
-        part_c.start()
-        queue[1].s2()
-
-        def back_own(yy, carry):
-            fc[yy] = back_rows(yy * 2 + c)
-            return carry
-
-        lax.fori_loop(0, 2, back_own, 0)
-        queue[2].s2()
-        queue[0].s4()
-
     part_c = k.remote(fb, fr, k.pc)
-    pl.run_scoped(
-        backward, vmem((1024, THIRD), BF), vmem((THIRD, 1024), BF), vmem((1024, THIRD), BF), vmem((1024, THIRD), BF),
-        vmem((THIRD, 1024), F32), vmem((D, 1024), BF), vmem((128, 1024), BF), vmem((128, 1024), BF),
-        vmem((1024, 128), F32), vmem((1024, 128), F32), vmem((1024, 3 * THIRD), BF), vmem((1024, THIRD), BF),
-        vmem((D, 1152), BF))
-
+
+    def both(alt, gpc):
+        pl.run_scoped(
+            functools.partial(feed, alt=alt, gpc=gpc), vmem((2, D, D), BF), vmem((2, 2, D, THIRD), BF),
+            vmem((512, FF), BF), vmem((512, FF), F32), vmem((512, D), BF), vmem((D, 512), BF))
+        pl.run_scoped(
+            functools.partial(backward, alt, gpc), vmem((1024, THIRD), BF), vmem((THIRD, 1024), BF), vmem((1024, THIRD), BF),
+            vmem((1024, THIRD), BF), vmem((THIRD, 1024), F32), vmem((D, 1024), BF), vmem((128, 1024), BF),
+            vmem((128, 1024), BF), vmem((1024, 128), F32), vmem((1024, 128), F32), vmem((1024, THIRD), BF),
+            vmem((3, D, THIRD), BF))
+
+    pl.run_scoped(both, vmem((D, 512), BF), vmem((512, D), BF))
+
+    queue[1].s2()
     gain = vrows[0:1, 0:D]
     vs[0:2, :] = jnp.zeros((2, D), F32)
-    part_c.wait_recv()
-
-    def last_back(yy, carry):
-        normed, scale = unit_rows(tok_all[yy, c].astype(F32))
-        grad = fc[yy] + fr[yy]
-        vs[0:1, :] += jnp.sum(grad * normed, axis=0, keepdims=True)
-        vs[1:2, :] += jnp.sum(grad, axis=0, keepdims=True)
-        gtb[yy] = (fa[yy] + norm_back(grad * gain, normed, scale)).astype(BF)
-        return carry
-
-    lax.fori_loop(0, 2, last_back, 0)
-    gt_own = k.local(gtb.at[y], out_gt.at[y])
-    gt_y = k.remote(gtb.at[y2], out_gt.at[y], k.py)
-    gt_own.start()
-    gt_y.start()
-    queue[1].s3()
+
+    def sums(core, ref):
+        def add(yy, carry):
+            normed, _ = unit_rows(tok_all[yy, core].astype(F32))
+            grad = ref[yy]
+            vs[0:1, :] += jnp.sum(grad * normed, axis=0, keepdims=True)
+            vs[1:2, :] += jnp.sum(grad, axis=0, keepdims=True)
+            return carry
+
+        lax.fori_loop(0, 2, add, 0)
+
+    sums(c2, fb)
+    sums(c, fc)
     for index, wide in enumerate(WIDTHS):
-        if index == 2:
-            row = vbq[...]
-        elif index == 6:
-            row = vup[...]
-        else:
-            row = vs[index : index + 1, :]
+        row = vbq[...] if index == 2 else vup[...] if index == 6 else vs[index : index + 1, :]
         vtab[pl.ds(index, 32, stride=8), :] = collect_rows(row, wide)
     table = vtab.reshape(4, 2, 2, 2, 8, 128)
     v0 = k.remote(table.at[:, :, :, c2], vr0, k.pc)
@@ -796,9 +818,20 @@
         return rows_at((((zz * 2 + xx) * 2 + yy) * 2 + c) * 8, 8, 8)
 
     v0.start()
-    queue[2].s3()
-    up.s5()
-    outp.s5()
+    queue[2].s2()
+    part_c.wait_recv()
+
+    def last_back(yy):
+        normed, scale = unit_rows(tok_all[yy, c].astype(F32))
+        grad = fc[yy] + fr[yy]
+        gtb[yy] = (fa[yy] + norm_back(grad * gain, normed, scale)).astype(BF)
+
+    gt_own = k.local(gtb.at[y], out_gt.at[y])
+    gt_y = k.remote(gtb.at[y2], out_gt.at[y], k.py)
+    last_back(y2)
+    gt_y.start()
+    last_back(y)
+    gt_own.start()
     v0.wait_recv()
 
     def add_core(i, carry):
@@ -808,8 +841,10 @@
 
     lax.fori_loop(0, 16, add_core, 0)
     v1.start()
-    queue[1].s4()
-    queue[0].s5()
+    queue[1].s3()
+    queue[2].s3()
+    up.s4()
+    queue[0].s4()
     v1.wait_recv()
 
     def add_y(i, carry):
@@ -818,7 +853,8 @@
 
     lax.fori_loop(0, 8, add_y, 0)
     v2.start()
-    queue[2].s4()
+    outp.s5()
+    queue[1].s4()
     v2.wait_recv()
 
     def add_x(zz, carry):
@@ -827,6 +863,9 @@
 
     lax.fori_loop(0, 4, add_x, 0)
     start(v3)
+    queue[2].s4()
+    up.s5()
+    queue[0].s5()
     queue[1].s5()
     queue[2].s5()
     arrive(v3)
@@ -848,12 +887,12 @@
         sds((96, D), F32), sds((8, 128), F32),
     )
     held = (
-        sds((4, 2, 2, 48, 1152), BF), sds((2, 4, 2, 2, 48, 384), BF), sds((2, 4, 2, 2, 48, 1536), BF),
-        sds((2, 4, 2, 2, 192, 384), BF), sds((4, 2, 2, 2, 8, 128), BF), sds((1024, THIRD), BF), sds((THIRD, 1024), BF),
+        sds((3, 4, 2, 2, 48, 384), BF), sds((2, 4, 2, 2, 48, 384), BF), sds((2, 4, 2, 2, 48, 1536), BF),
+        sds((2, 4, 2, 2, 192, 384), BF), sds((4, 2, 2, 2, 8, 128), F32), sds((1024, THIRD), BF), sds((THIRD, 1024), BF),
         sds((1024, THIRD), BF), sds((1024, THIRD), BF), sds((THIRD, 1024), F32), sds((D, 1024), BF),
     )
     scratch = [
-        vmem((4, 2, 2, 2, 8, 128), BF), vmem((2, 2, 256, D), BF), vmem((8, FF), F32),
+        vmem((8, 128), F32), vmem((2, 3, 24, THIRD), BF), vmem((4, 2, 2, 2, 8, 128), F32), vmem((2, 2, 256, D), BF), vmem((8, FF), F32),
         vmem((2, D, THIRD), BF), vmem((2, 2, 256, THIRD), BF), vmem((2, 256, D), BF), vmem((2, 256, D), BF),
         vmem((2, 256, D), BF), vmem((2, 2, 256, THIRD), BF), vmem((2, 256, D), F32), vmem((2, 256, D), F32),
         vmem((2, 256, D), F32), vmem((2, 256, D), F32), vmem((8, 1024), F32),
@@ -878,7 +917,7 @@
     return pl.pallas_call(
         layer_kernel,
         out_shape=results + held,
-        in_specs=[SM] + [ANY] * 7,
+        in_specs=[SM] + [ANY] * 2 + [VM] * 12,
         out_specs=(ANY, ANY) + (VM,) * 5 + (ANY,) * len(held),
         scratch_shapes=scratch,
         compiler_params=pltpu.CompilerParams(
@@ -886,18 +925,30 @@
     )(*operands)[: len(results)]
 
 
-def pack_vectors(vectors):
-    return jnp.stack([jnp.pad(v, (0, 128 - v.shape[0])) for v in vectors])
+def finish_kernel(bo, gt, gq, go, gu, gd, gvec, *out):
+    for source, result in zip((bo, gt, gq, go, gu, gd), out[:6]):
+        result[...] = source[...]
+    for index, wide in enumerate(WIDTHS):
+        out[6 + index][...] = gvec[index, 0:wide]
+
+
+def finish_call(*operands):
+    sds = jax.ShapeDtypeStruct
+    shapes = tuple(sds(o.shape, o.dtype) for o in operands[:6]) + tuple(sds((wide,), F32) for wide in WIDTHS)
+    return pl.pallas_call(
+        finish_kernel, out_shape=shapes, in_specs=[VM] * 7, out_specs=(VM,) * 14,
+        compiler_params=pltpu.CompilerParams(vmem_limit_bytes=32 * 2**20),
+    )(*operands)
 
 
 def body(
     tokens, cotangent, prefix, ln1_gain, ln1_bias, w_qkv, b_qkv, w_out, b_out,
     ln2_gain, ln2_bias, w_up, b_up, w_down, b_down,
 ):
-    vec = pack_vectors((ln1_gain, ln1_bias, b_qkv, b_out, ln2_gain, ln2_bias, b_up, b_down))
-    block_out, grad_tokens, gq, go, gu, gd, gvec = layer_call(
-        prefix, tokens, cotangent, vec, w_qkv, w_out, w_up, w_down)
-    rows = [gvec[i, :wide] for i, wide in enumerate(WIDTHS)]
+    results = layer_call(
+        prefix, tokens, cotangent, ln1_gain, ln1_bias, b_qkv, b_out, ln2_gain, ln2_bias, b_up, b_down,
+        w_qkv, w_out, w_up, w_down)
+    block_out, grad_tokens, gq, go, gu, gd, *rows = finish_call(*results)
     return (
         block_out, grad_tokens, rows[0], rows[1], gq, rows[2], go, rows[3], rows[4], rows[5], gu, rows[6], gd, rows[7],
     )

time: 238 us -> 211 us (0.89)
  Pallas kernels: 224 us -> 202 us
  local copies, waits for them, and re-layouts: 12.9 us -> 6.67 us
    pallas_call x1, Pallas kernels: 224 us -> 201 us  [layer_call(): pl.pallas_call(layer_kernel, out_shape=results + held, in_specs=[SM] + [A...]
    squeeze x3 -> x0, local copies, waits for them, and re-layouts: 3.88 us -> none  [body(): rows = [gvec[i, :wide] for i, wide in enumerate(WIDTHS)]]
    another operation x5 -> x0, local copies, waits for them, and re-layouts: 3.31 us -> none  [pack_vectors(): return jnp.stack([jnp.pad(v, (0, 128 - v.shape[0])) for v in vectors])]
    unnamed x16 -> x14, local copies, waits for them, and re-layouts: 5.76 us -> 6.67 us
where the time goes in v3:
time: 211 us; the launch traced here: 210 us
  Pallas kernels  202 us (96%)
  local copies, waits for them, and re-layouts  6.67 us (3%)
    pallas_call x1, Pallas kernels, layer_call(): pl.pallas_call(layer_kernel, out_shape=results + held, in_specs=[SM] + [A...  201 us
    unnamed x14, local copies, waits for them, and re-layouts  6.67 us

profile of v3, /device:TPU:0, one launch (start us, length us, event | category | flops | bytes accessed | tf_op | source)
XLA Modules:
  0.0 210.0 jit_solution(16361467559172811726)
XLA Ops:
  0.7 200.9 %shard_map.254 = (bf16[2,256,768]{2,1,0:T(8,128)(2,1)}, bf16[2,256,768]{2,1,0:T(8,128)(2,1)}, f32[24,2304]{1,0:T(8,128)}, f32[24,768]{1,0:T(8,128)}, f32[24,3072...) custom-call(s32[2]{0:T(128)} %prefix.1, ...), custom_call_target="tpu_custom_call" | custom-call | tf_op jit(solution)/shard_map/pallas_call | solution.py:917
  201.5 0.0 copy-start
  201.5 1.1 copy-done
  202.7 0.0 copy-start.1
  202.7 1.1 copy-done.1
  203.8 0.0 copy-start.2
  203.8 1.0 copy-done.2
  204.8 0.0 copy-start.3
  204.8 1.0 copy-done.3
  205.7 0.0 copy-start.4
  205.7 0.9 copy-done.4
  206.7 0.0 copy-start.5
  206.7 0.9 copy-done.5
  207.5 0.0 copy-start.6
  207.5 0.7 copy-done.6
  208.2 1.6 shard_map.255
Async XLA Ops:
  201.5 1.1 copy-start
  202.7 1.1 copy-start.1
  203.8 1.0 copy-start.2
  204.8 1.0 copy-start.3
  205.7 0.9 copy-start.4
  206.7 0.9 copy-start.5
  207.5 0.7 copy-start.6

commit v4 on v3

--- a/solution.py
+++ b/solution.py
@@ -26,7 +26,7 @@
 LAST = (((1,), (1,)), ((), ()))
 FIRST = (((0,), (0,)), ((), ()))
 ALL = slice(None)
-REMOTES = 128
+REMOTES = 160
 LOCALS = 64
 
 
@@ -141,7 +141,7 @@
 
 
 class Gather:
-    def __init__(self, links, own, other, mine, theirs, cut, full=None):
+    def __init__(self, links, own, other, mine, theirs, cut, whole=True):
         k = links
         rows = own.shape[0]
         at = pl.ds(pl.multiple_of(k.c * rows, 8), rows)
@@ -154,7 +154,7 @@
                    k.remote(mine.at[:, x, y, :, b], mine.at[:, x, y, :, b], k.py)]
         self.c3 = [k.remote(mine.at[:, :, y, :, a], mine.at[:, :, y, :, a], k.py),
                    k.remote(mine.at[:, x, :, :, b], mine.at[:, x, :, :, b], k.px)]
-        self.c4 = [] if full is None else [k.remote(full.at[k.c], full.at[k.c], k.pc)]
+        self.c4 = [k.remote(mine, mine, k.pc)] if whole else []
 
     def s0(self):
         start(self.c0)
@@ -181,17 +181,17 @@
 
 
 class Scatter:
-    def __init__(self, links, grad, r0, r1a, r1b, r2a, r2b, r3, tot, fin, put, cut, base=None, whole=True):
+    def __init__(self, links, grad, prefix, other, r0, r1a, r1b, r2a, r2b, r3, tot, fin, put, cut, base=None):
         k = links
-        self.k, self.grad, self.whole, self.put = k, grad, whole, put
+        self.k, self.grad, self.prefix, self.put = k, grad, prefix, put
         self.r0, self.r1a, self.r1b, self.r2a, self.r2b, self.r3, self.tot, self.fin = r0, r1a, r1b, r2a, r2b, r3, tot, fin
-        self.mine = grad.at[k.c] if whole else grad
+        self.whole = other is not None
+        mine = self.mine = grad.at[prefix] if prefix else grad
         self.a = (ALL, slice(0, cut))
         self.b = (ALL, slice(cut, None))
         x, y, x2, y2 = k.x, k.y, k.x2, k.y2
         at = iter([None] * 10 if base is None else base)
-        mine = self.mine
-        self.c0 = [k.remote(grad.at[k.c2], r0, k.pc, next(at))] if whole else []
+        self.c0 = [k.remote(grad.at[other], r0, k.pc, next(at))] if self.whole else []
         self.c1 = [k.remote(mine.at[(ALL, ALL, y2) + self.a], r1a, k.py, next(at)),
                    k.remote(mine.at[(ALL, x2, ALL) + self.b], r1b, k.px, next(at))]
         self.c2 = [k.remote(mine.at[(ALL, x2, y) + self.a], r2a, k.px, next(at)),
@@ -200,7 +200,7 @@
         self.c4 = [k.remote(tot.at[k.c2], fin, k.pc, next(at))]
 
     def at(self, place):
-        return ((self.k.c,) if self.whole else ()) + place
+        return self.prefix + place
 
     def s0(self):
         start(self.c0)
@@ -263,6 +263,11 @@
             copy.wait_send()
 
 
+def masked(size, seen, low):
+    last = jnp.where(seen, size[low:], NEG)
+    return last if low == 0 else jnp.concatenate([size[:low], last], axis=0)
+
+
 def gelu_parts(value):
     rate = 0.7978845608028654
     bent = jnp.tanh(rate * (value + 0.044715 * (value * value * value)))
@@ -288,7 +293,7 @@
     wq, wo, wu, wd, gv, k_qs, k_qst, k_k, k_v, k_att, k_n1t,
     vec_s, wq_p, gvm, tok_all, vrows, wom, al_send, al, cotm, ga_send, ga_all, fa, fb, fc, fr, lt,
     gd, gu, go, gq,
-    r0d, r0u, r0o, r1ad, r1bd, r1au, r1bu, r1ao, r1bo, r2ad, r2bd, r2au, r2bu, r2ao, r2bo, r3d, r3u, r3o,
+    r0d, r0u, r0o, r1ad, r1bd, r1au, r1bu, r1av, r1bv, r1ao, r1bo, r2ad, r2bd, r2au, r2bu, r2av, r2bv, r2ao, r2bo, r3d, r3u, r3o,
     td, tu, to, fd, fu, fo,
     q1a, q1b, q2a, q2b, q3, tq, fq,
     vs, vbq, vup, vtab, vr0, vr1, vr2, vr3,
@@ -308,40 +313,41 @@
             for kind in range(3):
                 first = kind * D + core * THIRD + u * 128
                 wq_p[core, u, :, kind * 128 : (kind + 1) * 128] = wq_s[:, first : first + 128]
-    cuts = (128, 256, 128)
-    gather_q = [Gather(k, wq_p.at[c, u], wq_p.at[c2, u], wq.at[u], wq.at[u], cuts[u]) for u in range(3)]
+    gather_q = [Gather(k, wq_p.at[c, u], wq_p.at[c2, u], wq.at[u], wq.at[u], 128, False) for u in range(3)]
 
     def halves(shard, full, cut):
         half = full.shape[-1]
-        return Gather(k, shard.at[:, lanes(c * half, half)], shard.at[:, lanes(c2 * half, half)], full.at[c], full.at[c2],
-                      cut, full)
-
-    gather_o = halves(wo_s, wo, 256)
-    gather_u = halves(wu_s, wu, 768)
+        return Gather(k, shard.at[:, lanes(c * half, half)], shard.at[:, lanes(c2 * half, half)], full.at[c], full.at[c2], cut)
+
+    gather_o = halves(wo_s, wo, 128)
     gather_d = halves(wd_s, wd, 128)
+    gather_u = [Gather(k, wu_s.at[:, lanes(c * 1536 + part * D, D)], wu_s.at[:, lanes(c2 * 1536 + part * D, D)],
+                       wu.at[c, part], wu.at[c2, part], 256 - 128 * part) for part in range(2)]
     own_vec = k.local(vec_s, gv.at[z, x, y, c])
     own_tok = k.local(tok.at[y], tok_all.at[y, c])
     own_cot = k.local(cot.at[y], cotm.at[y])
     own_vec.start()
     start(gather_q[0].own)
     own_tok.start()
-    start(gather_q[1].own + gather_q[2].own + gather_o.own + gather_u.own + gather_d.own)
+    others = [gather_q[1], gather_q[2], gather_o] + gather_u + [gather_d]
+    for gather in others:
+        start(gather.own)
     own_cot.start()
     k.greeted()
 
     vec_c = k.remote(vec_s, gv.at[z, x, y, c], k.pc)
     tok_y = k.remote(tok.at[y2], tok_all.at[y, c], k.py)
     cot_y = k.remote(cot.at[y2], cotm.at[y], k.py)
+    vec_c.start()
     gather_q[0].s0()
-    vec_c.start()
     tok_y.start()
-    for gather in (gather_q[1], gather_q[2], gather_o, gather_u, gather_d):
+    for gather in others:
         gather.s0()
-    gather_q[0].s1()
     own_vec.wait()
     vec_c.wait_recv()
     vec_z = [k.remote(gv.at[z, x, y], gv.at[z, x, y], dev) for dev in k.pz]
     start(vec_z)
+    gather_q[0].s1()
     gather_q[1].s1()
     own_tok.wait()
     arrive(vec_z)
@@ -349,18 +355,17 @@
     vec_x.start()
     gather_q[0].s2()
     gather_q[2].s1()
-    tok_y.wait_recv()
-    tok_c = k.remote(tok_all.at[:, c], tok_all.at[:, c], k.pc)
-    tok_c.start()
-    cot_y.start()
     vec_x.wait_recv()
     vec_y = k.remote(gv.at[:, :, y], gv.at[:, :, y], k.py)
     vec_y.start()
     gather_q[1].s2()
     gather_o.s1()
     gather_q[0].s3()
+    tok_y.wait_recv()
+    tok_c = k.remote(tok_all.at[:, c], tok_all.at[:, c], k.pc)
+    tok_c.start()
     gather_q[2].s2()
-    gather_u.s1()
+    gather_u[0].s1()
     vec_y.wait_recv()
     table = k.local(gv, gvm)
     table.start()
@@ -368,6 +373,7 @@
     table = gvm[...].reshape(256, 128).astype(BF)
     for index, wide in enumerate(WIDTHS):
         vrows[index : index + 1, 0 : 32 * wide] = spread_row(table, index, wide)
+    gather_q[1].s3()
     tok_c.wait_recv()
 
     mine_cols = lanes(c * THIRD, THIRD)
@@ -394,7 +400,6 @@
         keep = [k.local(n1t, k_n1t), k.local(qs, k_qs), k.local(qst, k_qst), k.local(keys_ref, k_k),
                 k.local(values_ref, k_v), k.local(att, k_att)]
         keep[0].start()
-        gather_q[1].s3()
         load_q = [k.local(wq3.at[u], wqm.at[u]) for u in range(3)]
         load_o = k.local(wo.reshape(2, D, THIRD), wom)
 
@@ -404,9 +409,10 @@
             load_q[u].wait()
 
         slots = {
-            (0, 3): [gather_q[2].s3, gather_o.s2], (0, 2): [gather_u.s2, gather_d.s1], (0, 1): [gather_o.s3], (0, 0): [],
-            (1, 3): [], (1, 2): [gather_u.s3], (1, 1): [gather_o.s4, gather_d.s2], (1, 0): [],
-            (2, 3): [], (2, 2): [gather_o.done, load_o.start], (2, 1): [], (2, 0): [],
+            (0, 3): [gather_q[2].s3, gather_o.s2, gather_u[1].s1], (0, 2): [gather_u[0].s2],
+            (0, 1): [gather_o.s3, gather_d.s1], (0, 0): [gather_u[1].s2],
+            (1, 3): [gather_u[0].s3], (1, 2): [gather_o.s4], (1, 1): [gather_d.s2], (1, 0): [gather_u[1].s3],
+            (2, 3): [gather_o.done, load_o.start, gather_u[0].s4], (2, 2): [cot_y.start], (2, 1): [gather_d.s3], (2, 0): [],
         }
 
         def unit(u, carry):
@@ -417,7 +423,7 @@
                     head(which)
 
             def project(b, inner):
-                rows = rows_at(b * 256, 256)
+                rows = rows_at(b * 512, 512)
                 value = jnp.dot(n1[rows, :], wqm[u], preferred_element_type=F32)
                 parts = []
                 for kind in range(3):
@@ -431,7 +437,7 @@
                 vt[cols, rows] = parts[2].astype(F32).T.astype(BF)
                 return inner
 
-            lax.fori_loop(0, 4, project, 0)
+            lax.fori_loop(0, 2, project, 0)
             for block in (3, 2, 1, 0):
                 attend(u, block)
                 for which in range(3):
@@ -449,11 +455,13 @@
             keys = keys_ref[0:rows, cols]
             queries = qst[cols, qcols]
             qpos = block * 256 + lax.broadcasted_iota(jnp.int32, (1, 256), 1)
-            seen = lax.broadcasted_iota(jnp.int32, (rows, 256), 0) <= jnp.maximum(qpos, limit)
+            low = block * 256
+            seen = low + lax.broadcasted_iota(jnp.int32, (rows - low, 256), 0) <= jnp.maximum(qpos, limit)
             for half in range(2):
                 chosen = jnp.where(sub // 64 == half, queries, jnp.zeros_like(queries))
                 scores = jnp.dot(keys, chosen, preferred_element_type=F32)
-                size = jnp.where(seen, jnp.abs(scores), NEG)
+                size = jnp.abs(scores)
+                size = masked(size, seen, low)
                 top = jnp.max(size, axis=0, keepdims=True)
                 exponent = jnp.exp(size - top)
                 total = jnp.sum(exponent, axis=0, keepdims=True)
@@ -467,8 +475,6 @@
         al_own.start()
         al_c.start()
         start(keep[1:])
-        gather_u.s4()
-        gather_d.s3()
         load_o.wait()
         al_own.wait()
         al_c.wait_recv()
@@ -484,9 +490,17 @@
             out[:, lanes(core * half, half)] = value
         return put
 
-    down = Scatter(k, gd, r0d, r1ad, r1bd, r2ad, r2bd, r3d, td, fd, put_to(out_d, THIRD), 128)
-    up = Scatter(k, gu, r0u, r1au, r1bu, r2au, r2bu, r3u, tu, fu, put_to(out_u, 1536), 768)
-    outp = Scatter(k, go, r0o, r1ao, r1bo, r2ao, r2bo, r3o, to, fo, put_to(out_o, THIRD), 256)
+    down = Scatter(k, gd, (c,), c2, r0d, r1ad, r1bd, r2ad, r2bd, r3d, td, fd, put_to(out_d, THIRD), 128)
+
+    def put_up(part):
+        def put(value, core):
+            out_u[:, lanes(core * 1536 + part * D, D)] = value
+        return put
+
+    up = [Scatter(k, gu, (c, part), (c2, part), r0u.at[part], (r1au, r1av)[part], (r1bu, r1bv)[part], (r2au, r2av)[part],
+                  (r2bu, r2bv)[part], r3u.at[part], tu.at[part], fu.at[part], put_up(part), 256 - 128 * part)
+          for part in range(2)]
+    outp = Scatter(k, go, (c,), c2, r0o, r1ao, r1bo, r2ao, r2bo, r3o, to, fo, put_to(out_o, THIRD), 128)
 
     def feed(wbuf, wdb, hid, slope, n2, n2t, alt, gpc):
         b_out, gain, shift = vrows[3:4, 0:D], vrows[4:5, 0:D], vrows[5:6, 0:D]
@@ -507,7 +521,7 @@
         own_cot.wait()
         cot_y.wait_recv()
 
-        wu2 = wu.reshape(2, D, 1536)
+        wu2 = wu.reshape(2, 2, D, D)
         wd2 = wd.reshape(2, FF, THIRD)
 
         def chunk(j, first, second):
@@ -516,7 +530,7 @@
 
         def up_load(j, slot, order):
             h, part = chunk(j, *order)
-            return k.local(wu2.at[h, :, part * D : (part + 1) * D], wbuf.at[slot])
+            return k.local(wu2.at[h, part], wbuf.at[slot])
 
         def down_load(j, slot, order):
             h, part = chunk(j, *order)
@@ -525,32 +539,36 @@
         forth = (c, c2)
         loads = [up_load(j, j % 2, forth) for j in range(4)]
         loads[0].start()
+        gather_u[1].s4()
         for j in range(4):
+            loads[j].wait()
+            if j == 0:
+                loads[1].start()
             if j == 1:
-                gather_u.done()
-            if j < 3:
-                loads[j + 1].start()
-            loads[j].wait()
+                gather_u[0].done()
+                loads[2].start()
+            if j == 2:
+                gather_u[1].done()
+                loads[3].start()
             h, part = chunk(j, *forth)
-            cols = lanes(h * 1536 + part * D, D)
-
-            def ahead(yy, carry):
-                rows = rows_at(yy * 256, 256)
-                value = jnp.dot(n2[rows, :], wbuf[j % 2], preferred_element_type=F32) + vrows[6:7, cols]
+
+            def ahead(side, carry):
+                there = lanes(side * THIRD, THIRD)
+                cols = lanes(h * 1536 + part * D + side * THIRD, THIRD)
+                value = jnp.dot(n2[...], wbuf[j % 2, :, there], preferred_element_type=F32) + vrows[6:7, cols]
                 result, bend = gelu_parts(value)
-                hid[rows, cols] = result.astype(BF)
-                slope[rows, cols] = bend
+                hid[:, cols] = result.astype(BF)
+                slope[:, cols] = bend
                 return carry
 
             lax.fori_loop(0, 2, ahead, 0)
+
         vs[7:8, :] = jnp.sum(cotm[0].astype(F32), axis=0, keepdims=True) + jnp.sum(
             cotm[1].astype(F32), axis=0, keepdims=True)
 
         def down_grad(i, carry):
-            total = jnp.zeros((THIRD, D), F32)
-            for yy in range(2):
-                total += lax.dot_general(hid[yy * 256 : (yy + 1) * 256, lanes(i * THIRD, THIRD)], cotm[yy], FIRST,
-                                         preferred_element_type=F32)
+            total = lax.dot_general(hid[:, lanes(i * THIRD, THIRD)], cotm[...].reshape(512, D), FIRST,
+                                    preferred_element_type=F32)
             zz, xx = i // 2, lax.rem(i, 2)
             for yy in range(2):
                 for h in range(2):
@@ -578,38 +596,48 @@
             again[j].wait()
             lower[j].wait()
             h, part = chunk(j, *back)
-            cols = lanes(h * 1536 + part * D, D)
-
-            def behind(yy, carry):
-                rows = rows_at(yy * 256, 256)
-                units = hid[rows, cols]
+            first = h * 1536 + part * D
+
+            def behind(side, carry):
+                there = lanes(side * THIRD, THIRD)
+                cols = lanes(first + side * THIRD, THIRD)
+                units = hid[:, lanes(first, D)]
+                fc[:, :, there] += jnp.dot(units, wdb[slot, side], preferred_element_type=F32).reshape(2, 256, THIRD)
                 grad = None
-                for side in range(2):
-                    there = slice(side * THIRD, (side + 1) * THIRD)
-                    fc[yy, :, there] += jnp.dot(units, wdb[slot, side], preferred_element_type=F32)
-                    term = lax.dot_general(cotm[yy, :, there], wdb[slot, side], LAST, preferred_element_type=F32)
+                for other in range(2):
+                    term = lax.dot_general(
+                        cotm[:, :, other * THIRD : (other + 1) * THIRD].reshape(512, THIRD), wdb[slot, other, there, :],
+                        LAST, preferred_element_type=F32)
                     grad = term if grad is None else grad + term
-                grad = (grad * slope[rows, cols]).astype(BF)
-                gpc[rows, :] = grad
+                grad = (grad * slope[:, cols]).astype(BF)
+                gpc[:, there] = grad
                 vup[0:1, cols] += jnp.sum(grad.astype(F32), axis=0, keepdims=True)
-                fb[yy] += lax.dot_general(grad, wbuf[slot], LAST, preferred_element_type=F32)
                 return carry
 
             lax.fori_loop(0, 2, behind, 0)
 
+            def normed_grad(side, carry):
+                there = lanes(side * THIRD, THIRD)
+                term = lax.dot_general(gpc[...], wbuf[slot, there, :], LAST, preferred_element_type=F32)
+                fb[:, :, there] += term.reshape(2, 256, THIRD)
+                return carry
+
+            lax.fori_loop(0, 2, normed_grad, 0)
+
             def up_grad(zz, carry):
-                total = jnp.dot(n2t[rows_at(zz * 192, 192, 64), :], gpc[...], preferred_element_type=F32)
-                for i in range(4):
-                    gu[h, zz, i // 2, i % 2, :, part * D : (part + 1) * D] = total[i * 48 : (i + 1) * 48].astype(BF)
+                total = jnp.dot(n2t[rows_at(zz * THIRD, THIRD, 128), :], gpc[...], preferred_element_type=F32)
+                for i in range(8):
+                    gu[h, part, zz * 2 + i // 4, i // 2 % 2, i % 2] = total[i * 48 : (i + 1) * 48].astype(BF)
                 return carry
 
-            lax.fori_loop(0, 4, up_grad, 0)
-            if j == 1:
-                up.s0()
+            lax.fori_loop(0, 2, up_grad, 0)
+            if j < 2:
+                up[j].s0()
             if j == 2:
+                up[0].s1()
                 down.s2()
         bo[...] = (fa[...] + fc[...] + vrows[7:8, 0:D].reshape(1, 1, D)).astype(BF)
-        up.s1()
+        up[1].s1()
 
     ga_c = k.remote(ga_send.at[:, :, peer_cols], ga_all.at[:, c], k.pc)
     def turn(alt, gpc):
@@ -640,13 +668,13 @@
         ga_c.start()
 
         def out_grad(zz, carry):
-            total = jnp.dot(alt[rows_at(zz * 192, 192, 64), :], gpc[...], preferred_element_type=F32)
-            for i in range(4):
+            total = jnp.dot(alt[rows_at(zz * THIRD, THIRD, 128), :], gpc[...], preferred_element_type=F32)
+            for i in range(8):
                 for h in range(2):
-                    go[h, zz, i // 2, i % 2] = total[i * 48 : (i + 1) * 48, h * THIRD : (h + 1) * THIRD].astype(BF)
+                    go[h, zz * 2 + i // 4, i // 2 % 2, i % 2] = total[i * 48 : (i + 1) * 48, h * THIRD : (h + 1) * THIRD].astype(BF)
             return carry
 
-        lax.fori_loop(0, 4, out_grad, 0)
+        lax.fori_loop(0, 2, out_grad, 0)
         outp.s0()
 
     def put_q(u):
@@ -658,8 +686,8 @@
     bases = [k.fresh(3) for _ in range(8)]
 
     def query_scatter(u):
-        return Scatter(k, gq.at[u], None, q1a.at[u], q1b.at[u], q2a.at[u], q2b.at[u], q3.at[u], tq.at[u], fq.at[u],
-                       put_q(u), 128, base=[b + u for b in bases], whole=False)
+        return Scatter(k, gq.at[u], (), None, None, q1a.at[u], q1b.at[u], q2a.at[u], q2b.at[u], q3.at[u], tq.at[u], fq.at[u],
+                       put_q(u), 128, base=[b + u for b in bases])
 
     queue = [query_scatter(u) for u in range(3)]
     bo_own = k.local(bo.at[y], out_bo.at[y])
@@ -681,9 +709,9 @@
         lane = lax.broadcasted_iota(jnp.int32, (256, 128), 1)
         vbq[...] = jnp.zeros_like(vbq)
         slots = {
-            (0, 3): [outp.s1, down.s3], (0, 2): [], (0, 1): [up.s2], (0, 0): [send_out],
-            (1, 3): [outp.s2], (1, 2): [down.s4], (1, 1): [up.s3], (1, 0): [outp.s3, down.s5],
-            (2, 3): [queue[0].s2], (2, 2): [], (2, 1): [queue[0].s3], (2, 0): [outp.s4],
+            (0, 3): [outp.s1, down.s3], (0, 2): [], (0, 1): [up[0].s2], (0, 0): [send_out, up[1].s2],
+            (1, 3): [outp.s2], (1, 2): [down.s4], (1, 1): [up[0].s3], (1, 0): [up[1].s3, down.s5],
+            (2, 3): [queue[0].s2], (2, 2): [outp.s3], (2, 1): [queue[0].s3], (2, 0): [up[0].s4],
         }
 
         def unit(u, carry):
@@ -704,7 +732,8 @@
                 queries = qs[qrange, cols]
                 grads = ga_all[block // 2, block % 2, :, cols]
                 qpos = block * 256 + lax.broadcasted_iota(jnp.int32, (1, 256), 1)
-                seen = lax.broadcasted_iota(jnp.int32, (rows, 256), 0) <= jnp.maximum(qpos, limit)
+                low = block * 256
+                seen = low + lax.broadcasted_iota(jnp.int32, (rows - low, 256), 0) <= jnp.maximum(qpos, limit)
                 prod = grads_t.astype(F32) * att[cols, qrange]
                 dqs, dks, dvs = [], None, None
                 for half in range(2):
@@ -716,7 +745,7 @@
                     zero = jnp.zeros((), BF)
                     scores = jnp.dot(keys, jnp.where(in_sub, queries_t, zero), preferred_element_type=F32)
                     pull = jnp.dot(values, jnp.where(in_sub, grads_t, zero), preferred_element_type=F32)
-                    share = jnp.exp(jnp.where(seen, jnp.abs(scores) - total, NEG))
+                    share = jnp.exp(masked(jnp.abs(scores) - total, seen, low))
                     signed = jnp.where(scores > 0, share, jnp.where(scores < 0, -share, 0.0))
                     grad_scores = (share * pull - signed * delta).astype(BF)
                     signed = signed.astype(BF)
@@ -742,12 +771,12 @@
                 vbq[0:1, lanes(kind * D + c * THIRD + u * 128)] = sums[:, part]
 
             def weights(zz, inner):
-                block = jnp.dot(n1t[rows_at(zz * 192, 192, 64), :], gpu[...], preferred_element_type=F32)
-                for i in range(4):
-                    gq[u, zz, i // 2, i % 2] = block[i * 48 : (i + 1) * 48].astype(BF)
+                block = jnp.dot(n1t[rows_at(zz * THIRD, THIRD, 128), :], gpu[...], preferred_element_type=F32)
+                for i in range(8):
+                    gq[u, zz * 2 + i // 4, i // 2 % 2, i % 2] = block[i * 48 : (i + 1) * 48].astype(BF)
                 return inner
 
-            lax.fori_loop(0, 4, weights, 0)
+            lax.fori_loop(0, 2, weights, 0)
             for which in range(3):
                 @pl.when(u == which)
                 def _():
@@ -789,7 +818,6 @@
 
     pl.run_scoped(both, vmem((D, 512), BF), vmem((512, D), BF))
 
-    queue[1].s2()
     gain = vrows[0:1, 0:D]
     vs[0:2, :] = jnp.zeros((2, D), F32)
 
@@ -818,7 +846,6 @@
         return rows_at((((zz * 2 + xx) * 2 + yy) * 2 + c) * 8, 8, 8)
 
     v0.start()
-    queue[2].s2()
     part_c.wait_recv()
 
     def last_back(yy):
@@ -841,9 +868,8 @@
 
     lax.fori_loop(0, 16, add_core, 0)
     v1.start()
-    queue[1].s3()
-    queue[2].s3()
-    up.s4()
+    queue[1].s2()
+    queue[2].s2()
     queue[0].s4()
     v1.wait_recv()
 
@@ -853,8 +879,8 @@
 
     lax.fori_loop(0, 8, add_y, 0)
     v2.start()
-    outp.s5()
-    queue[1].s4()
+    queue[1].s3()
+    queue[2].s3()
     v2.wait_recv()
 
     def add_x(zz, carry):
@@ -863,11 +889,12 @@
 
     lax.fori_loop(0, 4, add_x, 0)
     start(v3)
+    up[1].s4()
+    outp.s4()
+    queue[1].s4()
     queue[2].s4()
-    up.s5()
-    queue[0].s5()
-    queue[1].s5()
-    queue[2].s5()
+    for scatter in (up[0], up[1], outp, queue[0], queue[1], queue[2]):
+        scatter.s5()
     arrive(v3)
     out_vec[...] = vtab[tile(z, x, y), :] + vr3[0] + vr3[1] + vr3[2]
     landed([gt_own, bo_own])
@@ -876,6 +903,7 @@
         copy.wait_send()
     for scatter in queue:
         scatter.gone()
+    assert k.remotes <= REMOTES and k.locals <= LOCALS
 
 
 def layer_call(*operands):
@@ -887,7 +915,7 @@
         sds((96, D), F32), sds((8, 128), F32),
     )
     held = (
-        sds((3, 4, 2, 2, 48, 384), BF), sds((2, 4, 2, 2, 48, 384), BF), sds((2, 4, 2, 2, 48, 1536), BF),
+        sds((3, 4, 2, 2, 48, 384), BF), sds((2, 4, 2, 2, 48, 384), BF), sds((2, 2, 4, 2, 2, 48, 768), BF),
         sds((2, 4, 2, 2, 192, 384), BF), sds((4, 2, 2, 2, 8, 128), F32), sds((1024, THIRD), BF), sds((THIRD, 1024), BF),
         sds((1024, THIRD), BF), sds((1024, THIRD), BF), sds((THIRD, 1024), F32), sds((D, 1024), BF),
     )
@@ -897,16 +925,16 @@
         vmem((2, 256, D), BF), vmem((2, 2, 256, THIRD), BF), vmem((2, 256, D), F32), vmem((2, 256, D), F32),
         vmem((2, 256, D), F32), vmem((2, 256, D), F32), vmem((8, 1024), F32),
     ]
-    kinds = ((192, 384, 128), (48, 1536, 768), (48, 384, 256))
-    scratch += [vmem((2, 4, 2, 2, r, n), BF) for r, n, _ in kinds] + [vmem((3, 4, 2, 2, 48, 384), BF)]
-    scratch += [vmem((4, 2, 2, r, n), BF) for r, n, _ in kinds]
-    for r, n, cut in kinds:
-        scratch += [vmem((4, 2, r, cut), BF), vmem((4, 2, r, n - cut), BF)]
-    for r, n, cut in kinds:
-        scratch += [vmem((4, r, cut), BF), vmem((4, r, n - cut), BF)]
-    scratch += [vmem((3, r, n), BF) for r, n, _ in kinds]
-    scratch += [vmem((2, r // 2, n), F32) for r, n, _ in kinds]
-    scratch += [vmem((r // 2, n), F32) for r, n, _ in kinds]
+    kinds = (((), 192, 384, (128,)), ((2,), 48, 768, (256, 128)), ((), 48, 384, (128,)))
+    scratch += [vmem((2,) + p + (4, 2, 2, r, n), BF) for p, r, n, _ in kinds] + [vmem((3, 4, 2, 2, 48, 384), BF)]
+    scratch += [vmem(p + (4, 2, 2, r, n), BF) for p, r, n, _ in kinds]
+    for lead in ((4, 2), (4,)):
+        for _, r, n, cuts in kinds:
+            for cut in cuts:
+                scratch += [vmem(lead + (r, cut), BF), vmem(lead + (r, n - cut), BF)]
+    scratch += [vmem(p + (3, r, n), BF) for p, r, n, _ in kinds]
+    scratch += [vmem(p + (2, r // 2, n), F32) for p, r, n, _ in kinds]
+    scratch += [vmem(p + (r // 2, n), F32) for p, r, n, _ in kinds]
     scratch += [
         vmem((3, 4, 2, 48, 128), BF), vmem((3, 4, 2, 48, 256), BF), vmem((3, 4, 48, 128), BF), vmem((3, 4, 48, 256), BF),
         vmem((3, 3, 48, 384), BF), vmem((3, 2, 24, 384), F32), vmem((3, 24, 384), F32),
@@ -925,19 +953,23 @@
     )(*operands)[: len(results)]
 
 
-def finish_kernel(bo, gt, gq, go, gu, gd, gvec, *out):
-    for source, result in zip((bo, gt, gq, go, gu, gd), out[:6]):
-        result[...] = source[...]
+def finish_kernel(*refs):
+    sources, results, (table, sems) = refs[:7], refs[7:21], refs[21:]
+    copies = [pltpu.make_async_copy(source, result, sems.at[i])
+              for i, (source, result) in enumerate(zip(sources, results[:6] + (table,)))]
+    start(copies)
+    landed(copies)
     for index, wide in enumerate(WIDTHS):
-        out[6 + index][...] = gvec[index, 0:wide]
+        results[6 + index][...] = table[index, 0:wide]
 
 
 def finish_call(*operands):
     sds = jax.ShapeDtypeStruct
     shapes = tuple(sds(o.shape, o.dtype) for o in operands[:6]) + tuple(sds((wide,), F32) for wide in WIDTHS)
     return pl.pallas_call(
-        finish_kernel, out_shape=shapes, in_specs=[VM] * 7, out_specs=(VM,) * 14,
-        compiler_params=pltpu.CompilerParams(vmem_limit_bytes=32 * 2**20),
+        finish_kernel, out_shape=shapes, in_specs=[ANY] * 7, out_specs=(VM,) * 14,
+        scratch_shapes=[pltpu.VMEM((8, 128), F32), pltpu.SemaphoreType.DMA((7,))],
+        compiler_params=pltpu.CompilerParams(vmem_limit_bytes=60 * 2**20),
     )(*operands)
 
 

time: 211 us -> 194 us (0.919)
  Pallas kernels: 202 us -> 193 us
  local copies, waits for them, and re-layouts: 6.67 us -> 0 us
    pallas_call x1, Pallas kernels: 201 us -> 189 us  [layer_call(): pl.pallas_call(layer_kernel, out_shape=results + held, in_specs=[SM] + [A...]
    unnamed x14 -> x0, local copies, waits for them, and re-layouts: 6.67 us -> none
where the time goes in v4:
time: 194 us; the launch traced here: 193 us
  Pallas kernels  193 us (99%)
    pallas_call x1, Pallas kernels, layer_call(): pl.pallas_call(layer_kernel, out_shape=results + held, in_specs=[SM] + [A...  189 us

profile of v4, /device:TPU:0, one launch (start us, length us, event | category | flops | bytes accessed | tf_op | source)
XLA Modules:
  0.0 193.3 jit_solution(8233390068234043305)
XLA Ops:
  0.7 189.4 %shard_map.254 = (bf16[2,256,768]{2,1,0:T(8,128)(2,1)}, bf16[2,256,768]{2,1,0:T(8,128)(2,1)}, f32[24,2304]{1,0:T(8,128)}, f32[24,768]{1,0:T(8,128)}, f32[24,3072...) custom-call(s32[2]{0:T(128)} %prefix.1, ...), custom_call_target="tpu_custom_call" | custom-call | tf_op jit(solution)/shard_map/pallas_call | solution.py:945
  190.0 3.1 %shard_map.255 = (bf16[2,256,768]{2,1,0:T(8,128)(2,1)}, bf16[2,256,768]{2,1,0:T(8,128)(2,1)}, f32[24,2304]{1,0:T(8,128)}, f32[24,768]{1,0:T(8,128)}, f32[24,3072...) custom-call(bf16[2,256,768]{2,1,0:T(8,128)(2,1)} %get-tuple-element., ...), custom_call_target="tpu_custom_call" | custom-call | tf_op jit(solution)/shard_map/pallas_call | solution.py:969

commit v5 on v4

--- a/solution.py
+++ b/solution.py
@@ -26,7 +26,7 @@
 LAST = (((1,), (1,)), ((), ()))
 FIRST = (((0,), (0,)), ((), ()))
 ALL = slice(None)
-REMOTES = 160
+REMOTES = 224
 LOCALS = 64
 
 
@@ -100,6 +100,31 @@
     return pl.ds(pl.multiple_of(first, step), count)
 
 
+class Cut:
+    def __init__(self, rows, columns, a, upto=None, upto_row=None):
+        first = slice(0, upto_row or rows)
+        end = upto or columns
+        self.rows, self.columns = rows, columns
+        self.a = (first, slice(0, a))
+        self.b = (first, slice(a, end))
+        self.ab = (first, slice(0, end))
+        self.f = None
+        self.axis = 0 if upto_row else 1
+        if upto:
+            self.f = (slice(0, rows), slice(upto, columns))
+        if upto_row:
+            self.f = (slice(upto_row, rows), slice(0, columns))
+
+    def shape(self, part):
+        return tuple(side.stop - side.start for side in part)
+
+
+CUTS = {
+    "down": Cut(192, 384, 128, upto_row=160), "up0": Cut(48, 768, 256, upto=640), "up1": Cut(48, 768, 128, upto=640),
+    "out": Cut(48, 384, 128), "q0": Cut(48, 384, 128), "q1": Cut(48, 384, 128), "q2": Cut(48, 384, 128),
+}
+
+
 class Links:
     def __init__(self, ssem, rsem, lsem):
         self.ssem, self.rsem, self.lsem = ssem, rsem, lsem
@@ -112,18 +137,13 @@
         self.zs = [lax.rem(z + d, 4) for d in (1, 2, 3)]
         self.pz = [device(zz, x, y, c) for zz in self.zs]
 
-    def fresh(self, count=1):
-        first = self.remotes
-        self.remotes += count
-        return first
-
-    def remote(self, src, dst, dev, at=None):
-        i = self.fresh() if at is None else at
+    def remote(self, src, dst, dev):
+        i = self.remotes
+        self.remotes += 1
         copy = pltpu.make_async_remote_copy(
             src_ref=src, dst_ref=dst, send_sem=self.ssem.at[i], recv_sem=self.rsem.at[i],
             device_id=dev, device_id_type=MESH)
-        if at is None:
-            self.sent.append(copy)
+        self.sent.append(copy)
         return copy
 
     def local(self, src, dst):
@@ -148,12 +168,18 @@
         z, x, y = k.z, k.x, k.y
         self.own = [k.local(own, mine.at[z, x, y, at])]
         self.c0 = [k.remote(other, theirs.at[z, x, y, at], k.pc)]
-        self.c1 = [k.remote(mine.at[z, x, y], mine.at[z, x, y], dev) for dev in k.pz]
-        a, b = slice(0, cut), slice(cut, None)
-        self.c2 = [k.remote(mine.at[:, x, y, :, a], mine.at[:, x, y, :, a], k.px),
-                   k.remote(mine.at[:, x, y, :, b], mine.at[:, x, y, :, b], k.py)]
-        self.c3 = [k.remote(mine.at[:, :, y, :, a], mine.at[:, :, y, :, a], k.py),
-                   k.remote(mine.at[:, x, :, :, b], mine.at[:, x, :, :, b], k.px)]
+        a, b, ab, f = cut.a, cut.b, cut.ab, cut.f
+
+        def send(place, dev):
+            return k.remote(mine.at[place], mine.at[place], dev)
+
+        self.c1 = [send((z, x, y) + ab, dev) for dev in k.pz]
+        self.c2 = [send((ALL, x, y) + a, k.px), send((ALL, x, y) + b, k.py)]
+        self.c3 = [send((ALL, ALL, y) + a, k.py), send((ALL, x, ALL) + b, k.px)]
+        if f:
+            self.c1.append(send((z, x, y) + f, k.py))
+            self.c2.append(send((z, x, ALL) + f, k.px))
+            self.c3 += [send((z, ALL, ALL) + f, dev) for dev in k.pz]
         self.c4 = [k.remote(mine, mine, k.pc)] if whole else []
 
     def s0(self):
@@ -181,23 +207,41 @@
 
 
 class Scatter:
-    def __init__(self, links, grad, prefix, other, r0, r1a, r1b, r2a, r2b, r3, tot, fin, put, cut, base=None):
+    @staticmethod
+    def buffers(cut, whole):
+        block = (cut.rows, cut.columns)
+        a, b, ab = cut.shape(cut.a), cut.shape(cut.b), cut.shape(cut.ab)
+        low = [(4, 2, 2) + block] if whole else []
+        low += [(4, 2) + a, (4, 2) + b, (4,) + a, (4,) + b, (3,) + ab]
+        if cut.f:
+            f = cut.shape(cut.f)
+            low += [(3, 2, 2) + f, (2,) + f, f]
+        half = (cut.rows // 2, cut.columns)
+        return [pltpu.VMEM(shape, BF) for shape in low] + [pltpu.VMEM((2,) + half, F32), pltpu.VMEM(half, F32)]
+
+    def __init__(self, links, grad, prefix, other, cut, work, put):
         k = links
-        self.k, self.grad, self.prefix, self.put = k, grad, prefix, put
-        self.r0, self.r1a, self.r1b, self.r2a, self.r2b, self.r3, self.tot, self.fin = r0, r1a, r1b, r2a, r2b, r3, tot, fin
+        self.k, self.grad, self.prefix, self.cut, self.put = k, grad, prefix, cut, put
         self.whole = other is not None
-        mine = self.mine = grad.at[prefix] if prefix else grad
-        self.a = (ALL, slice(0, cut))
-        self.b = (ALL, slice(cut, None))
-        x, y, x2, y2 = k.x, k.y, k.x2, k.y2
-        at = iter([None] * 10 if base is None else base)
-        self.c0 = [k.remote(grad.at[other], r0, k.pc, next(at))] if self.whole else []
-        self.c1 = [k.remote(mine.at[(ALL, ALL, y2) + self.a], r1a, k.py, next(at)),
-                   k.remote(mine.at[(ALL, x2, ALL) + self.b], r1b, k.px, next(at))]
-        self.c2 = [k.remote(mine.at[(ALL, x2, y) + self.a], r2a, k.px, next(at)),
-                   k.remote(mine.at[(ALL, x, y2) + self.b], r2b, k.py, next(at))]
-        self.c3 = [k.remote(mine.at[k.zs[d], x, y], r3.at[d], k.pz[d], next(at)) for d in range(3)]
-        self.c4 = [k.remote(tot.at[k.c2], fin, k.pc, next(at))]
+        mine = self.mine = grad.at[prefix]
+        if self.whole:
+            self.r0 = next(work)
+            self.c0 = [k.remote(grad.at[other], self.r0, k.pc)]
+        else:
+            self.c0 = []
+        self.r1a, self.r1b, self.r2a, self.r2b, self.r3 = [next(work) for _ in range(5)]
+        z, x, y, x2, y2 = k.z, k.x, k.y, k.x2, k.y2
+        a, b, ab, f = cut.a, cut.b, cut.ab, cut.f
+        self.c1 = [k.remote(mine.at[(ALL, ALL, y2) + a], self.r1a, k.py), k.remote(mine.at[(ALL, x2, ALL) + b], self.r1b, k.px)]
+        self.c2 = [k.remote(mine.at[(ALL, x2, y) + a], self.r2a, k.px), k.remote(mine.at[(ALL, x, y2) + b], self.r2b, k.py)]
+        self.c3 = [k.remote(mine.at[(k.zs[d], x, y) + ab], self.r3.at[d], k.pz[d]) for d in range(3)]
+        if f:
+            self.rf1, self.rf2, self.rf3 = [next(work) for _ in range(3)]
+            self.c1 += [k.remote(mine.at[(k.zs[d], ALL, ALL) + f], self.rf1.at[d], k.pz[d]) for d in range(3)]
+            self.c2.append(k.remote(mine.at[(z, x2, ALL) + f], self.rf2, k.px))
+            self.c3.append(k.remote(mine.at[(z, x, y2) + f], self.rf3, k.py))
+        self.tot, self.fin = next(work), next(work)
+        self.c4 = [k.remote(self.tot.at[k.c2], self.fin, k.pc)]
 
     def at(self, place):
         return self.prefix + place
@@ -219,35 +263,49 @@
 
     def s2(self):
         arrive(self.c1)
-        k = self.k
+        k, cut = self.k, self.cut
 
         def add(i, carry):
             zz, other = i // 2, lax.rem(i, 2)
-            add_into(self.grad, self.at((zz, other, k.y) + self.a), self.r1a[zz, other])
-            add_into(self.grad, self.at((zz, k.x, other) + self.b), self.r1b[zz, other])
+            add_into(self.grad, self.at((zz, other, k.y) + cut.a), self.r1a[zz, other])
+            add_into(self.grad, self.at((zz, k.x, other) + cut.b), self.r1b[zz, other])
             return carry
 
         lax.fori_loop(0, 8, add, 0)
+        if cut.f:
+            def add_f(i, carry):
+                xx, yy = i // 2, lax.rem(i, 2)
+                three = self.rf1[0, xx, yy].astype(F32) + self.rf1[1, xx, yy].astype(F32) + self.rf1[2, xx, yy].astype(F32)
+                add_into(self.grad, self.at((k.z, xx, yy) + cut.f), three)
+                return carry
+
+            lax.fori_loop(0, 4, add_f, 0)
         start(self.c2)
 
     def s3(self):
         arrive(self.c2)
-        k = self.k
+        k, cut = self.k, self.cut
 
         def add(zz, carry):
-            add_into(self.grad, self.at((zz, k.x, k.y) + self.a), self.r2a[zz])
-            add_into(self.grad, self.at((zz, k.x, k.y) + self.b), self.r2b[zz])
+            add_into(self.grad, self.at((zz, k.x, k.y) + cut.a), self.r2a[zz])
+            add_into(self.grad, self.at((zz, k.x, k.y) + cut.b), self.r2b[zz])
             return carry
 
         lax.fori_loop(0, 4, add, 0)
+        if cut.f:
+            for yy in range(2):
+                add_into(self.grad, self.at((k.z, k.x, yy) + cut.f), self.rf2[yy])
         start(self.c3)
 
     def s4(self):
         arrive(self.c3)
-        k = self.k
-        total = self.mine[k.z, k.x, k.y].astype(F32)
+        k, cut = self.k, self.cut
+        total = self.mine[(k.z, k.x, k.y) + cut.ab].astype(F32)
         for d in range(3):
             total = total + self.r3[d].astype(F32)
+        if cut.f:
+            rest = self.mine[(k.z, k.x, k.y) + cut.f].astype(F32) + self.rf3[...].astype(F32)
+            total = jnp.concatenate([total, rest], axis=cut.axis)
         rows = total.shape[0] // 2
         self.tot[0] = total[:rows]
         self.tot[1] = total[rows:]
@@ -258,9 +316,9 @@
         arrive(self.c4)
         self.put(self.fin[...], self.k.c2)
 
-    def gone(self):
-        for copy in self.c0 + self.c1 + self.c2 + self.c3 + self.c4:
-            copy.wait_send()
+
+def sign_of(value):
+    return jnp.clip(value * 1e38, -1.0, 1.0)
 
 
 def masked(size, seen, low):
@@ -290,17 +348,15 @@
 def layer_kernel(
     prefix, tok, cot, v0_s, v1_s, v2_s, v3_s, v4_s, v5_s, v6_s, v7_s, wq_s, wo_s, wu_s, wd_s,
     out_bo, out_gt, out_q, out_o, out_u, out_d, out_vec,
-    wq, wo, wu, wd, gv, k_qs, k_qst, k_k, k_v, k_att, k_n1t,
+    wq, wo, wu, wd, gv, k_qst, k_k, k_v, k_att, k_n1t,
     vec_s, wq_p, gvm, tok_all, vrows, wom, al_send, al, cotm, ga_send, ga_all, fa, fb, fc, fr, lt,
     gd, gu, go, gq,
-    r0d, r0u, r0o, r1ad, r1bd, r1au, r1bu, r1av, r1bv, r1ao, r1bo, r2ad, r2bd, r2au, r2bu, r2av, r2bv, r2ao, r2bo, r3d, r3u, r3o,
-    td, tu, to, fd, fu, fo,
-    q1a, q1b, q2a, q2b, q3, tq, fq,
     vs, vbq, vup, vtab, vr0, vr1, vr2, vr3,
-    ssem, rsem, lsem,
+    ssem, rsem, lsem, *work,
 ):
     k = Links(ssem, rsem, lsem)
     bo, gtb = al, cotm
+    work = iter(work)
     z, x, y, c, x2, y2, c2 = k.z, k.x, k.y, k.c, k.x2, k.y2, k.c2
     k.greet()
     vmem = pltpu.VMEM
@@ -313,16 +369,17 @@
             for kind in range(3):
                 first = kind * D + core * THIRD + u * 128
                 wq_p[core, u, :, kind * 128 : (kind + 1) * 128] = wq_s[:, first : first + 128]
-    gather_q = [Gather(k, wq_p.at[c, u], wq_p.at[c2, u], wq.at[u], wq.at[u], 128, False) for u in range(3)]
+    gather_q = [Gather(k, wq_p.at[c, u], wq_p.at[c2, u], wq.at[u], wq.at[u], CUTS[f"q{u}"], False)
+                for u in range(3)]
 
     def halves(shard, full, cut):
         half = full.shape[-1]
         return Gather(k, shard.at[:, lanes(c * half, half)], shard.at[:, lanes(c2 * half, half)], full.at[c], full.at[c2], cut)
 
-    gather_o = halves(wo_s, wo, 128)
-    gather_d = halves(wd_s, wd, 128)
+    gather_o = halves(wo_s, wo, CUTS["out"])
+    gather_d = halves(wd_s, wd, CUTS["down"])
     gather_u = [Gather(k, wu_s.at[:, lanes(c * 1536 + part * D, D)], wu_s.at[:, lanes(c2 * 1536 + part * D, D)],
-                       wu.at[c, part], wu.at[c2, part], 256 - 128 * part) for part in range(2)]
+                       wu.at[c, part], wu.at[c2, part], CUTS[f"up{part}"]) for part in range(2)]
     own_vec = k.local(vec_s, gv.at[z, x, y, c])
     own_tok = k.local(tok.at[y], tok_all.at[y, c])
     own_cot = k.local(cot.at[y], cotm.at[y])
@@ -384,7 +441,7 @@
     sub = lax.broadcasted_iota(jnp.int32, (128, 256), 0)
     wq3 = wq.reshape(3, D, THIRD)
 
-    def forward(n1, n1t, vt, qs, qst, keys_ref, values_ref, att, wqm):
+    def forward(n1, n1t, vt, qst, keys_ref, values_ref, att, wqm):
         gain = vrows[0:1, 0:D]
         shift = vrows[1:2, 0:D]
 
@@ -397,7 +454,7 @@
             return carry
 
         lax.fori_loop(0, 4, norm_block, 0)
-        keep = [k.local(n1t, k_n1t), k.local(qs, k_qs), k.local(qst, k_qst), k.local(keys_ref, k_k),
+        keep = [k.local(n1t, k_n1t), k.local(qst, k_qst), k.local(keys_ref, k_k),
                 k.local(values_ref, k_v), k.local(att, k_att)]
         keep[0].start()
         load_q = [k.local(wq3.at[u], wqm.at[u]) for u in range(3)]
@@ -430,7 +487,6 @@
                     bias = vrows[2:3, lanes(kind * D + c * THIRD + u * 128)]
                     parts.append((value[:, kind * 128 : (kind + 1) * 128] + bias).astype(BF))
                 queries = parts[0].astype(F32) * 0.125
-                qs[rows, cols] = queries.astype(BF)
                 qst[cols, rows] = queries.T.astype(BF)
                 keys_ref[rows, cols] = parts[1]
                 values_ref[rows, cols] = parts[2]
@@ -465,7 +521,7 @@
                 top = jnp.max(size, axis=0, keepdims=True)
                 exponent = jnp.exp(size - top)
                 total = jnp.sum(exponent, axis=0, keepdims=True)
-                weights = jnp.where(scores > 0, exponent, jnp.where(scores < 0, -exponent, 0.0)).astype(BF)
+                weights = (sign_of(scores) * exponent).astype(BF)
                 at = pl.ds(pl.multiple_of(u * 128 + half * 64, 64), 64)
                 att[at, qcols] = jnp.dot(vt[at, 0:rows], weights, preferred_element_type=F32) / total
                 lt[pl.ds(u * 2 + half, 1), qcols] = top + jnp.log(total)
@@ -481,7 +537,7 @@
         landed(keep)
 
     pl.run_scoped(
-        forward, vmem((1024, D), BF), vmem((D, 1024), BF), vmem((THIRD, 1024), BF), vmem((1024, THIRD), BF),
+        forward, vmem((1024, D), BF), vmem((D, 1024), BF), vmem((THIRD, 1024), BF),
         vmem((THIRD, 1024), BF), vmem((1024, THIRD), BF), vmem((1024, THIRD), BF), vmem((THIRD, 1024), F32),
         vmem((3, D, THIRD), BF))
 
@@ -490,17 +546,15 @@
             out[:, lanes(core * half, half)] = value
         return put
 
-    down = Scatter(k, gd, (c,), c2, r0d, r1ad, r1bd, r2ad, r2bd, r3d, td, fd, put_to(out_d, THIRD), 128)
+    down = Scatter(k, gd, (c,), (c2,), CUTS["down"], work, put_to(out_d, THIRD))
 
     def put_up(part):
         def put(value, core):
             out_u[:, lanes(core * 1536 + part * D, D)] = value
         return put
 
-    up = [Scatter(k, gu, (c, part), (c2, part), r0u.at[part], (r1au, r1av)[part], (r1bu, r1bv)[part], (r2au, r2av)[part],
-                  (r2bu, r2bv)[part], r3u.at[part], tu.at[part], fu.at[part], put_up(part), 256 - 128 * part)
-          for part in range(2)]
-    outp = Scatter(k, go, (c,), c2, r0o, r1ao, r1bo, r2ao, r2bo, r3o, to, fo, put_to(out_o, THIRD), 128)
+    up = [Scatter(k, gu, (c, part), (c2, part), CUTS[f"up{part}"], work, put_up(part)) for part in range(2)]
+    outp = Scatter(k, go, (c,), (c2,), CUTS["out"], work, put_to(out_o, THIRD))
 
     def feed(wbuf, wdb, hid, slope, n2, n2t, alt, gpc):
         b_out, gain, shift = vrows[3:4, 0:D], vrows[4:5, 0:D], vrows[5:6, 0:D]
@@ -534,7 +588,8 @@
 
         def down_load(j, slot, order):
             h, part = chunk(j, *order)
-            return k.local(wd2.at[:, rows_at(h * 1536 + part * D, D), :], wdb.at[slot])
+            rows = rows_at(h * 1536 + part * D, D)
+            return [k.local(wd2.at[side, rows, :], wdb.at[slot, :, side * THIRD : (side + 1) * THIRD]) for side in range(2)]
 
         forth = (c, c2)
         loads = [up_load(j, j % 2, forth) for j in range(4)]
@@ -552,16 +607,11 @@
                 loads[3].start()
             h, part = chunk(j, *forth)
 
-            def ahead(side, carry):
-                there = lanes(side * THIRD, THIRD)
-                cols = lanes(h * 1536 + part * D + side * THIRD, THIRD)
-                value = jnp.dot(n2[...], wbuf[j % 2, :, there], preferred_element_type=F32) + vrows[6:7, cols]
-                result, bend = gelu_parts(value)
-                hid[:, cols] = result.astype(BF)
-                slope[:, cols] = bend
-                return carry
-
-            lax.fori_loop(0, 2, ahead, 0)
+            cols = lanes(h * 1536 + part * D, D)
+            value = jnp.dot(n2[...], wbuf[j % 2], preferred_element_type=F32) + vrows[6:7, cols]
+            result, bend = gelu_parts(value)
+            hid[:, cols] = result.astype(BF)
+            slope[:, cols] = bend
 
         vs[7:8, :] = jnp.sum(cotm[0].astype(F32), axis=0, keepdims=True) + jnp.sum(
             cotm[1].astype(F32), axis=0, keepdims=True)
@@ -579,7 +629,6 @@
         down.s0()
         fb[...] = jnp.zeros_like(fb)
         fc[...] = jnp.zeros_like(fc)
-        vup[...] = jnp.zeros_like(vup)
         gather_d.s4()
         back = (c2, c)
         again = [up_load(j, j % 2, back) for j in range(4)]
@@ -587,42 +636,22 @@
         again[0].start()
         down.s1()
         gather_d.done()
-        lower[0].start()
+        start(lower[0])
         for j in range(4):
             slot = j % 2
             if j < 3:
                 again[j + 1].start()
-                lower[j + 1].start()
+                start(lower[j + 1])
             again[j].wait()
-            lower[j].wait()
+            landed(lower[j])
             h, part = chunk(j, *back)
-            first = h * 1536 + part * D
-
-            def behind(side, carry):
-                there = lanes(side * THIRD, THIRD)
-                cols = lanes(first + side * THIRD, THIRD)
-                units = hid[:, lanes(first, D)]
-                fc[:, :, there] += jnp.dot(units, wdb[slot, side], preferred_element_type=F32).reshape(2, 256, THIRD)
-                grad = None
-                for other in range(2):
-                    term = lax.dot_general(
-                        cotm[:, :, other * THIRD : (other + 1) * THIRD].reshape(512, THIRD), wdb[slot, other, there, :],
-                        LAST, preferred_element_type=F32)
-                    grad = term if grad is None else grad + term
-                grad = (grad * slope[:, cols]).astype(BF)
-                gpc[:, there] = grad
-                vup[0:1, cols] += jnp.sum(grad.astype(F32), axis=0, keepdims=True)
-                return carry
-
-            lax.fori_loop(0, 2, behind, 0)
-
-            def normed_grad(side, carry):
-                there = lanes(side * THIRD, THIRD)
-                term = lax.dot_general(gpc[...], wbuf[slot, there, :], LAST, preferred_element_type=F32)
-                fb[:, :, there] += term.reshape(2, 256, THIRD)
-                return carry
-
-            lax.fori_loop(0, 2, normed_grad, 0)
+            cols = lanes(h * 1536 + part * D, D)
+            fc[...] += jnp.dot(hid[:, cols], wdb[slot], preferred_element_type=F32).reshape(2, 256, D)
+            grad = lax.dot_general(cotm[...].reshape(512, D), wdb[slot], LAST, preferred_element_type=F32)
+            grad = (grad * slope[:, cols]).astype(BF)
+            gpc[...] = grad
+            vup[0:1, cols] = jnp.sum(grad.astype(F32), axis=0, keepdims=True)
+            fb[...] += lax.dot_general(gpc[...], wbuf[slot], LAST, preferred_element_type=F32).reshape(2, 256, D)
 
             def up_grad(zz, carry):
                 total = jnp.dot(n2t[rows_at(zz * THIRD, THIRD, 128), :], gpc[...], preferred_element_type=F32)
@@ -683,22 +712,24 @@
                 out_q[:, lanes(kind * D + core * THIRD + u * 128)] = value[:, kind * 128 : (kind + 1) * 128]
         return put
 
-    bases = [k.fresh(3) for _ in range(8)]
-
-    def query_scatter(u):
-        return Scatter(k, gq.at[u], (), None, None, q1a.at[u], q1b.at[u], q2a.at[u], q2b.at[u], q3.at[u], tq.at[u], fq.at[u],
-                       put_q(u), 128, base=[b + u for b in bases])
-
-    queue = [query_scatter(u) for u in range(3)]
+    queue = [Scatter(k, gq, (u,), None, CUTS[f"q{u}"], work, put_q(u)) for u in range(3)]
     bo_own = k.local(bo.at[y], out_bo.at[y])
     bo_y = k.remote(bo.at[y2], out_bo.at[y], k.py)
+
+    def collect(index):
+        row = vbq[...] if index == 2 else vup[...] if index == 6 else vs[index : index + 1, :]
+        vtab[pl.ds(index, 32, stride=8), :] = collect_rows(row, WIDTHS[index])
+
+    def early():
+        for index in (3, 4, 5, 6, 7):
+            collect(index)
 
     def send_out():
         bo_own.start()
         bo_y.start()
 
-    def backward(alt, gpc, qs, qst, keys_ref, values_ref, att, n1t, gt, kt, dk, dv, gpu, wqm):
-        loads = [k.local(k_qs, qs), k.local(k_qst, qst), k.local(k_k, keys_ref), k.local(k_v, values_ref),
+    def backward(alt, gpc, qst, keys_ref, values_ref, att, n1t, gt, kt, dk, dv, gpu, wqm):
+        loads = [k.local(k_qst, qst), k.local(k_k, keys_ref), k.local(k_v, values_ref),
                  k.local(k_att, att), k.local(k_n1t, n1t), k.local(wq3, wqm)]
         start(loads)
         turn(alt, gpc)
@@ -706,11 +737,10 @@
         fc[...] = jnp.zeros_like(fc)
         ga_c.wait_recv()
         landed(loads)
-        lane = lax.broadcasted_iota(jnp.int32, (256, 128), 1)
         vbq[...] = jnp.zeros_like(vbq)
         slots = {
             (0, 3): [outp.s1, down.s3], (0, 2): [], (0, 1): [up[0].s2], (0, 0): [send_out, up[1].s2],
-            (1, 3): [outp.s2], (1, 2): [down.s4], (1, 1): [up[0].s3], (1, 0): [up[1].s3, down.s5],
+            (1, 3): [outp.s2], (1, 2): [down.s4], (1, 1): [up[0].s3], (1, 0): [up[1].s3, down.s5, early],
             (2, 3): [queue[0].s2], (2, 2): [outp.s3], (2, 1): [queue[0].s3], (2, 0): [up[0].s4],
         }
 
@@ -729,33 +759,26 @@
                 values = values_ref[0:rows, cols]
                 queries_t = qst[cols, qrange]
                 grads_t = gt[:, qrange]
-                queries = qs[qrange, cols]
-                grads = ga_all[block // 2, block % 2, :, cols]
                 qpos = block * 256 + lax.broadcasted_iota(jnp.int32, (1, 256), 1)
                 low = block * 256
                 seen = low + lax.broadcasted_iota(jnp.int32, (rows - low, 256), 0) <= jnp.maximum(qpos, limit)
                 prod = grads_t.astype(F32) * att[cols, qrange]
-                dqs, dks, dvs = [], None, None
+                dqs = []
                 for half in range(2):
                     part = slice(half * 64, half * 64 + 64)
                     in_sub = sub // 64 == half
-                    in_lane = lane // 64 == half
                     delta = jnp.sum(prod[part], axis=0, keepdims=True)
                     total = lt[pl.ds(u * 2 + half, 1), qrange]
                     zero = jnp.zeros((), BF)
                     scores = jnp.dot(keys, jnp.where(in_sub, queries_t, zero), preferred_element_type=F32)
                     pull = jnp.dot(values, jnp.where(in_sub, grads_t, zero), preferred_element_type=F32)
                     share = jnp.exp(masked(jnp.abs(scores) - total, seen, low))
-                    signed = jnp.where(scores > 0, share, jnp.where(scores < 0, -share, 0.0))
+                    signed = sign_of(scores) * share
                     grad_scores = (share * pull - signed * delta).astype(BF)
                     signed = signed.astype(BF)
-                    dvt = jnp.dot(signed, jnp.where(in_lane, grads, zero), preferred_element_type=F32)
-                    dkt = jnp.dot(grad_scores, jnp.where(in_lane, queries, zero), preferred_element_type=F32)
-                    dvs = dvt if dvs is None else dvs + dvt
-                    dks = dkt if dks is None else dks + dkt
+                    dv[part, 0:rows] += lax.dot_general(grads_t[part], signed, LAST, preferred_element_type=F32)
+                    dk[part, 0:rows] += lax.dot_general(queries_t[part], grad_scores, LAST, preferred_element_type=F32)
                     dqs.append(jnp.dot(kt[part, 0:rows], grad_scores, preferred_element_type=F32))
-                dk[0:rows, :] += dks
-                dv[0:rows, :] += dvs
                 gpu[qrange, 0:128] = (jnp.concatenate(dqs, axis=0).T * 0.125).astype(BF)
                 for which in range(3):
                     if slots[which, block]:
@@ -763,8 +786,10 @@
                         def _():
                             for step in slots[which, block]:
                                 step()
-            gpu[:, 128:256] = dk[...].astype(BF)
-            gpu[:, 256:384] = dv[...].astype(BF)
+            for b in range(4):
+                rows = slice(b * 256, (b + 1) * 256)
+                gpu[rows, 128:256] = dk[:, rows].T.astype(BF)
+                gpu[rows, 256:384] = dv[:, rows].T.astype(BF)
             sums = jnp.sum(gpu[...].astype(F32), axis=0, keepdims=True)
             for kind in range(3):
                 part = slice(kind * 128, (kind + 1) * 128)
@@ -808,34 +833,37 @@
 
     def both(alt, gpc):
         pl.run_scoped(
-            functools.partial(feed, alt=alt, gpc=gpc), vmem((2, D, D), BF), vmem((2, 2, D, THIRD), BF),
+            functools.partial(feed, alt=alt, gpc=gpc), vmem((2, D, D), BF), vmem((2, D, D), BF),
             vmem((512, FF), BF), vmem((512, FF), F32), vmem((512, D), BF), vmem((D, 512), BF))
         pl.run_scoped(
-            functools.partial(backward, alt, gpc), vmem((1024, THIRD), BF), vmem((THIRD, 1024), BF), vmem((1024, THIRD), BF),
+            functools.partial(backward, alt, gpc), vmem((THIRD, 1024), BF), vmem((1024, THIRD), BF),
             vmem((1024, THIRD), BF), vmem((THIRD, 1024), F32), vmem((D, 1024), BF), vmem((128, 1024), BF),
-            vmem((128, 1024), BF), vmem((1024, 128), F32), vmem((1024, 128), F32), vmem((1024, THIRD), BF),
+            vmem((128, 1024), BF), vmem((128, 1024), F32), vmem((128, 1024), F32), vmem((1024, THIRD), BF),
             vmem((3, D, THIRD), BF))
 
     pl.run_scoped(both, vmem((D, 512), BF), vmem((512, D), BF))
 
     gain = vrows[0:1, 0:D]
     vs[0:2, :] = jnp.zeros((2, D), F32)
-
-    def sums(core, ref):
-        def add(yy, carry):
-            normed, _ = unit_rows(tok_all[yy, core].astype(F32))
-            grad = ref[yy]
-            vs[0:1, :] += jnp.sum(grad * normed, axis=0, keepdims=True)
-            vs[1:2, :] += jnp.sum(grad, axis=0, keepdims=True)
-            return carry
-
-        lax.fori_loop(0, 2, add, 0)
-
-    sums(c2, fb)
-    sums(c, fc)
-    for index, wide in enumerate(WIDTHS):
-        row = vbq[...] if index == 2 else vup[...] if index == 6 else vs[index : index + 1, :]
-        vtab[pl.ds(index, 32, stride=8), :] = collect_rows(row, wide)
+    part_c.wait_recv()
+
+    def last_back(yy):
+        normed, scale = unit_rows(tok_all[yy, c].astype(F32))
+        grad = fc[yy] + fr[yy]
+        vs[0:1, :] += jnp.sum(grad * normed, axis=0, keepdims=True)
+        vs[1:2, :] += jnp.sum(grad, axis=0, keepdims=True)
+        gtb[yy] = (fa[yy] + norm_back(grad * gain, normed, scale)).astype(BF)
+
+    gt_own = k.local(gtb.at[y], out_gt.at[y])
+    gt_y = k.remote(gtb.at[y2], out_gt.at[y], k.py)
+    last_back(y2)
+    gt_y.start()
+    queue[1].s2()
+    last_back(y)
+    gt_own.start()
+    queue[2].s2()
+    for index in range(3):
+        collect(index)
     table = vtab.reshape(4, 2, 2, 2, 8, 128)
     v0 = k.remote(table.at[:, :, :, c2], vr0, k.pc)
     v1 = k.remote(table.at[:, :, y2, c], vr1, k.py)
@@ -846,19 +874,7 @@
         return rows_at((((zz * 2 + xx) * 2 + yy) * 2 + c) * 8, 8, 8)
 
     v0.start()
-    part_c.wait_recv()
-
-    def last_back(yy):
-        normed, scale = unit_rows(tok_all[yy, c].astype(F32))
-        grad = fc[yy] + fr[yy]
-        gtb[yy] = (fa[yy] + norm_back(grad * gain, normed, scale)).astype(BF)
-
-    gt_own = k.local(gtb.at[y], out_gt.at[y])
-    gt_y = k.remote(gtb.at[y2], out_gt.at[y], k.py)
-    last_back(y2)
-    gt_y.start()
-    last_back(y)
-    gt_own.start()
+    queue[1].s3()
     v0.wait_recv()
 
     def add_core(i, carry):
@@ -868,9 +884,9 @@
 
     lax.fori_loop(0, 16, add_core, 0)
     v1.start()
-    queue[1].s2()
-    queue[2].s2()
+    queue[2].s3()
     queue[0].s4()
+    up[1].s4()
     v1.wait_recv()
 
     def add_y(i, carry):
@@ -879,8 +895,9 @@
 
     lax.fori_loop(0, 8, add_y, 0)
     v2.start()
-    queue[1].s3()
-    queue[2].s3()
+    outp.s4()
+    up[0].s5()
+    queue[0].s5()
     v2.wait_recv()
 
     def add_x(zz, carry):
@@ -889,20 +906,18 @@
 
     lax.fori_loop(0, 4, add_x, 0)
     start(v3)
-    up[1].s4()
-    outp.s4()
     queue[1].s4()
+    up[1].s5()
+    outp.s5()
     queue[2].s4()
-    for scatter in (up[0], up[1], outp, queue[0], queue[1], queue[2]):
-        scatter.s5()
+    queue[1].s5()
+    queue[2].s5()
     arrive(v3)
     out_vec[...] = vtab[tile(z, x, y), :] + vr3[0] + vr3[1] + vr3[2]
     landed([gt_own, bo_own])
     arrive([gt_y, bo_y])
     for copy in k.sent:
         copy.wait_send()
-    for scatter in queue:
-        scatter.gone()
     assert k.remotes <= REMOTES and k.locals <= LOCALS
 
 
@@ -916,7 +931,7 @@
     )
     held = (
         sds((3, 4, 2, 2, 48, 384), BF), sds((2, 4, 2, 2, 48, 384), BF), sds((2, 2, 4, 2, 2, 48, 768), BF),
-        sds((2, 4, 2, 2, 192, 384), BF), sds((4, 2, 2, 2, 8, 128), F32), sds((1024, THIRD), BF), sds((THIRD, 1024), BF),
+        sds((2, 4, 2, 2, 192, 384), BF), sds((4, 2, 2, 2, 8, 128), F32), sds((THIRD, 1024), BF),
         sds((1024, THIRD), BF), sds((1024, THIRD), BF), sds((THIRD, 1024), F32), sds((D, 1024), BF),
     )
     scratch = [
@@ -925,23 +940,15 @@
         vmem((2, 256, D), BF), vmem((2, 2, 256, THIRD), BF), vmem((2, 256, D), F32), vmem((2, 256, D), F32),
         vmem((2, 256, D), F32), vmem((2, 256, D), F32), vmem((8, 1024), F32),
     ]
-    kinds = (((), 192, 384, (128,)), ((2,), 48, 768, (256, 128)), ((), 48, 384, (128,)))
-    scratch += [vmem((2,) + p + (4, 2, 2, r, n), BF) for p, r, n, _ in kinds] + [vmem((3, 4, 2, 2, 48, 384), BF)]
-    scratch += [vmem(p + (4, 2, 2, r, n), BF) for p, r, n, _ in kinds]
-    for lead in ((4, 2), (4,)):
-        for _, r, n, cuts in kinds:
-            for cut in cuts:
-                scratch += [vmem(lead + (r, cut), BF), vmem(lead + (r, n - cut), BF)]
-    scratch += [vmem(p + (3, r, n), BF) for p, r, n, _ in kinds]
-    scratch += [vmem(p + (2, r // 2, n), F32) for p, r, n, _ in kinds]
-    scratch += [vmem(p + (r // 2, n), F32) for p, r, n, _ in kinds]
     scratch += [
-        vmem((3, 4, 2, 48, 128), BF), vmem((3, 4, 2, 48, 256), BF), vmem((3, 4, 48, 128), BF), vmem((3, 4, 48, 256), BF),
-        vmem((3, 3, 48, 384), BF), vmem((3, 2, 24, 384), F32), vmem((3, 24, 384), F32),
+        vmem((2, 4, 2, 2, 192, 384), BF), vmem((2, 2, 4, 2, 2, 48, 768), BF), vmem((2, 4, 2, 2, 48, 384), BF),
+        vmem((3, 4, 2, 2, 48, 384), BF),
         vmem((8, D), F32), vmem((1, 3 * D), F32), vmem((1, FF), F32), vmem((256, 128), F32), vmem((4, 2, 2, 8, 128), F32),
         vmem((4, 2, 8, 128), F32), vmem((4, 8, 128), F32), vmem((3, 8, 128), F32),
         dma((REMOTES,)), dma((REMOTES,)), dma((LOCALS,)),
     ]
+    for name in ("down", "up0", "up1", "out", "q0", "q1", "q2"):
+        scratch += Scatter.buffers(CUTS[name], not name.startswith("q"))
     return pl.pallas_call(
         layer_kernel,
         out_shape=results + held,

time: 194 us -> 190 us (0.979)
  Pallas kernels: 193 us -> 188 us
    pallas_call x1, Pallas kernels: 189 us -> 185 us  [layer_call(): pl.pallas_call(layer_kernel, out_shape=results + held, in_specs=[SM] + [A...]
where the time goes in v5:
time: 190 us; the launch traced here: 189 us
  Pallas kernels  188 us (99%)
    pallas_call x1, Pallas kernels, layer_call(): pl.pallas_call(layer_kernel, out_shape=results + held, in_specs=[SM] + [A...  185 us

profile of v5, /device:TPU:0, one launch (start us, length us, event | category | flops | bytes accessed | tf_op | source)
XLA Modules:
  0.0 189.2 jit_solution(1771512667609570193)
XLA Ops:
  0.7 185.2 %shard_map.254 = (bf16[2,256,768]{2,1,0:T(8,128)(2,1)}, bf16[2,256,768]{2,1,0:T(8,128)(2,1)}, f32[24,2304]{1,0:T(8,128)}, f32[24,768]{1,0:T(8,128)}, f32[24,3072...) custom-call(s32[2]{0:T(128)} %prefix.1, ...), custom_call_target="tpu_custom_call" | custom-call | tf_op jit(solution)/shard_map/pallas_call | solution.py:952
  185.8 3.1 %shard_map.255 = (bf16[2,256,768]{2,1,0:T(8,128)(2,1)}, bf16[2,256,768]{2,1,0:T(8,128)(2,1)}, f32[24,2304]{1,0:T(8,128)}, f32[24,768]{1,0:T(8,128)}, f32[24,3072...) custom-call(bf16[2,256,768]{2,1,0:T(8,128)(2,1)} %get-tuple-element., ...), custom_call_target="tpu_custom_call" | custom-call | tf_op jit(solution)/shard_map/pallas_call | solution.py:976

commit v6 on v5

--- a/solution.py
+++ b/solution.py
@@ -378,6 +378,8 @@
 
     gather_o = halves(wo_s, wo, CUTS["out"])
     gather_d = halves(wd_s, wd, CUTS["down"])
+    k.sent.pop()
+    gather_d.c4 = [k.remote(wd.at[c, zz], wd.at[c, zz], k.pc) for zz in (2 * c, 2 * c + 1, 2 * c2, 2 * c2 + 1)]
     gather_u = [Gather(k, wu_s.at[:, lanes(c * 1536 + part * D, D)], wu_s.at[:, lanes(c2 * 1536 + part * D, D)],
                        wu.at[c, part], wu.at[c2, part], CUTS[f"up{part}"]) for part in range(2)]
     own_vec = k.local(vec_s, gv.at[z, x, y, c])
@@ -437,6 +439,7 @@
     peer_cols = lanes(c2 * THIRD, THIRD)
     al_own = k.local(al_send.at[:, c], al.at[:, :, mine_cols])
     al_c = k.remote(al_send.at[:, c2], al.at[:, :, mine_cols], k.pc)
+    gathered = len(k.sent)
     limit = prefix[y] - 1
     sub = lax.broadcasted_iota(jnp.int32, (128, 256), 0)
     wq3 = wq.reshape(3, D, THIRD)
@@ -635,12 +638,13 @@
         lower = [down_load(j, j % 2, back) for j in range(4)]
         again[0].start()
         down.s1()
-        gather_d.done()
+        gather_d.c4[0].wait_recv()
         start(lower[0])
         for j in range(4):
             slot = j % 2
             if j < 3:
                 again[j + 1].start()
+                gather_d.c4[j + 1].wait_recv()
                 start(lower[j + 1])
             again[j].wait()
             landed(lower[j])
@@ -728,20 +732,19 @@
         bo_own.start()
         bo_y.start()
 
-    def backward(alt, gpc, qst, keys_ref, values_ref, att, n1t, gt, kt, dk, dv, gpu, wqm):
+    def backward(alt, gpc, qst, keys_ref, values_ref, att, n1t, gt, kt, dk, dv, gpu, wqm, gp):
         loads = [k.local(k_qst, qst), k.local(k_k, keys_ref), k.local(k_v, values_ref),
-                 k.local(k_att, att), k.local(k_n1t, n1t), k.local(wq3, wqm)]
+                 k.local(k_att, att), k.local(k_n1t, n1t), ]
+        loads += [k.local(wq3.at[u], wqm.at[:, u * THIRD : (u + 1) * THIRD]) for u in range(3)]
         start(loads)
         turn(alt, gpc)
-        fb[...] = jnp.zeros_like(fb)
-        fc[...] = jnp.zeros_like(fc)
         ga_c.wait_recv()
         landed(loads)
         vbq[...] = jnp.zeros_like(vbq)
         slots = {
-            (0, 3): [outp.s1, down.s3], (0, 2): [], (0, 1): [up[0].s2], (0, 0): [send_out, up[1].s2],
-            (1, 3): [outp.s2], (1, 2): [down.s4], (1, 1): [up[0].s3], (1, 0): [up[1].s3, down.s5, early],
-            (2, 3): [queue[0].s2], (2, 2): [outp.s3], (2, 1): [queue[0].s3], (2, 0): [up[0].s4],
+            (0, 3): [outp.s1], (0, 2): [], (0, 1): [down.s3], (0, 0): [up[0].s2, send_out],
+            (1, 3): [], (1, 2): [up[1].s2], (1, 1): [outp.s2], (1, 0): [down.s4, up[0].s3, early],
+            (2, 3): [up[1].s3], (2, 2): [queue[0].s2, down.s5], (2, 1): [outp.s3], (2, 0): [queue[0].s3, up[0].s4],
         }
 
         def unit(u, carry):
@@ -794,6 +797,7 @@
             for kind in range(3):
                 part = slice(kind * 128, (kind + 1) * 128)
                 vbq[0:1, lanes(kind * D + c * THIRD + u * 128)] = sums[:, part]
+                gp[:, lanes(u * THIRD + kind * 128)] = gpu[:, part]
 
             def weights(zz, inner):
                 block = jnp.dot(n1t[rows_at(zz * THIRD, THIRD, 128), :], gpu[...], preferred_element_type=F32)
@@ -806,28 +810,26 @@
                 @pl.when(u == which)
                 def _():
                     queue[which].s1()
-
-            def back_rows(b):
-                return lax.dot_general(gpu[rows_at(b * 256, 256), :], wqm[u], LAST, preferred_element_type=F32)
-
-            def back_peer(yy, inner):
-                fb[yy] += back_rows(yy * 2 + c2)
-                return inner
-
-            def back_own(yy, inner):
-                fc[yy] += back_rows(yy * 2 + c)
-                return inner
-
-            lax.fori_loop(0, 2, back_peer, 0)
-
-            @pl.when(u == 2)
-            def _():
-                part_c.start()
-
-            lax.fori_loop(0, 2, back_own, 0)
             return carry
 
         lax.fori_loop(0, 3, unit, 0)
+
+        def back_rows(b):
+            return lax.dot_general(gp[rows_at(b * 256, 256), :], wqm[...], LAST, preferred_element_type=F32)
+
+        def back_peer(yy, carry):
+            fb[yy] = back_rows(yy * 2 + c2)
+            return carry
+
+        def back_own(yy, carry):
+            fc[yy] = back_rows(yy * 2 + c)
+            return carry
+
+        lax.fori_loop(0, 2, back_peer, 0)
+        part_c.start()
+        queue[1].s2()
+        lax.fori_loop(0, 2, back_own, 0)
+        queue[2].s2()
 
     part_c = k.remote(fb, fr, k.pc)
 
@@ -839,7 +841,7 @@
             functools.partial(backward, alt, gpc), vmem((THIRD, 1024), BF), vmem((1024, THIRD), BF),
             vmem((1024, THIRD), BF), vmem((THIRD, 1024), F32), vmem((D, 1024), BF), vmem((128, 1024), BF),
             vmem((128, 1024), BF), vmem((128, 1024), F32), vmem((128, 1024), F32), vmem((1024, THIRD), BF),
-            vmem((3, D, THIRD), BF))
+            vmem((D, 3 * THIRD), BF), vmem((1024, 3 * THIRD), BF))
 
     pl.run_scoped(both, vmem((D, 512), BF), vmem((512, D), BF))
 
@@ -858,10 +860,10 @@
     gt_y = k.remote(gtb.at[y2], out_gt.at[y], k.py)
     last_back(y2)
     gt_y.start()
-    queue[1].s2()
+    queue[1].s3()
     last_back(y)
     gt_own.start()
-    queue[2].s2()
+    queue[2].s3()
     for index in range(3):
         collect(index)
     table = vtab.reshape(4, 2, 2, 2, 8, 128)
@@ -874,7 +876,7 @@
         return rows_at((((zz * 2 + xx) * 2 + yy) * 2 + c) * 8, 8, 8)
 
     v0.start()
-    queue[1].s3()
+    queue[0].s4()
     v0.wait_recv()
 
     def add_core(i, carry):
@@ -884,9 +886,10 @@
 
     lax.fori_loop(0, 16, add_core, 0)
     v1.start()
-    queue[2].s3()
-    queue[0].s4()
+    for copy in k.sent[:gathered]:
+        copy.wait_send()
     up[1].s4()
+    queue[1].s4()
     v1.wait_recv()
 
     def add_y(i, carry):
@@ -906,17 +909,16 @@
 
     lax.fori_loop(0, 4, add_x, 0)
     start(v3)
-    queue[1].s4()
+    queue[2].s4()
     up[1].s5()
     outp.s5()
-    queue[2].s4()
     queue[1].s5()
     queue[2].s5()
     arrive(v3)
     out_vec[...] = vtab[tile(z, x, y), :] + vr3[0] + vr3[1] + vr3[2]
     landed([gt_own, bo_own])
     arrive([gt_y, bo_y])
-    for copy in k.sent:
+    for copy in k.sent[gathered:]:
         copy.wait_send()
     assert k.remotes <= REMOTES and k.locals <= LOCALS
 

time: 190 us -> 184 us (0.968)
  Pallas kernels: 188 us -> 183 us
    pallas_call x1, Pallas kernels: 185 us -> 179 us  [layer_call(): pl.pallas_call(layer_kernel, out_shape=results + held, in_specs=[SM] + [A...]
where the time goes in v6:
time: 184 us; the launch traced here: 183 us
  Pallas kernels  183 us (99%)
    pallas_call x1, Pallas kernels, layer_call(): pl.pallas_call(layer_kernel, out_shape=results + held, in_specs=[SM] + [A...  179 us

profile of v6, /device:TPU:0, one launch (start us, length us, event | category | flops | bytes accessed | tf_op | source)
XLA Modules:
  0.0 183.4 jit_solution(8944104713573725237)
XLA Ops:
  0.7 179.5 %shard_map.254 = (bf16[2,256,768]{2,1,0:T(8,128)(2,1)}, bf16[2,256,768]{2,1,0:T(8,128)(2,1)}, f32[24,2304]{1,0:T(8,128)}, f32[24,768]{1,0:T(8,128)}, f32[24,3072...) custom-call(s32[2]{0:T(128)} %prefix.1, ...), custom_call_target="tpu_custom_call" | custom-call | tf_op jit(solution)/shard_map/pallas_call | solution.py:954
  180.1 3.1 %shard_map.255 = (bf16[2,256,768]{2,1,0:T(8,128)(2,1)}, bf16[2,256,768]{2,1,0:T(8,128)(2,1)}, f32[24,2304]{1,0:T(8,128)}, f32[24,768]{1,0:T(8,128)}, f32[24,3072...) custom-call(bf16[2,256,768]{2,1,0:T(8,128)(2,1)} %get-tuple-element., ...), custom_call_target="tpu_custom_call" | custom-call | tf_op jit(solution)/shard_map/pallas_call | solution.py:978

commit v7 on v6

--- a/solution.py
+++ b/solution.py
@@ -113,6 +113,8 @@
         if upto:
             self.f = (slice(0, rows), slice(upto, columns))
         if upto_row:
+            self.a = (slice(0, upto_row // 2), slice(0, columns))
+            self.b = (slice(upto_row // 2, upto_row), slice(0, columns))
             self.f = (slice(upto_row, rows), slice(0, columns))
 
     def shape(self, part):

time: 184 us -> 181 us (0.984)
  Pallas kernels: 183 us -> 180 us
    pallas_call x1, Pallas kernels: 179 us -> 176 us  [layer_call(): pl.pallas_call(layer_kernel, out_shape=results + held, in_specs=[SM] + [A...]
where the time goes in v7:
time: 181 us; the launch traced here: 180 us
  Pallas kernels  180 us (99%)
    pallas_call x1, Pallas kernels, layer_call(): pl.pallas_call(layer_kernel, out_shape=results + held, in_specs=[SM] + [A...  176 us

profile of v7, /device:TPU:0, one launch (start us, length us, event | category | flops | bytes accessed | tf_op | source)
XLA Modules:
  0.0 180.4 jit_solution(11964475693017268220)
XLA Ops:
  0.7 176.4 %shard_map.254 = (bf16[2,256,768]{2,1,0:T(8,128)(2,1)}, bf16[2,256,768]{2,1,0:T(8,128)(2,1)}, f32[24,2304]{1,0:T(8,128)}, f32[24,768]{1,0:T(8,128)}, f32[24,3072...) custom-call(s32[2]{0:T(128)} %prefix.1, ...), custom_call_target="tpu_custom_call" | custom-call | tf_op jit(solution)/shard_map/pallas_call | solution.py:956
  177.1 3.1 %shard_map.255 = (bf16[2,256,768]{2,1,0:T(8,128)(2,1)}, bf16[2,256,768]{2,1,0:T(8,128)(2,1)}, f32[24,2304]{1,0:T(8,128)}, f32[24,768]{1,0:T(8,128)}, f32[24,3072...) custom-call(bf16[2,256,768]{2,1,0:T(8,128)(2,1)} %get-tuple-element., ...), custom_call_target="tpu_custom_call" | custom-call | tf_op jit(solution)/shard_map/pallas_call | solution.py:980

commit v8 on v7

--- a/solution.py
+++ b/solution.py
@@ -632,8 +632,6 @@
 
         lax.fori_loop(0, 8, down_grad, 0)
         down.s0()
-        fb[...] = jnp.zeros_like(fb)
-        fc[...] = jnp.zeros_like(fc)
         gather_d.s4()
         back = (c2, c)
         again = [up_load(j, j % 2, back) for j in range(4)]
@@ -652,12 +650,14 @@
             landed(lower[j])
             h, part = chunk(j, *back)
             cols = lanes(h * 1536 + part * D, D)
-            fc[...] += jnp.dot(hid[:, cols], wdb[slot], preferred_element_type=F32).reshape(2, 256, D)
+            term = jnp.dot(hid[:, cols], wdb[slot], preferred_element_type=F32).reshape(2, 256, D)
+            fc[...] = term if j == 0 else fc[...] + term
             grad = lax.dot_general(cotm[...].reshape(512, D), wdb[slot], LAST, preferred_element_type=F32)
             grad = (grad * slope[:, cols]).astype(BF)
             gpc[...] = grad
             vup[0:1, cols] = jnp.sum(grad.astype(F32), axis=0, keepdims=True)
-            fb[...] += lax.dot_general(gpc[...], wbuf[slot], LAST, preferred_element_type=F32).reshape(2, 256, D)
+            term = lax.dot_general(gpc[...], wbuf[slot], LAST, preferred_element_type=F32).reshape(2, 256, D)
+            fb[...] = term if j == 0 else fb[...] + term
 
             def up_grad(zz, carry):
                 total = jnp.dot(n2t[rows_at(zz * THIRD, THIRD, 128), :], gpc[...], preferred_element_type=F32)

time: 181 us -> 183 us (1.011)
  no operation moved by 1% of the time
where the time goes in v8:
time: 183 us; the launch traced here: 182 us
  Pallas kernels  181 us (99%)
    pallas_call x1, Pallas kernels, layer_call(): pl.pallas_call(layer_kernel, out_shape=results + held, in_specs=[SM] + [A...  178 us

profile of v8, /device:TPU:0, one launch (start us, length us, event | category | flops | bytes accessed | tf_op | source)
XLA Modules:
  0.0 182.2 jit_solution(2000950815285597470)
XLA Ops:
  0.7 178.2 %shard_map.254 = (bf16[2,256,768]{2,1,0:T(8,128)(2,1)}, bf16[2,256,768]{2,1,0:T(8,128)(2,1)}, f32[24,2304]{1,0:T(8,128)}, f32[24,768]{1,0:T(8,128)}, f32[24,3072...) custom-call(s32[2]{0:T(128)} %prefix.1, ...), custom_call_target="tpu_custom_call" | custom-call | tf_op jit(solution)/shard_map/pallas_call | solution.py:956
  178.8 3.1 %shard_map.255 = (bf16[2,256,768]{2,1,0:T(8,128)(2,1)}, bf16[2,256,768]{2,1,0:T(8,128)(2,1)}, f32[24,2304]{1,0:T(8,128)}, f32[24,768]{1,0:T(8,128)}, f32[24,3072...) custom-call(bf16[2,256,768]{2,1,0:T(8,128)(2,1)} %get-tuple-element., ...), custom_call_target="tpu_custom_call" | custom-call | tf_op jit(solution)/shard_map/pallas_call | solution.py:980
